TPU v7x, 32 devices: a whole 2x2x4 slice. The times are simulated.
32 devices in a mesh: dp: 8 (over y, x, core), mp: 4 (over z).
Axes of the slice: x: 2, y: 2, z: 4, core: 2. Of those that a mesh axis runs over, the one named last changes fastest.
Arguments:
- layer_input: bfloat16 [8192, 2048], P(('dp', 'mp')), may hold values from -6 to 6
- query_weight: bfloat16 [2048, 2048], P('dp', 'mp'), may hold values from -0.125 to 0.125
- key_weight: bfloat16 [2048, 2048], P('dp', 'mp'), may hold values from -0.125 to 0.125
- value_weight: bfloat16 [2048, 2048], P('dp', 'mp'), may hold values from -0.125 to 0.125
- out_weight: bfloat16 [2048, 2048], P('mp', 'dp'), may hold values from -0.125 to 0.125
- gate_weight: bfloat16 [2048, 8192], P('dp', 'mp'), may hold values from -0.125 to 0.125
- up_weight: bfloat16 [2048, 8192], P('dp', 'mp'), may hold values from -0.125 to 0.125
- down_weight: bfloat16 [8192, 2048], P('mp', 'dp'), may hold values from -0.0625 to 0.0625
- query_gain: bfloat16 [16, 128], P('mp', 'dp'), may hold values from 0.099609375 to 1.8984375
- key_gain: bfloat16 [16, 128], P('mp', 'dp'), may hold values from 0.099609375 to 1.8984375
- attn_gain: bfloat16 [2048], P('dp'), may hold values from 0.099609375 to 1.8984375
- mlp_gain: bfloat16 [2048], P('dp'), may hold values from 0.099609375 to 1.8984375
- seq_lens: int32 [8, 2], P('dp'), may hold values from 0 to 1024, as said below
- out_grad: bfloat16 [8192, 2048], P(('dp', 'mp')), may hold values from -6 to 6
Outputs:
- layer_output: bfloat16 [8192, 2048], P(('dp', 'mp'))
- input_grad: float32 [8192, 2048], P(('dp', 'mp'))
- query_weight_grad: float32 [2048, 2048], P('dp', 'mp')
- key_weight_grad: float32 [2048, 2048], P('dp', 'mp')
- value_weight_grad: float32 [2048, 2048], P('dp', 'mp')
- out_weight_grad: float32 [2048, 2048], P('mp', 'dp')
- gate_weight_grad: float32 [2048, 8192], P('dp', 'mp')
- up_weight_grad: float32 [2048, 8192], P('dp', 'mp')
- down_weight_grad: float32 [8192, 2048], P('mp', 'dp')
- query_gain_grad: float32 [16, 128], P('mp', 'dp')
- key_gain_grad: float32 [16, 128], P('mp', 'dp')
- attn_gain_grad: float32 [2048], P('dp')
- mlp_gain_grad: float32 [2048], P('dp')
Inputs may be any that keep to these rules, and one draw needn't show every extreme that they name: `seq_lens`: row g lists the lengths of the sequences packed in order from the start of data group g's 1024 positions: each nonzero length is 512 or more, zeros follow the last sequence, and together they cover at most 1024 positions; the positions after them are padding. At least one group holds a single sequence of 1024.
All inputs are finite; a program needn't handle non-finite values.
Results may differ from a plain program's by a relative error of at most 0.022.
Values may be sent and summed in bfloat16 or wider, within the bound.
A program may use at most 192 MiB of HBM per device.

v0:
```python
import math

import jax
import jax.numpy as jnp
from jax import lax
from jax.sharding import PartitionSpec as P

EPS = 1e-06
THETA = 500000.0
MASKED = -1000000000.0


def plain_dot(former, latter):
    return jnp.dot(former, latter, preferred_element_type=jnp.float32)


def inner_dot(former, latter):
    return lax.dot_general(
        former, latter, (((0,), (0,)), ((), ())), preferred_element_type=jnp.float32
    )


def outer_dot(former, latter):
    return lax.dot_general(
        former, latter, (((1,), (1,)), ((), ())), preferred_element_type=jnp.float32
    )


def layout(lengths, group_size):
    slot_count = lengths.shape[0]
    seq_ends = jnp.cumsum(lengths, dtype=jnp.int32)
    starts = seq_ends - lengths
    places = jnp.arange(group_size, dtype=jnp.int32)
    slot_ids = jnp.arange(slot_count, dtype=jnp.int32)
    segment = jnp.sum(
        (places[:, None] >= seq_ends[None, :]).astype(jnp.int32), axis=1, dtype=jnp.int32
    )
    chosen = (segment[:, None] == slot_ids[None, :]).astype(jnp.int32)
    padded = (segment == slot_count).astype(jnp.int32)
    begins = (
        jnp.sum(chosen * starts[None, :], axis=1, dtype=jnp.int32)
        + padded * seq_ends[slot_count - 1]
    )
    return (segment, places - begins, places < seq_ends[slot_count - 1])


def rotary_tables(positions, head_size):
    half_dim = head_size // 2
    frequency = jnp.exp(
        jnp.arange(half_dim, dtype=jnp.float32) * (-2.0 * math.log(THETA) / head_size)
    )
    angles = positions.astype(jnp.float32)[:, None] * frequency[None, :]
    doubled = jnp.concatenate([angles, angles], axis=1)
    return (jnp.cos(doubled)[:, None, :], jnp.sin(doubled)[:, None, :])


def rotate(values, cos_table, sin_table):
    half_dim = values.shape[-1] // 2
    turned = jnp.concatenate([-values[..., half_dim:], values[..., :half_dim]], axis=-1)
    return values * cos_table + turned * sin_table


def rotate_back(values, cos_table, sin_table):
    scaled = values * sin_table
    half_dim = values.shape[-1] // 2
    turned = jnp.concatenate([scaled[..., half_dim:], -scaled[..., :half_dim]], axis=-1)
    return values * cos_table + turned


def norm_back(values, inverse, gain_row, upstream):
    weighted = upstream * gain_row
    mean_term = jnp.mean(weighted * values, axis=1, keepdims=True)
    grad_values = inverse * weighted - values * inverse**3 * mean_term
    return (grad_values, jnp.sum(upstream * values * inverse, axis=0))


def local(
    layer_input,
    query_weight,
    key_weight,
    value_weight,
    out_weight,
    gate_weight,
    up_weight,
    down_weight,
    query_gain,
    key_gain,
    attn_gain,
    mlp_gain,
    seq_lens,
    out_grad,
):
    row_count = layer_input.shape[0]
    model_width = layer_input.shape[1]
    group_size = row_count * lax.axis_size("mp")
    local_heads = query_gain.shape[0]
    head_size = query_gain.shape[1] * lax.axis_size("dp")
    local_width = local_heads * head_size
    row_first = lax.axis_index("mp") * row_count
    segment, positions, valid = layout(seq_lens[0], group_size)
    cos_table, sin_table = rotary_tables(positions, head_size)
    row_valid = lax.dynamic_slice_in_dim(valid, row_first, row_count, 0).astype(jnp.float32)
    fetched = (
        lax.all_gather(query_weight, "dp", axis=0, tiled=True),
        lax.all_gather(key_weight, "dp", axis=0, tiled=True),
        lax.all_gather(value_weight, "dp", axis=0, tiled=True),
        lax.all_gather(out_weight, "dp", axis=1, tiled=True),
        lax.all_gather(gate_weight, "dp", axis=0, tiled=True),
        lax.all_gather(up_weight, "dp", axis=0, tiled=True),
        lax.all_gather(down_weight, "dp", axis=1, tiled=True),
        lax.all_gather(query_gain, "dp", axis=1, tiled=True),
        lax.all_gather(key_gain, "dp", axis=1, tiled=True),
        lax.all_gather(attn_gain, "dp", axis=0, tiled=True),
        lax.all_gather(mlp_gain, "dp", axis=0, tiled=True),
    )
    (
        full_query,
        full_key,
        full_value,
        full_out,
        full_gate,
        full_up,
        full_down,
        gain_query,
        gain_key,
        gain_attn,
        gain_mlp,
    ) = fetched
    inputs_full = lax.all_gather(layer_input, "mp", axis=0, tiled=True)
    query_raw = plain_dot(inputs_full, full_query)
    key_raw = plain_dot(inputs_full, full_key)
    value_low = (
        plain_dot(inputs_full, full_value)
        .astype(jnp.bfloat16)
        .reshape(group_size, local_heads, head_size)
    )
    query_sums, key_sums = lax.psum(
        (jnp.sum(query_raw * query_raw, axis=1), jnp.sum(key_raw * key_raw, axis=1)), "mp"
    )
    query_inv = lax.rsqrt(query_sums / model_width + EPS)[:, None]
    key_inv = lax.rsqrt(key_sums / model_width + EPS)[:, None]
    query_scale = gain_query.reshape(local_width).astype(jnp.float32)
    key_scale = gain_key.reshape(local_width).astype(jnp.float32)
    query_low = rotate(
        (query_raw * query_inv * query_scale).reshape(group_size, local_heads, head_size),
        cos_table,
        sin_table,
    ).astype(jnp.bfloat16)
    key_low = rotate(
        (key_raw * key_inv * key_scale).reshape(group_size, local_heads, head_size),
        cos_table,
        sin_table,
    ).astype(jnp.bfloat16)
    block_rows = min(512, group_size)
    block_count = group_size // block_rows
    score_scale = 1.0 / math.sqrt(head_size)
    places = jnp.arange(group_size, dtype=jnp.int32)

    def block_scores(first_row, key_end):
        scores = (
            jnp.einsum(
                "qhd,khd->hqk",
                query_low[first_row:key_end],
                key_low[:key_end],
                preferred_element_type=jnp.float32,
            )
            * score_scale
        )
        allowed = (segment[first_row:key_end, None] == segment[None, :key_end]) & (
            places[first_row:key_end, None] >= places[None, :key_end]
        )
        return jnp.where(allowed[None], scores, MASKED)

    log_totals = []
    block_outputs = []
    for block_index in range(block_count):
        first_row = block_index * block_rows
        key_end = first_row + block_rows
        scores = block_scores(first_row, key_end)
        row_max = jnp.max(scores, axis=-1, keepdims=True)
        exponents = jnp.exp(scores - row_max)
        row_total = jnp.sum(exponents, axis=-1, keepdims=True)
        attn_probs = (exponents / row_total).astype(jnp.bfloat16)
        log_totals.append(row_max + jnp.log(row_total))
        block_outputs.append(
            jnp.einsum(
                "hqk,khd->qhd", attn_probs, value_low[:key_end], preferred_element_type=jnp.float32
            )
        )
    attended = (
        jnp.concatenate(block_outputs, axis=0).astype(jnp.bfloat16).reshape(group_size, local_width)
    )
    branch = lax.psum_scatter(plain_dot(attended, full_out), "mp", scatter_dimension=0, tiled=True)
    branch_inv = lax.rsqrt(jnp.mean(branch * branch, axis=1, keepdims=True) + EPS)
    attn_scale = gain_attn.astype(jnp.float32)
    middle = layer_input.astype(jnp.float32) + branch * branch_inv * attn_scale
    middle_full = lax.all_gather(middle.astype(jnp.bfloat16), "mp", axis=0, tiled=True)
    gate_proj = plain_dot(middle_full, full_gate)
    up_proj = plain_dot(middle_full, full_up)
    sigmoid_gate = jax.nn.sigmoid(gate_proj)
    activated = gate_proj * sigmoid_gate
    hidden = (activated * up_proj).astype(jnp.bfloat16)
    mlp_out = lax.psum_scatter(plain_dot(hidden, full_down), "mp", scatter_dimension=0, tiled=True)
    mlp_inv = lax.rsqrt(jnp.mean(mlp_out * mlp_out, axis=1, keepdims=True) + EPS)
    mlp_scale = gain_mlp.astype(jnp.float32)
    layer_output = (middle + mlp_out * mlp_inv * mlp_scale).astype(jnp.bfloat16)
    fetched = (
        lax.all_gather(query_weight, "dp", axis=0, tiled=True),
        lax.all_gather(key_weight, "dp", axis=0, tiled=True),
        lax.all_gather(value_weight, "dp", axis=0, tiled=True),
        lax.all_gather(out_weight, "dp", axis=1, tiled=True),
        lax.all_gather(gate_weight, "dp", axis=0, tiled=True),
        lax.all_gather(up_weight, "dp", axis=0, tiled=True),
        lax.all_gather(down_weight, "dp", axis=1, tiled=True),
        lax.all_gather(query_gain, "dp", axis=1, tiled=True),
        lax.all_gather(key_gain, "dp", axis=1, tiled=True),
        lax.all_gather(attn_gain, "dp", axis=0, tiled=True),
        lax.all_gather(mlp_gain, "dp", axis=0, tiled=True),
    )
    (
        full_query,
        full_key,
        full_value,
        full_out,
        full_gate,
        full_up,
        full_down,
        gain_query,
        gain_key,
        gain_attn,
        gain_mlp,
    ) = fetched
    upstream = out_grad.astype(jnp.float32) * row_valid[:, None]
    mlp_grad, mlp_gain_part = norm_back(mlp_out, mlp_inv, mlp_scale, upstream)
    mlp_grad_full = lax.all_gather(mlp_grad.astype(jnp.bfloat16), "mp", axis=0, tiled=True)
    down_part = inner_dot(hidden, mlp_grad_full)
    hidden_grad = outer_dot(mlp_grad_full, full_down)
    gate_grad = (
        hidden_grad * up_proj * sigmoid_gate * (1.0 + gate_proj * (1.0 - sigmoid_gate))
    ).astype(jnp.bfloat16)
    up_grad = (hidden_grad * activated).astype(jnp.bfloat16)
    gate_part = inner_dot(middle_full, gate_grad)
    up_part = inner_dot(middle_full, up_grad)
    grad_gate, grad_up, grad_down = (
        lax.psum_scatter(
            gate_part.astype(jnp.bfloat16), "dp", scatter_dimension=0, tiled=True
        ).astype(jnp.float32),
        lax.psum_scatter(
            up_part.astype(jnp.bfloat16), "dp", scatter_dimension=0, tiled=True
        ).astype(jnp.float32),
        lax.psum_scatter(
            down_part.astype(jnp.bfloat16), "dp", scatter_dimension=1, tiled=True
        ).astype(jnp.float32),
    )
    middle_grad = upstream + lax.psum_scatter(
        (outer_dot(gate_grad, full_gate) + outer_dot(up_grad, full_up)).astype(jnp.bfloat16),
        "mp",
        scatter_dimension=0,
        tiled=True,
    ).astype(jnp.float32)
    branch_grad, attn_gain_part = norm_back(branch, branch_inv, attn_scale, middle_grad)
    branch_low = branch_grad.astype(jnp.bfloat16)
    branch_full = lax.all_gather(branch_low, "mp", axis=0, tiled=True)
    out_part = inner_dot(attended, branch_full)
    mixed_grad = (
        outer_dot(branch_full, full_out)
        .astype(jnp.bfloat16)
        .reshape(group_size, local_heads, head_size)
    )
    query_grads = []
    key_grad = jnp.zeros((group_size, local_heads, head_size), jnp.float32)
    value_grad = jnp.zeros((group_size, local_heads, head_size), jnp.float32)
    for block_index in range(block_count):
        first_row = block_index * block_rows
        key_end = first_row + block_rows
        scores = block_scores(first_row, key_end)
        attn_probs = jnp.exp(scores - log_totals[block_index])
        probs_low = attn_probs.astype(jnp.bfloat16)
        grad_block = mixed_grad[first_row:key_end]
        prob_grad = jnp.einsum(
            "qhd,khd->hqk", grad_block, value_low[:key_end], preferred_element_type=jnp.float32
        )
        score_grad = (
            attn_probs * (prob_grad - jnp.sum(attn_probs * prob_grad, axis=-1, keepdims=True))
        ).astype(jnp.bfloat16)
        query_grads.append(
            jnp.einsum(
                "hqk,khd->qhd", score_grad, key_low[:key_end], preferred_element_type=jnp.float32
            )
            * score_scale
        )
        key_extra = (
            jnp.einsum(
                "hqk,qhd->khd",
                score_grad,
                query_low[first_row:key_end],
                preferred_element_type=jnp.float32,
            )
            * score_scale
        )
        value_extra = jnp.einsum(
            "hqk,qhd->khd", probs_low, grad_block, preferred_element_type=jnp.float32
        )
        padding = ((0, group_size - key_end), (0, 0), (0, 0))
        key_grad = key_grad + jnp.pad(key_extra, padding)
        value_grad = value_grad + jnp.pad(value_extra, padding)
    query_norm_grad = rotate_back(
        jnp.concatenate(query_grads, axis=0), cos_table, sin_table
    ).reshape(group_size, local_width)
    key_norm_grad = rotate_back(key_grad, cos_table, sin_table).reshape(group_size, local_width)
    query_weighted = query_norm_grad * query_scale
    key_weighted = key_norm_grad * key_scale
    query_gain_part = jnp.sum(query_norm_grad * query_raw * query_inv, axis=0).reshape(
        local_heads, head_size
    )
    key_gain_part = jnp.sum(key_norm_grad * key_raw * key_inv, axis=0).reshape(
        local_heads, head_size
    )
    query_dots, key_dots, attn_gain_sum, mlp_gain_sum = lax.psum(
        (
            jnp.sum(query_weighted * query_raw, axis=1),
            jnp.sum(key_weighted * key_raw, axis=1),
            attn_gain_part,
            mlp_gain_part,
        ),
        "mp",
    )
    query_raw_grad = (
        query_inv * query_weighted - query_raw * query_inv**3 * (query_dots / model_width)[:, None]
    ).astype(jnp.bfloat16)
    key_raw_grad = (
        key_inv * key_weighted - key_raw * key_inv**3 * (key_dots / model_width)[:, None]
    ).astype(jnp.bfloat16)
    value_low_grad = value_grad.reshape(group_size, local_width).astype(jnp.bfloat16)
    query_part = inner_dot(inputs_full, query_raw_grad)
    key_part = inner_dot(inputs_full, key_raw_grad)
    value_part = inner_dot(inputs_full, value_low_grad)
    (
        grad_query,
        grad_key,
        grad_value,
        grad_out,
        grad_query_gain,
        grad_key_gain,
        grad_attn_gain,
        grad_mlp_gain,
    ) = (
        lax.psum_scatter(
            query_part.astype(jnp.bfloat16), "dp", scatter_dimension=0, tiled=True
        ).astype(jnp.float32),
        lax.psum_scatter(
            key_part.astype(jnp.bfloat16), "dp", scatter_dimension=0, tiled=True
        ).astype(jnp.float32),
        lax.psum_scatter(
            value_part.astype(jnp.bfloat16), "dp", scatter_dimension=0, tiled=True
        ).astype(jnp.float32),
        lax.psum_scatter(
            out_part.astype(jnp.bfloat16), "dp", scatter_dimension=1, tiled=True
        ).astype(jnp.float32),
        lax.psum_scatter(
            query_gain_part.astype(jnp.bfloat16), "dp", scatter_dimension=1, tiled=True
        ).astype(jnp.float32),
        lax.psum_scatter(
            key_gain_part.astype(jnp.bfloat16), "dp", scatter_dimension=1, tiled=True
        ).astype(jnp.float32),
        lax.psum_scatter(
            attn_gain_sum.astype(jnp.bfloat16), "dp", scatter_dimension=0, tiled=True
        ).astype(jnp.float32),
        lax.psum_scatter(
            mlp_gain_sum.astype(jnp.bfloat16), "dp", scatter_dimension=0, tiled=True
        ).astype(jnp.float32),
    )
    input_grad = middle_grad + lax.psum_scatter(
        (
            outer_dot(query_raw_grad, full_query)
            + outer_dot(key_raw_grad, full_key)
            + outer_dot(value_low_grad, full_value)
        ).astype(jnp.bfloat16),
        "mp",
        scatter_dimension=0,
        tiled=True,
    ).astype(jnp.float32)
    return (
        layer_output,
        input_grad,
        grad_query,
        grad_key,
        grad_value,
        grad_out,
        grad_gate,
        grad_up,
        grad_down,
        grad_query_gain,
        grad_key_gain,
        grad_attn_gain,
        grad_mlp_gain,
    )


def solution(mesh):
    return jax.shard_map(
        local,
        mesh=mesh,
        in_specs=(
            P(("dp", "mp"), None),
            P("dp", "mp"),
            P("dp", "mp"),
            P("dp", "mp"),
            P("mp", "dp"),
            P("dp", "mp"),
            P("dp", "mp"),
            P("mp", "dp"),
            P("mp", "dp"),
            P("mp", "dp"),
            P("dp"),
            P("dp"),
            P("dp", None),
            P(("dp", "mp"), None),
        ),
        out_specs=(
            P(("dp", "mp"), None),
            P(("dp", "mp"), None),
            P("dp", "mp"),
            P("dp", "mp"),
            P("dp", "mp"),
            P("mp", "dp"),
            P("dp", "mp"),
            P("dp", "mp"),
            P("mp", "dp"),
            P("mp", "dp"),
            P("mp", "dp"),
            P("dp"),
            P("dp"),
        ),
        check_vma=False,
    )
```

profile of v0, /device:TPU:0, one launch (start us, length us, event | category | flops | bytes accessed | tf_op | source)
XLA Modules:
  0.0 1631.8 jit_solution(5138193222718099694)
XLA Ops:
  40.6 82.4 %all-gather.16.cloned.1.call-done = bf16[1024,2048]{1,0:T(8,128)(2,1)} async-done(((bf16[256,2048]{1,0:T(8,128)(2,1)}), bf16[1024,2048]{1,0:T(8,128)(2,1)}) %all-gather.16.cloned.1.call-update) | async-done | bytes 4194320 | tf_op jit(solution)/shard_map/all_gather | solution.py:129
  129.5 21.8 %all-gather.20.cloned.1.call-done = bf16[2048,512]{1,0:T(8,128)(2,1)} async-done(((bf16[256,512]{1,0:T(8,128)(2,1)}), bf16[2048,512]{1,0:T(8,128)(2,1)}) %all-gather.20.cloned.1.call-update) | async-done | bytes 2097168 | tf_op jit(solution)/shard_map/all_gather | solution.py:104
  228.0 134.9 %reduce-scatter.18.cloned.1.call-done = f32[256,2048]{1,0:T(8,128)} async-done(((f32[1024,2048]{1,0:T(8,128)}), f32[256,2048]{1,0:T(8,128)}) %reduce-scatter.18.cloned.1.call-update) | async-done | bytes 2097168 | tf_op jit(solution)/shard_map/reduce_scatter | solution.py:193
  368.1 51.7 %all-gather.28.cloned.1.call-done = bf16[2048,2048]{1,0:T(8,128)(2,1)} async-done(((bf16[256,2048]{1,0:T(8,128)(2,1)}), bf16[2048,2048]{1,0:T(8,128)(2,1)}) %all-gather.28.cloned.1.call-update) | async-done | bytes 8388624 | tf_op jit(solution)/shard_map/all_gather | solution.py:108
  419.9 82.9 %all-gather.26.cloned.1.call-done = bf16[1024,2048]{1,0:T(8,128)(2,1)} async-done(((bf16[256,2048]{1,0:T(8,128)(2,1)}), bf16[1024,2048]{1,0:T(8,128)(2,1)}) %all-gather.26.cloned.1.call-update) | async-done | bytes 4194320 | tf_op jit(solution)/shard_map/all_gather | solution.py:197
  502.8 14.6 fusion.58
  517.4 40.3 %all-gather.30.cloned.1.call-done = bf16[2048,2048]{1,0:T(8,128)(2,1)} async-done(((bf16[256,2048]{1,0:T(8,128)(2,1)}), bf16[2048,2048]{1,0:T(8,128)(2,1)}) %all-gather.30.cloned.1.call-update) | async-done | bytes 8388624 | tf_op jit(solution)/shard_map/all_gather | solution.py:109
  557.7 17.0 %multiply_convert_fusion.3 = (bf16[1024,2048]{1,0:T(8,128)(2,1)}, f32[1024,2048]{1,0:T(8,128)}) fusion(f32[1024,2048]{1,0:T(8,128)} %fusion.58, bf16[1024,2048]{1,0:T(8,128)(2,1)} %all-gather.26.cloned.1.call-done, bf16[2048,2048]{1,0:T(8,128)(2,1)} %all-gather.30.cloned.1.call-done), kind=kOutput, calls=%fused_computation.7 | convolution fusion | flops 8602517504 | bytes 33554432 | tf_op jit(solution)/shard_map/dot_general | solution.py:14
  574.6 40.8 %all-gather.32.cloned.1.call-done = bf16[2048,2048]{1,0:T(8,128)(2,1)} async-done(((bf16[2048,256]{1,0:T(8,128)(2,1)}), bf16[2048,2048]{1,0:T(8,128)(2,1)}) %all-gather.32.cloned.1.call-update) | async-done | bytes 8388624 | tf_op jit(solution)/shard_map/all_gather | solution.py:110
  640.2 134.4 %reduce-scatter.20.cloned.1.call-done = f32[256,2048]{1,0:T(8,128)} async-done(((f32[1024,2048]{1,0:T(8,128)}), f32[256,2048]{1,0:T(8,128)}) %reduce-scatter.20.cloned.1.call-update) | async-done | bytes 2097168 | tf_op jit(solution)/shard_map/reduce_scatter | solution.py:203
  779.8 81.6 %all-gather.34.cloned.1.call-done = bf16[1024,2048]{1,0:T(8,128)(2,1)} async-done(((bf16[256,2048]{1,0:T(8,128)(2,1)}), bf16[1024,2048]{1,0:T(8,128)(2,1)}) %all-gather.34.cloned.1.call-update) | async-done | bytes 4194320 | tf_op jit(solution)/shard_map/all_gather | solution.py:235
  861.4 20.6 %multiply_convert_fusion.1 = (bf16[1024,2048]{1,0:T(8,128)(2,1)}, bf16[1024,2048]{1,0:T(8,128)(2,1)}) fusion(f32[1024,2048]{1,0:T(8,128)} %fusion.58, f32[1024,2048]{1,0:T(8,128)} %get-tuple-element.134, bf16[1024,2048]{1,0:T(8,128)(2,1)} %all-gather.34.cloned.1.call-done, bf16[2048,2048]{1,0:T(8,128)(2,1)} %all-gather.32.cloned.1.call-done), kind=kOutput, calls=%fused_computation.5 | convolution fusion | flops 8617197568 | bytes 37748736 | tf_op jit(solution)/shard_map/dot_general | solution.py:24
  907.9 75.4 %reduce-scatter.22.cloned.1.call-done = bf16[256,2048]{1,0:T(8,128)(2,1)} async-done(((bf16[1024,2048]{1,0:T(8,128)(2,1)}), bf16[256,2048]{1,0:T(8,128)(2,1)}) %reduce-scatter.22.cloned.1.call-update) | async-done | bytes 1048592 | tf_op jit(solution)/shard_map/reduce_scatter | solution.py:255
  1033.4 36.5 %all-gather.36.cloned.1.call-done = bf16[1024,2048]{1,0:T(8,128)(2,1)} async-done(((bf16[256,2048]{1,0:T(8,128)(2,1)}), bf16[1024,2048]{1,0:T(8,128)(2,1)}) %all-gather.36.cloned.1.call-update) | async-done | bytes 4194320 | tf_op jit(solution)/shard_map/all_gather | solution.py:263
  1139.8 15.9 all-reduce.4
  1191.2 26.9 %reduce-scatter.34.cloned.1.call-done = bf16[256,2048]{1,0:T(8,128)(2,1)} async-done(((bf16[2048,2048]{1,0:T(8,128)(2,1)}), bf16[256,2048]{1,0:T(8,128)(2,1)}) %reduce-scatter.34.cloned.1.call-update) | async-done | bytes 1048592 | tf_op jit(solution)/shard_map/reduce_scatter | solution.py:245
  1220.8 72.2 %reduce-scatter.36.cloned.1.call-done = bf16[256,2048]{1,0:T(8,128)(2,1)} async-done(((bf16[2048,2048]{1,0:T(8,128)(2,1)}), bf16[256,2048]{1,0:T(8,128)(2,1)}) %reduce-scatter.36.cloned.1.call-update) | async-done | bytes 1048592 | tf_op jit(solution)/shard_map/reduce_scatter | solution.py:248
  1310.3 17.6 %reduce-scatter.42.cloned.1.call-done = bf16[16,4]{1,0:T(8,128)(2,1)} async-done(((bf16[128,4]{1,0:T(8,128)(2,1)}), bf16[16,4]{1,0:T(8,128)(2,1)}) %reduce-scatter.42.cloned.1.call-update) | async-done | bytes 144
  1329.2 33.8 %reduce-scatter.40.cloned.1.call-done = bf16[16,4]{1,0:T(8,128)(2,1)} async-done(((bf16[128,4]{1,0:T(8,128)(2,1)}), bf16[16,4]{1,0:T(8,128)(2,1)}) %reduce-scatter.40.cloned.1.call-update) | async-done | bytes 144
  1364.3 43.0 %reduce-scatter.32.cloned.1.call-done = bf16[512,256]{1,0:T(8,128)(2,1)} async-done(((bf16[512,2048]{1,0:T(8,128)(2,1)}), bf16[512,256]{1,0:T(8,128)(2,1)}) %reduce-scatter.32.cloned.1.call-update) | async-done | bytes 262160 | tf_op jit(solution)/shard_map/reduce_scatter | solution.py:357
  1409.1 43.2 %reduce-scatter.30.cloned.1.call-done = bf16[256,512]{0,1:T(8,128)(2,1)} async-done(((bf16[2048,512]{0,1:T(8,128)(2,1)}), bf16[256,512]{0,1:T(8,128)(2,1)}) %reduce-scatter.30.cloned.1.call-update) | async-done | bytes 262160 | tf_op jit(solution)/shard_map/reduce_scatter | solution.py:354
  1454.2 42.7 %reduce-scatter.28.cloned.1.call-done = bf16[256,512]{0,1:T(8,128)(2,1)} async-done(((bf16[2048,512]{0,1:T(8,128)(2,1)}), bf16[256,512]{0,1:T(8,128)(2,1)}) %reduce-scatter.28.cloned.1.call-update) | async-done | bytes 262160 | tf_op jit(solution)/shard_map/reduce_scatter | solution.py:351
  1498.7 43.6 %reduce-scatter.26.cloned.1.call-done = bf16[256,512]{0,1:T(8,128)(2,1)} async-done(((bf16[2048,512]{0,1:T(8,128)(2,1)}), bf16[256,512]{0,1:T(8,128)(2,1)}) %reduce-scatter.26.cloned.1.call-update) | async-done | bytes 262160 | tf_op jit(solution)/shard_map/reduce_scatter | solution.py:348
  1544.2 77.0 %reduce-scatter.24.cloned.1.call-done = bf16[256,2048]{1,0:T(8,128)(2,1)} async-done(((bf16[1024,2048]{1,0:T(8,128)(2,1)}), bf16[256,2048]{1,0:T(8,128)(2,1)}) %reduce-scatter.24.cloned.1.call-update) | async-done | bytes 1048592 | tf_op jit(solution)/shard_map/reduce_scatter | solution.py:373
  (336 shorter events, 364.5 us)
Async XLA Ops:
  7.2 33.4 %all-gather.22.cloned.1.call-start = ((), (), s32[]{:S(2)}) async-start(), calls=%async_computation.16 | async-start | bytes 2359296 | tf_op jit(solution)/shard_map/all_gather | solution.py:105
  7.9 115.0 %all-gather.16.cloned.1.call-start = ((), (), s32[]{:S(2)}) async-start(), calls=%async_computation.13 | async-start | bytes 5242880 | tf_op jit(solution)/shard_map/all_gather | solution.py:129
  8.7 142.6 %all-gather.20.cloned.1.call-start = ((), (), s32[]{:S(2)}) async-start(), calls=%async_computation.15 | async-start | bytes 2359296 | tf_op jit(solution)/shard_map/all_gather | solution.py:104
  9.4 177.0 %all-gather.18.cloned.1.call-start = ((), (), s32[]{:S(2)}) async-start(), calls=%async_computation.14 | async-start | bytes 2359296 | tf_op jit(solution)/shard_map/all_gather | solution.py:106
  10.0 200.9 %all-gather.24.cloned.1.call-start = ((), (), s32[]{:S(2)}) async-start(), calls=%async_computation.17 | async-start | bytes 2359296 | tf_op jit(solution)/shard_map/all_gather | solution.py:107
  10.6 352.3 %reduce-scatter.18.cloned.1.call-start = ((), (), s32[]{:S(2)}) async-start(), calls=%async_computation.18 | async-start | bytes 10485760 | tf_op jit(solution)/shard_map/reduce_scatter | solution.py:193
  218.2 201.6 %all-gather.28.cloned.1.call-start = ((), (), s32[]{:S(2)}) async-start(), calls=%async_computation.20 | async-start | bytes 9437184 | tf_op jit(solution)/shard_map/all_gather | solution.py:108
  219.0 283.8 %all-gather.26.cloned.1.call-start = ((), (), s32[]{:S(2)}) async-start(), calls=%async_computation.19 | async-start | bytes 5242880 | tf_op jit(solution)/shard_map/all_gather | solution.py:197
  366.8 190.9 %all-gather.30.cloned.1.call-start = ((), (), s32[]{:S(2)}) async-start(), calls=%async_computation.21 | async-start | bytes 9437184 | tf_op jit(solution)/shard_map/all_gather | solution.py:109
  367.5 247.9 %all-gather.32.cloned.1.call-start = ((), (), s32[]{:S(2)}) async-start(), calls=%async_computation.22 | async-start | bytes 9437184 | tf_op jit(solution)/shard_map/all_gather | solution.py:110
  368.1 406.5 %reduce-scatter.20.cloned.1.call-start = ((), (), s32[]{:S(2)}) async-start(), calls=%async_computation.23 | async-start | bytes 10485760 | tf_op jit(solution)/shard_map/reduce_scatter | solution.py:203
  630.0 231.4 %all-gather.34.cloned.1.call-start = ((), (), s32[]{:S(2)}) async-start(), calls=%async_computation.24 | async-start | bytes 5242880 | tf_op jit(solution)/shard_map/all_gather | solution.py:235
  779.8 203.5 %reduce-scatter.22.cloned.1.call-start = ((), (), s32[]{:S(2)}) async-start(), calls=%async_computation.25 | async-start | bytes 5242880 | tf_op jit(solution)/shard_map/reduce_scatter | solution.py:255
  907.9 162.0 %all-gather.36.cloned.1.call-start = ((), (), s32[]{:S(2)}) async-start(), calls=%async_computation.26 | async-start | bytes 5242880 | tf_op jit(solution)/shard_map/all_gather | solution.py:263
  988.5 200.0 %reduce-scatter.38.cloned.1.call-start = ((), (), s32[]{:S(2)}) async-start(), calls=%async_computation.34 | async-start | bytes 9437184 | tf_op jit(solution)/shard_map/reduce_scatter | solution.py:251
  1002.6 215.5 %reduce-scatter.34.cloned.1.call-start = ((), (), s32[]{:S(2)}) async-start(), calls=%async_computation.32 | async-start | bytes 9437184 | tf_op jit(solution)/shard_map/reduce_scatter | solution.py:245
  1017.2 275.9 %reduce-scatter.36.cloned.1.call-start = ((), (), s32[]{:S(2)}) async-start(), calls=%async_computation.33 | async-start | bytes 9437184 | tf_op jit(solution)/shard_map/reduce_scatter | solution.py:248
  1031.3 296.5 %reduce-scatter.42.cloned.1.call-start = ((), (), s32[]{:S(2)}) async-start(), calls=%async_computation.36 | async-start | bytes 36864
  1103.9 259.0 %reduce-scatter.40.cloned.1.call-start = ((), (), s32[]{:S(2)}) async-start(), calls=%async_computation.35 | async-start | bytes 36864
  1119.3 288.0 %reduce-scatter.32.cloned.1.call-start = ((), (), s32[]{:S(2)}) async-start(), calls=%async_computation.31 | async-start | bytes 2359296 | tf_op jit(solution)/shard_map/reduce_scatter | solution.py:357
  1125.7 326.6 %reduce-scatter.30.cloned.1.call-start = ((), (), s32[]{:S(2)}) async-start(), calls=%async_computation.30 | async-start | bytes 2359296 | tf_op jit(solution)/shard_map/reduce_scatter | solution.py:354
  1139.1 357.7 %reduce-scatter.28.cloned.1.call-start = ((), (), s32[]{:S(2)}) async-start(), calls=%async_computation.29 | async-start | bytes 2359296 | tf_op jit(solution)/shard_map/reduce_scatter | solution.py:351
  1165.0 377.3 %reduce-scatter.26.cloned.1.call-start = ((), (), s32[]{:S(2)}) async-start(), calls=%async_computation.28 | async-start | bytes 2359296 | tf_op jit(solution)/shard_map/reduce_scatter | solution.py:348
  1172.5 448.8 %reduce-scatter.24.cloned.1.call-start = ((), (), s32[]{:S(2)}) async-start(), calls=%async_computation.27 | async-start | bytes 5242880 | tf_op jit(solution)/shard_map/reduce_scatter | solution.py:373
  (81 other events, 1591.6 us)
Sparse Core Ops, SparseCore 0:
  9.9 30.5 all-gather.21
  42.1 80.7 all-gather.15
  124.8 26.4 all-gather.19
  153.0 27.8 all-gather.17
  182.7 28.1 all-gather.23
  218.3 144.4 reduce-scatter.17
  364.7 55.0 all-gather.27
  422.0 80.7 all-gather.25
  504.7 52.9 all-gather.29
  559.4 55.9 all-gather.31
  630.1 144.4 reduce-scatter.19
  779.9 81.4 all-gather.33
  908.0 75.2 reduce-scatter.21
  988.6 81.2 all-gather.35
  1073.6 69.7 reduce-scatter.37
  1146.7 71.2 reduce-scatter.33
  1221.8 71.2 reduce-scatter.35
  1296.5 31.2 reduce-scatter.41
  1331.7 31.2 reduce-scatter.39
  1366.1 41.2 reduce-scatter.31
  1411.0 41.2 reduce-scatter.29
  1455.6 41.2 reduce-scatter.27
  1501.1 41.2 reduce-scatter.25
  1544.5 76.7 reduce-scatter.23
where the time goes:
time: 1640 us; the launch traced here: 1630 us
  waiting for transfers between devices  1200 us (73%)
  matrix products  219 us (13%)
  blocking collectives  78 us (5%)
  other arithmetic  77.6 us (5%)
  local copies, waits for them, and re-layouts  39.8 us (2%)
  between operations  16.5 us (1%)
    reduce_scatter x1, waiting for transfers between devices, local(): lax.psum_scatter(plain_dot(attended, full_out), 'mp', scatter_dimension=0...  135 us
    reduce_scatter x1, waiting for transfers between devices, local(): lax.psum_scatter(plain_dot(hidden, full_down), 'mp', scatter_dimension=0,...  134 us
    all_gather x1, waiting for transfers between devices, local(): lax.all_gather(middle.astype(jnp.bfloat16), 'mp', axis=0, tiled=True)  82.9 us
    all_gather x1, waiting for transfers between devices, local(): inputs_full = lax.all_gather(layer_input, 'mp', axis=0, tiled=True)  82.4 us
    all_gather x1, waiting for transfers between devices, local(): lax.all_gather(mlp_grad.astype(jnp.bfloat16), 'mp', axis=0, tiled=True)  81.6 us
    reduce_scatter x1, waiting for transfers between devices, local(): lax.psum_scatter((outer_dot(query_raw_grad, full_query) + outer_dot(key_r...  77 us
    reduce_scatter x1, waiting for transfers between devices, local(): lax.psum_scatter((outer_dot(gate_grad, full_gate) + outer_dot(up_grad, fu...  75.4 us
    reduce_scatter x1, waiting for transfers between devices, local(): lax.psum_scatter(up_part.astype(jnp.bfloat16), 'dp', scatter_dimension=0,...  72.2 us
  transfers between devices with their start and end apart: 24, of which 22 were waited for; matrix products, arithmetic and copies ran while one was open for 15% of the time, Pallas kernels for 0%

commit v1 on v0

v1 whole, which is shorter than its diff:
```python
import functools
import math

import jax
import jax.numpy as jnp
from jax import lax
from jax.experimental import pallas as pl
from jax.experimental.pallas import tpu as pltpu
from jax.sharding import PartitionSpec as P

EPS = 1e-06
THETA = 500000.0
MASKED = -1000000000.0
CHUNKS = 4
STAGGER = 2
TILE = 256
QUERY_ROWS = 256
BF = jnp.bfloat16
F32 = jnp.float32
MIB = 1 << 20
HBM = pl.BlockSpec(memory_space=pl.ANY)
VMEM = pl.BlockSpec(memory_space=pltpu.VMEM)


def plain_dot(former, latter):
    return jnp.dot(former, latter, preferred_element_type=F32)


def inner_dot(former, latter):
    return lax.dot_general(
        former, latter, (((0,), (0,)), ((), ())), preferred_element_type=F32
    )


def outer_dot(former, latter):
    return lax.dot_general(
        former, latter, (((1,), (1,)), ((), ())), preferred_element_type=F32
    )


def layout(lengths, group_size):
    slot_count = lengths.shape[0]
    seq_ends = jnp.cumsum(lengths, dtype=jnp.int32)
    starts = seq_ends - lengths
    places = jnp.arange(group_size, dtype=jnp.int32)
    slot_ids = jnp.arange(slot_count, dtype=jnp.int32)
    segment = jnp.sum(
        (places[:, None] >= seq_ends[None, :]).astype(jnp.int32), axis=1, dtype=jnp.int32
    )
    chosen = (segment[:, None] == slot_ids[None, :]).astype(jnp.int32)
    padded = (segment == slot_count).astype(jnp.int32)
    begins = (
        jnp.sum(chosen * starts[None, :], axis=1, dtype=jnp.int32)
        + padded * seq_ends[slot_count - 1]
    )
    return (begins, places - begins, places < seq_ends[slot_count - 1])


def rotary_tables(positions, head_size):
    half_dim = head_size // 2
    frequency = jnp.exp(jnp.arange(half_dim, dtype=F32) * (-2.0 * math.log(THETA) / head_size))
    angles = positions.astype(F32)[:, None] * frequency[None, :]
    cos_half, sin_half = jnp.cos(angles), jnp.sin(angles)
    return (
        jnp.concatenate([cos_half, cos_half], axis=1),
        jnp.concatenate([-sin_half, sin_half], axis=1),
    )


def neighbour_barrier(me, n):
    barrier = pltpu.get_barrier_semaphore()

    @pl.when(me > 0)
    def _():
        pl.semaphore_signal(barrier, inc=1, device_id={"mp": me - 1})

    @pl.when(me < n - 1)
    def _():
        pl.semaphore_signal(barrier, inc=1, device_id={"mp": me + 1})

    pl.semaphore_wait(barrier, jnp.minimum(me, 1) + jnp.minimum(n - 1 - me, 1))


class LineGather:
    def __init__(self, n, me, own, full, send_sem, recv_sem, local_sem):
        self.n, self.me, self.own, self.full = n, me, own, full
        self.send_sem, self.recv_sem, self.local_sem = send_sem, recv_sem, local_sem

    def local_copy(self, c):
        return pltpu.make_async_copy(self.own(c), self.full(self.me, c), self.local_sem.at[c])

    def copy(self, c, step, way, block, src):
        return pltpu.make_async_remote_copy(
            src_ref=src,
            dst_ref=self.full(block, c),
            send_sem=self.send_sem.at[c, step - 1, way],
            recv_sem=self.recv_sem.at[c, step - 1, way],
            device_id={"mp": self.me + (1 if way == 0 else -1)},
        )

    def sides(self):
        return ((0, self.me), (1, self.n - 1 - self.me))

    def block_at(self, way, step):
        return self.me - step if way == 0 else self.me + step

    def step(self, c, step):
        n = self.n
        if step == 1:
            self.local_copy(c).start()
        for way, place in self.sides():
            if step > 1:

                @pl.when(place >= step - 1)
                def _(way=way):
                    block = self.block_at(way, step - 1)
                    self.copy(c, step - 1, way, block, self.own(c)).wait_recv()

            @pl.when((place >= step - 1) & (place < n - 1))
            def _(way=way):
                block = self.block_at(way, step - 1)
                src = self.own(c) if step == 1 else self.full(block, c)
                self.copy(c, step, way, block, src).start()

    def last(self, c):
        n = self.n
        for way, place in self.sides():

            @pl.when(place == n - 1)
            def _(way=way):
                block = self.block_at(way, n - 1)
                self.copy(c, n - 1, way, block, self.own(c)).wait_recv()

    def drain(self, c):
        self.local_copy(c).wait()
        for step in range(1, self.n):
            for way, place in self.sides():

                @pl.when((place >= step - 1) & (place < self.n - 1))
                def _(way=way):
                    self.copy(c, step, way, self.me, self.own(c)).wait_send()


class LineScatter:
    def __init__(self, n, me, rows, part, send, recv, send_sem, recv_sem):
        self.n, self.me, self.rows = n, me, rows
        self.part, self.send, self.recv = part, send, recv
        self.send_sem, self.recv_sem = send_sem, recv_sem

    def piece(self, c, owner):
        first = pl.multiple_of(owner * self.rows, self.rows)
        return self.part.at[c, pl.ds(first, self.rows)]

    def copy(self, c, step, way, src):
        return pltpu.make_async_remote_copy(
            src_ref=src,
            dst_ref=self.recv.at[c, step, way],
            send_sem=self.send_sem.at[c, step, way],
            recv_sem=self.recv_sem.at[c, step, way],
            device_id={"mp": self.me + (1 if way == 0 else -1)},
        )

    def sides(self):
        return ((0, self.me), (1, self.n - 1 - self.me))

    def step(self, c, step):
        n = self.n
        for way, place in self.sides():
            owner = n - 1 - step + self.me if way == 0 else step - (n - 1 - self.me)

            @pl.when(place == 0)
            def _(way=way, owner=owner):
                self.copy(c, step, way, self.piece(c, owner)).start()

            if step > 0:

                @pl.when((place > 0) & (place <= min(step, n - 2)))
                def _(way=way, owner=owner):
                    slot = self.send.at[c, step - 1, way]
                    self.copy(c, step - 1, way, slot).wait_recv()
                    slot[...] = (
                        self.piece(c, owner)[...].astype(F32)
                        + self.recv[c, step - 1, way].astype(F32)
                    ).astype(BF)
                    self.copy(c, step, way, slot).start()

    def total(self, c, out):
        n = self.n
        out[...] = self.piece(c, self.me)[...].astype(F32)
        for way, place in self.sides():

            @pl.when(place > 0)
            def _(way=way):
                self.copy(c, n - 2, way, self.recv.at[c, n - 2, way]).wait_recv()
                out[...] += self.recv[c, n - 2, way].astype(F32)

    def drain(self, c):
        n = self.n
        for step in range(n - 1):
            for way, place in self.sides():

                @pl.when(place <= min(step, n - 2))
                def _(way=way):
                    self.copy(c, step, way, self.recv.at[c, step, way]).wait_send()


def run_line(n, chunks, stagger, compute, scatter, row_work, gather):
    last_step = 2 * n - 2 if gather is not None else n - 1
    events = sorted(
        (step + stagger * c, c, step) for c in range(chunks) for step in range(last_step + 1)
    )
    for _, c, step in events:
        if step < n - 1:
            if step == 0:
                compute(c)
            scatter.step(c, step)
        elif step == n - 1:
            row_work(c)
            if gather is not None:
                gather.step(c, 1)
        elif step < 2 * n - 2:
            gather.step(c, step - n + 2)
        else:
            gather.last(c)
    for c in range(chunks):
        scatter.drain(c)
        if gather is not None:
            gather.drain(c)


def inverse_rms(rows):
    return lax.rsqrt(jnp.mean(rows * rows, axis=1, keepdims=True) + EPS)


def norm_back(values, inverse, gain_row, upstream):
    weighted = upstream * gain_row
    mean_term = jnp.mean(weighted * values, axis=1, keepdims=True)
    grad_values = inverse * weighted - values * (inverse * inverse * inverse) * mean_term
    return (grad_values, jnp.sum(upstream * values * inverse, axis=0, keepdims=True))


def scatter_scratch(n, rows, width):
    return [
        pltpu.VMEM((CHUNKS, n * rows, width), BF),
        pltpu.VMEM((CHUNKS, max(n - 2, 1), 2, rows, width), BF),
        pltpu.VMEM((CHUNKS, n - 1, 2, rows, width), BF),
        pltpu.SemaphoreType.DMA((CHUNKS, n - 1, 2)),
        pltpu.SemaphoreType.DMA((CHUNKS, n - 1, 2)),
        pltpu.VMEM((rows, width), F32),
    ]


def gather_scratch(n, rows, width):
    return [
        pltpu.VMEM((CHUNKS, rows, width), BF),
        pltpu.SemaphoreType.DMA((CHUNKS, n - 1, 2)),
        pltpu.SemaphoreType.DMA((CHUNKS, n - 1, 2)),
        pltpu.SemaphoreType.DMA((CHUNKS,)),
    ]


def chunk_span(c, rows):
    return pl.ds(c * rows, rows)


def make_gather(n, me, rows, own, full, send_sem, recv_sem, local_sem):
    return LineGather(
        n,
        me,
        lambda c: own.at[c],
        lambda block, c: full.at[block, chunk_span(c, rows)],
        send_sem,
        recv_sem,
        local_sem,
    )


def gather_rows_kernel(n, rows, block, full, send_sem, recv_sem, local_sem):
    me = lax.axis_index("mp")
    neighbour_barrier(me, n)
    gather = LineGather(
        n,
        me,
        lambda c: block.at[chunk_span(c, rows)],
        lambda index, c: full.at[index, chunk_span(c, rows)],
        send_sem,
        recv_sem,
        local_sem,
    )
    for step in range(1, n):
        for c in range(CHUNKS):
            gather.step(c, step)
    for c in range(CHUNKS):
        gather.last(c)
    for c in range(CHUNKS):
        gather.drain(c)


def gather_rows(n, block):
    rows = block.shape[0] // CHUNKS
    sems = gather_scratch(n, rows, block.shape[1])[1:]
    return pl.pallas_call(
        functools.partial(gather_rows_kernel, n, rows),
        out_shape=jax.ShapeDtypeStruct((n,) + block.shape, block.dtype),
        in_specs=[HBM],
        out_specs=HBM,
        scratch_shapes=sems,
        compiler_params=pltpu.CompilerParams(collective_id=0, has_side_effects=True),
        name="gather_rows",
    )(block)


def attn_out_kernel(
    n, rows, att, wo, x, scale, branch, middle, full,
    part, send, recv, rs_send_sem, rs_recv_sem, total, own, ag_send_sem, ag_recv_sem, local_sem,
    packed,
):
    me = lax.axis_index("mp")
    neighbour_barrier(me, n)
    width = wo.shape[1]
    block_rows = rows * CHUNKS

    def compute(c):
        for j in range(n):
            packed[j * rows : (j + 1) * rows] = att[
                j * block_rows + c * rows : j * block_rows + (c + 1) * rows
            ]

        @pl.loop(0, width // (2 * TILE))
        def _(tile):
            cols = pl.ds(pl.multiple_of(tile * 2 * TILE, 2 * TILE), 2 * TILE)
            part[c, :, cols] = plain_dot(packed[...], wo[:, cols]).astype(BF)

    scatter = LineScatter(n, me, rows, part, send, recv, rs_send_sem, rs_recv_sem)
    gather = make_gather(n, me, rows, own, full, ag_send_sem, ag_recv_sem, local_sem)

    def row_work(c):
        scatter.total(c, total)
        span = chunk_span(c, rows)
        value = total[...]
        branch[span] = value
        new = x[span].astype(F32) + value * inverse_rms(value) * scale[...]
        middle[span] = new
        own[c] = new.astype(BF)

    run_line(n, CHUNKS, STAGGER, compute, scatter, row_work, gather)


def attn_out(n, attended, full_out, layer_input, scale):
    row_count, width = layer_input.shape
    rows = row_count // CHUNKS
    return pl.pallas_call(
        functools.partial(attn_out_kernel, n, rows),
        out_shape=(
            jax.ShapeDtypeStruct((row_count, width), F32),
            jax.ShapeDtypeStruct((row_count, width), F32),
            jax.ShapeDtypeStruct((n, row_count, width), BF),
        ),
        in_specs=[VMEM] * 4,
        out_specs=(VMEM, VMEM, HBM),
        scratch_shapes=scatter_scratch(n, rows, width)
        + gather_scratch(n, rows, width)
        + [pltpu.VMEM((n * rows, attended.shape[1]), BF)],
        compiler_params=pltpu.CompilerParams(
            collective_id=1, has_side_effects=True, vmem_limit_bytes=56 * MIB
        ),
        name="attn_out",
    )(attended, full_out, layer_input, scale)


class WeightTiles:
    def __init__(self, source, held, sem, axis, size):
        self.source, self.held, self.sem, self.axis, self.size = source, held, sem, axis, size
        self.count = source.shape[axis] // size

    def at(self, ref, tile):
        span = pl.ds(pl.multiple_of(tile * self.size, self.size), self.size)
        return ref.at[:, span] if self.axis == 1 else ref.at[span]

    def copy(self, tile):
        return pltpu.make_async_copy(
            self.at(self.source, tile), self.at(self.held, tile), self.sem.at[tile]
        )

    def start(self):
        for tile in range(self.count):
            self.copy(tile).start()


def mlp_forward_kernel(
    n, rows, h_full, wg, wu, wd, middle, upstream_in, row_valid, scale,
    output, dm_full, gate_out, up_out, hidden_out, gain_out,
    part, send, recv, rs_send_sem, rs_recv_sem, total, own, ag_send_sem, ag_recv_sem, local_sem,
    vg, vu, vd, wsem, h_buf, h_sem, gate_buf, up_buf, hidden_buf, out_sem,
):
    me = lax.axis_index("mp")
    width, hidden_width = wg.shape

    def h_copy(c, j):
        return pltpu.make_async_copy(
            h_full.at[j, chunk_span(c, rows)],
            h_buf.at[c % 2, pl.ds(j * rows, rows)],
            h_sem.at[c % 2, j],
        )

    for j in range(n):
        h_copy(0, j).start()
    gate_tiles = WeightTiles(wg, vg, wsem.at[0], 1, TILE)
    up_tiles = WeightTiles(wu, vu, wsem.at[1], 1, TILE)
    down_tiles = WeightTiles(wd, vd, wsem.at[2], 1, TILE)
    for tile in range(gate_tiles.count):
        gate_tiles.copy(tile).start()
        up_tiles.copy(tile).start()
    down_tiles.start()
    neighbour_barrier(me, n)

    def save_copies(c, j):
        slot = c % 2
        span = pl.ds(j * rows, rows)
        return [
            pltpu.make_async_copy(
                buf.at[slot, span], out.at[j, chunk_span(c, rows)], out_sem.at[slot, k, j]
            )
            for k, (buf, out) in enumerate(
                ((gate_buf, gate_out), (up_buf, up_out), (hidden_buf, hidden_out))
            )
        ]

    def compute(c):
        slot = c % 2
        for j in range(n):
            h_copy(c, j).wait()
        if c + 1 < CHUNKS:
            for j in range(n):
                h_copy(c + 1, j).start()
        if c >= 2:
            for j in range(n):
                for copy in save_copies(c - 2, j):
                    copy.wait()

        @pl.loop(0, hidden_width // TILE)
        def _(tile):
            if c == 0:
                gate_tiles.copy(tile).wait()
                up_tiles.copy(tile).wait()
            cols = pl.ds(pl.multiple_of(tile * TILE, TILE), TILE)
            gate = plain_dot(h_buf[slot], vg[:, cols])
            up = plain_dot(h_buf[slot], vu[:, cols])
            gate_buf[slot, :, cols] = gate.astype(BF)
            up_buf[slot, :, cols] = up.astype(BF)
            hidden_buf[slot, :, cols] = (gate * jax.nn.sigmoid(gate) * up).astype(BF)

        for j in range(n):
            for copy in save_copies(c, j):
                copy.start()

        @pl.loop(0, width // TILE)
        def _(tile):
            if c == 0:
                down_tiles.copy(tile).wait()
            cols = pl.ds(pl.multiple_of(tile * TILE, TILE), TILE)
            part[c, :, cols] = plain_dot(hidden_buf[slot], vd[:, cols]).astype(BF)

    scatter = LineScatter(n, me, rows, part, send, recv, rs_send_sem, rs_recv_sem)
    gather = make_gather(n, me, rows, own, dm_full, ag_send_sem, ag_recv_sem, local_sem)

    def row_work(c):
        scatter.total(c, total)
        span = chunk_span(c, rows)
        value = total[...]
        inverse = inverse_rms(value)
        output[span] = (middle[span] + value * inverse * scale[...]).astype(BF)
        upstream = upstream_in[span].astype(F32) * row_valid[span]
        grad, gain = norm_back(value, inverse, scale[...], upstream)
        own[c] = grad.astype(BF)
        gain_out[...] = gain if c == 0 else gain_out[...] + gain

    run_line(n, CHUNKS, STAGGER, compute, scatter, row_work, gather)
    for c in range(max(CHUNKS - 2, 0), CHUNKS):
        for j in range(n):
            for copy in save_copies(c, j):
                copy.wait()


def mlp_forward(n, h_full, wg, wu, wd, middle, out_grad, row_valid, scale):
    row_count, width = middle.shape
    hidden_width = wg.shape[1]
    rows = row_count // CHUNKS
    saved = jax.ShapeDtypeStruct((n, row_count, hidden_width), BF)
    most = max(width, hidden_width) // TILE
    return pl.pallas_call(
        functools.partial(mlp_forward_kernel, n, rows),
        out_shape=(
            jax.ShapeDtypeStruct((row_count, width), BF),
            jax.ShapeDtypeStruct((n, row_count, width), BF),
            saved,
            saved,
            saved,
            jax.ShapeDtypeStruct((1, width), F32),
        ),
        in_specs=[HBM] * 4 + [VMEM] * 4,
        out_specs=(VMEM, HBM, HBM, HBM, HBM, VMEM),
        scratch_shapes=scatter_scratch(n, rows, width)
        + gather_scratch(n, rows, width)
        + [
            pltpu.VMEM(wg.shape, BF),
            pltpu.VMEM(wu.shape, BF),
            pltpu.VMEM(wd.shape, BF),
            pltpu.SemaphoreType.DMA((3, most)),
            pltpu.VMEM((2, n * rows, width), BF),
            pltpu.SemaphoreType.DMA((2, n)),
        ]
        + [pltpu.VMEM((2, n * rows, hidden_width), BF)] * 3
        + [pltpu.SemaphoreType.DMA((2, 3, n))],
        compiler_params=pltpu.CompilerParams(
            collective_id=2, has_side_effects=True, vmem_limit_bytes=60 * MIB
        ),
        name="mlp_forward",
    )(h_full, wg, wu, wd, middle, out_grad, row_valid, scale)


def mlp_backward_kernel(
    n, rows, dm_full, wg, wu, wd, gate_in, up_in, branch, upstream_in, row_valid, scale,
    middle_grad, da_full, gate_grad, up_grad, gain_out,
    part, send, recv, rs_send_sem, rs_recv_sem, total, own, ag_send_sem, ag_recv_sem, local_sem,
    vg, vu, vd, wsem, dm_buf, gate_buf, up_buf, in_sem, dgate_buf, dup_buf, out_sem,
):
    me = lax.axis_index("mp")
    width, hidden_width = wg.shape

    def in_copies(c, j):
        span = pl.ds(j * rows, rows)
        return [
            pltpu.make_async_copy(
                source.at[j, chunk_span(c, rows)], buf.at[span], in_sem.at[k, j]
            )
            for k, (source, buf) in enumerate(
                ((dm_full, dm_buf), (gate_in, gate_buf), (up_in, up_buf))
            )
        ]

    for j in range(n):
        for copy in in_copies(0, j):
            copy.start()
    down_tiles = WeightTiles(wd, vd, wsem.at[0], 0, TILE)
    gate_tiles = WeightTiles(wg, vg, wsem.at[1], 0, TILE)
    up_tiles = WeightTiles(wu, vu, wsem.at[2], 0, TILE)
    down_tiles.start()
    for tile in range(gate_tiles.count):
        gate_tiles.copy(tile).start()
        up_tiles.copy(tile).start()
    neighbour_barrier(me, n)

    def save_copies(c, j):
        slot = c % 2
        span = pl.ds(j * rows, rows)
        return [
            pltpu.make_async_copy(
                buf.at[slot, span], out.at[j, chunk_span(c, rows)], out_sem.at[slot, k, j]
            )
            for k, (buf, out) in enumerate(((dgate_buf, gate_grad), (dup_buf, up_grad)))
        ]

    def compute(c):
        slot = c % 2
        for j in range(n):
            for copy in in_copies(c, j):
                copy.wait()
        if c >= 2:
            for j in range(n):
                for copy in save_copies(c - 2, j):
                    copy.wait()

        @pl.loop(0, hidden_width // TILE)
        def _(tile):
            if c == 0:
                down_tiles.copy(tile).wait()
            cols = pl.ds(pl.multiple_of(tile * TILE, TILE), TILE)
            hidden_grad = outer_dot(dm_buf[...], vd[cols, :])
            gate = gate_buf[:, cols].astype(F32)
            up = up_buf[:, cols].astype(F32)
            sigmoid = jax.nn.sigmoid(gate)
            dgate_buf[slot, :, cols] = (
                hidden_grad * up * sigmoid * (1.0 + gate * (1.0 - sigmoid))
            ).astype(BF)
            dup_buf[slot, :, cols] = (hidden_grad * gate * sigmoid).astype(BF)

        if c + 1 < CHUNKS:
            for j in range(n):
                for copy in in_copies(c + 1, j):
                    copy.start()
        for j in range(n):
            for copy in save_copies(c, j):
                copy.start()

        @pl.loop(0, width // TILE)
        def _(tile):
            if c == 0:
                gate_tiles.copy(tile).wait()
                up_tiles.copy(tile).wait()
            cols = pl.ds(pl.multiple_of(tile * TILE, TILE), TILE)
            part[c, :, cols] = (
                outer_dot(dgate_buf[slot], vg[cols, :]) + outer_dot(dup_buf[slot], vu[cols, :])
            ).astype(BF)

    scatter = LineScatter(n, me, rows, part, send, recv, rs_send_sem, rs_recv_sem)
    gather = make_gather(n, me, rows, own, da_full, ag_send_sem, ag_recv_sem, local_sem)

    def row_work(c):
        scatter.total(c, total)
        span = chunk_span(c, rows)
        upstream = upstream_in[span].astype(F32) * row_valid[span] + total[...]
        middle_grad[span] = upstream
        value = branch[span]
        grad, gain = norm_back(value, inverse_rms(value), scale[...], upstream)
        own[c] = grad.astype(BF)
        gain_out[...] = gain if c == 0 else gain_out[...] + gain

    run_line(n, CHUNKS, STAGGER, compute, scatter, row_work, gather)
    for c in range(max(CHUNKS - 2, 0), CHUNKS):
        for j in range(n):
            for copy in save_copies(c, j):
                copy.wait()


def mlp_backward(n, dm_full, wg, wu, wd, gate, up, branch, out_grad, row_valid, scale):
    row_count, width = branch.shape
    hidden_width = wg.shape[1]
    rows = row_count // CHUNKS
    saved = jax.ShapeDtypeStruct((n, row_count, hidden_width), BF)
    most = max(width, hidden_width) // TILE
    return pl.pallas_call(
        functools.partial(mlp_backward_kernel, n, rows),
        out_shape=(
            jax.ShapeDtypeStruct((row_count, width), F32),
            jax.ShapeDtypeStruct((n, row_count, width), BF),
            saved,
            saved,
            jax.ShapeDtypeStruct((1, width), F32),
        ),
        in_specs=[HBM] * 6 + [VMEM] * 4,
        out_specs=(VMEM, HBM, HBM, HBM, VMEM),
        scratch_shapes=scatter_scratch(n, rows, width)
        + gather_scratch(n, rows, width)
        + [
            pltpu.VMEM(wg.shape, BF),
            pltpu.VMEM(wu.shape, BF),
            pltpu.VMEM(wd.shape, BF),
            pltpu.SemaphoreType.DMA((3, most)),
            pltpu.VMEM((n * rows, width), BF),
            pltpu.VMEM((n * rows, hidden_width), BF),
            pltpu.VMEM((n * rows, hidden_width), BF),
            pltpu.SemaphoreType.DMA((3, n)),
        ]
        + [pltpu.VMEM((2, n * rows, hidden_width), BF)] * 2
        + [pltpu.SemaphoreType.DMA((2, 2, n))],
        compiler_params=pltpu.CompilerParams(
            collective_id=3, has_side_effects=True, vmem_limit_bytes=60 * MIB
        ),
        name="mlp_backward",
    )(dm_full, wg, wu, wd, gate, up, branch, out_grad, row_valid, scale)


def input_grad_kernel(
    n, rows, grads, weight, base, out,
    part, send, recv, rs_send_sem, rs_recv_sem, total, packed,
):
    me = lax.axis_index("mp")
    neighbour_barrier(me, n)
    width = weight.shape[0]
    block_rows = rows * CHUNKS

    def compute(c):
        for j in range(n):
            packed[j * rows : (j + 1) * rows] = grads[
                j * block_rows + c * rows : j * block_rows + (c + 1) * rows
            ]

        @pl.loop(0, width // TILE)
        def _(tile):
            cols = pl.ds(pl.multiple_of(tile * TILE, TILE), TILE)
            part[c, :, cols] = outer_dot(packed[...], weight[cols, :]).astype(BF)

    scatter = LineScatter(n, me, rows, part, send, recv, rs_send_sem, rs_recv_sem)

    def row_work(c):
        scatter.total(c, total)
        span = chunk_span(c, rows)
        out[span] = base[span] + total[...]

    run_line(n, CHUNKS, 1, compute, scatter, row_work, None)


def input_gradient(n, grads, weight, base):
    row_count, width = base.shape
    rows = row_count // CHUNKS
    return pl.pallas_call(
        functools.partial(input_grad_kernel, n, rows),
        out_shape=jax.ShapeDtypeStruct((row_count, width), F32),
        in_specs=[VMEM] * 3,
        out_specs=VMEM,
        scratch_shapes=scatter_scratch(n, rows, width)
        + [pltpu.VMEM((n * rows, grads.shape[1]), BF)],
        compiler_params=pltpu.CompilerParams(
            collective_id=4, has_side_effects=True, vmem_limit_bytes=56 * MIB
        ),
        name="input_gradient",
    )(grads, weight, base)


def turn(values, cos, sin):
    return values * cos + pltpu.roll(values, values.shape[1] // 2, 1) * sin


def turn_back(values, cos, sin):
    return values * cos + pltpu.roll(values * sin, values.shape[1] // 2, 1)


def allowed_keys(starts, first_row, rows, key_end):
    places = first_row + lax.broadcasted_iota(jnp.int32, (rows, key_end), 0)
    keys = lax.broadcasted_iota(jnp.int32, (rows, key_end), 1)
    return (keys <= places) & (keys >= starts)


def attention_kernel(
    q_raw, k_raw, v_raw, q_inv, k_inv, q_gain, k_gain, cos, sin, starts,
    out, q_low, k_low, v_low, log_total,
):
    size, head = q_raw.shape
    score_scale = 1.0 / math.sqrt(head)
    q_low[...] = turn(q_raw[...] * q_inv[...] * q_gain[...], cos[...], sin[...]).astype(BF)
    k_low[...] = turn(k_raw[...] * k_inv[...] * k_gain[...], cos[...], sin[...]).astype(BF)
    v_low[...] = v_raw[...].astype(BF)
    rows = min(QUERY_ROWS, size)
    for first in range(0, size, rows):
        end = first + rows
        span = slice(first, end)
        scores = outer_dot(q_low[span], k_low[:end]) * score_scale
        scores = jnp.where(allowed_keys(starts[span], first, rows, end), scores, MASKED)
        row_max = jnp.max(scores, axis=1, keepdims=True)
        exponents = jnp.exp(scores - row_max)
        row_total = jnp.sum(exponents, axis=1, keepdims=True)
        probs = (exponents * (1.0 / row_total)).astype(BF)
        out[span] = plain_dot(probs, v_low[:end]).astype(BF)
        log_total[span] = row_max + jnp.log(row_total)


def head_specs(size, head, heads, count):
    return [pl.BlockSpec((size, head), lambda h, k=k: (0, k * heads + h)) for k in range(count)]


def attention(qkv_raw, q_inv, k_inv, q_gain, k_gain, cos, sin, starts, heads):
    size = qkv_raw.shape[0]
    head = cos.shape[1]
    column = pl.BlockSpec((size, 1), lambda h: (0, 0))
    table = pl.BlockSpec((size, head), lambda h: (0, 0))
    gain = pl.BlockSpec((1, head), lambda h: (0, h))
    by_head = pl.BlockSpec((size, head), lambda h: (0, h))
    low = jax.ShapeDtypeStruct((size, heads * head), BF)
    return pl.pallas_call(
        attention_kernel,
        grid=(heads,),
        out_shape=(low, low, low, low, jax.ShapeDtypeStruct((heads, size, 1), F32)),
        in_specs=head_specs(size, head, heads, 3)
        + [column, column, gain, gain, table, table, column],
        out_specs=(by_head,) * 4 + (pl.BlockSpec((None, size, 1), lambda h: (h, 0, 0)),),
        compiler_params=pltpu.CompilerParams(vmem_limit_bytes=48 * MIB),
        name="attention",
    )(qkv_raw, qkv_raw, qkv_raw, q_inv, k_inv, q_gain, k_gain, cos, sin, starts)


def attention_back_kernel(
    q_raw, k_raw, q_low, k_low, v_low, out_grad, log_total,
    q_inv, k_inv, q_gain, k_gain, cos, sin, starts,
    q_weighted, k_weighted, v_grad, q_dots, k_dots, q_gain_grad, k_gain_grad,
    q_grad, k_sum, v_sum,
):
    size, head = q_raw.shape
    score_scale = 1.0 / math.sqrt(head)
    rows = min(QUERY_ROWS, size)
    for first in reversed(range(0, size, rows)):
        end = first + rows
        span = slice(first, end)
        scores = outer_dot(q_low[span], k_low[:end]) * score_scale
        scores = jnp.where(allowed_keys(starts[span], first, rows, end), scores, MASKED)
        probs = jnp.exp(scores - log_total[span])
        prob_grad = outer_dot(out_grad[span], v_low[:end])
        probs_low = probs.astype(BF)
        weighted = probs * prob_grad
        score_grad = (
            weighted - probs * jnp.sum(weighted, axis=1, keepdims=True)
        ).astype(BF)
        q_grad[span] = plain_dot(score_grad, k_low[:end]) * score_scale
        k_extra = inner_dot(score_grad, q_low[span])
        v_extra = inner_dot(probs_low, out_grad[span])
        if end == size:
            k_sum[...] = k_extra
            v_sum[...] = v_extra
        else:
            k_sum[:end] += k_extra
            v_sum[:end] += v_extra
    first_head = pl.program_id(0) == 0
    for raw, inv, gain, grad, factor, weighted_out, dots, gain_grad in (
        (q_raw, q_inv, q_gain, q_grad, None, q_weighted, q_dots, q_gain_grad),
        (k_raw, k_inv, k_gain, k_sum, score_scale, k_weighted, k_dots, k_gain_grad),
    ):
        value = grad[...] if factor is None else grad[...] * factor
        normed = turn_back(value, cos[...], sin[...])
        weighted = normed * gain[...]
        weighted_out[...] = weighted
        gain_grad[...] = jnp.sum(normed * raw[...] * inv[...], axis=0, keepdims=True)
        dot = jnp.sum(weighted * raw[...], axis=1, keepdims=True)

        @pl.when(first_head)
        def _():
            dots[...] = dot

        @pl.when(jnp.logical_not(first_head))
        def _():
            dots[...] += dot

    v_grad[...] = v_sum[...].astype(BF)


def attention_back(
    qkv_raw, q_low, k_low, v_low, out_grad, log_total, q_inv, k_inv, q_gain, k_gain, cos, sin,
    starts, heads,
):
    size = qkv_raw.shape[0]
    head = cos.shape[1]
    column = pl.BlockSpec((size, 1), lambda h: (0, 0))
    table = pl.BlockSpec((size, head), lambda h: (0, 0))
    gain = pl.BlockSpec((1, head), lambda h: (0, h))
    by_head = pl.BlockSpec((size, head), lambda h: (0, h))
    wide = jax.ShapeDtypeStruct((size, heads * head), F32)
    dots = jax.ShapeDtypeStruct((size, 1), F32)
    gains = jax.ShapeDtypeStruct((1, heads * head), F32)
    return pl.pallas_call(
        attention_back_kernel,
        grid=(heads,),
        out_shape=(
            wide, wide, jax.ShapeDtypeStruct((size, heads * head), BF), dots, dots, gains, gains,
        ),
        in_specs=head_specs(size, head, heads, 2)
        + [by_head] * 4
        + [pl.BlockSpec((None, size, 1), lambda h: (h, 0, 0))]
        + [column, column, gain, gain, table, table, column],
        out_specs=(by_head, by_head, by_head, column, column, gain, gain),
        scratch_shapes=[pltpu.VMEM((size, head), F32)] * 3,
        compiler_params=pltpu.CompilerParams(vmem_limit_bytes=48 * MIB),
        name="attention_back",
    )(
        qkv_raw, qkv_raw, q_low, k_low, v_low, out_grad, log_total,
        q_inv, k_inv, q_gain, k_gain, cos, sin, starts,
    )


def local(
    layer_input,
    query_weight,
    key_weight,
    value_weight,
    out_weight,
    gate_weight,
    up_weight,
    down_weight,
    query_gain,
    key_gain,
    attn_gain,
    mlp_gain,
    seq_lens,
    out_grad,
):
    n = lax.axis_size("mp")
    n_dp = lax.axis_size("dp")
    me = lax.axis_index("mp")
    row_count, model_width = layer_input.shape
    group_size = row_count * n
    local_heads, gain_part = query_gain.shape
    head_size = gain_part * n_dp
    local_width = local_heads * head_size

    full_qkv = lax.all_gather(
        jnp.concatenate([query_weight, key_weight, value_weight], axis=1), "dp", axis=0, tiled=True
    )
    full_out = lax.all_gather(out_weight, "dp", axis=1, tiled=True)
    full_gate = lax.all_gather(gate_weight, "dp", axis=0, tiled=True)
    full_up = lax.all_gather(up_weight, "dp", axis=0, tiled=True)
    full_down = lax.all_gather(down_weight, "dp", axis=1, tiled=True)
    head_part = local_heads * gain_part
    gain_parts = lax.all_gather(
        jnp.concatenate(
            [query_gain.reshape(head_part), key_gain.reshape(head_part), attn_gain, mlp_gain]
        ),
        "dp",
        axis=0,
    ).astype(F32)
    width_part = attn_gain.shape[0]

    def head_gain(first):
        piece = gain_parts[:, first : first + head_part].reshape(n_dp, local_heads, gain_part)
        return piece.transpose(1, 0, 2).reshape(1, local_width)

    query_scale = head_gain(0)
    key_scale = head_gain(head_part)
    attn_scale = gain_parts[:, 2 * head_part : 2 * head_part + width_part].reshape(1, model_width)
    mlp_scale = gain_parts[:, 2 * head_part + width_part :].reshape(1, model_width)

    starts, positions, valid = layout(seq_lens[0], group_size)
    starts = starts[:, None]
    cos_table, sin_table = rotary_tables(positions, head_size)
    row_valid = lax.dynamic_slice_in_dim(valid, me * row_count, row_count, 0).astype(F32)[:, None]

    inputs_full = gather_rows(n, layer_input).reshape(group_size, model_width)
    qkv_raw = plain_dot(inputs_full, full_qkv)
    query_raw = qkv_raw[:, :local_width]
    key_raw = qkv_raw[:, local_width : 2 * local_width]
    query_sums, key_sums = lax.psum(
        (jnp.sum(query_raw * query_raw, axis=1), jnp.sum(key_raw * key_raw, axis=1)), "mp"
    )
    query_inv = lax.rsqrt(query_sums / model_width + EPS)[:, None]
    key_inv = lax.rsqrt(key_sums / model_width + EPS)[:, None]
    attended, query_low, key_low, value_low, log_total = attention(
        qkv_raw, query_inv, key_inv, query_scale, key_scale, cos_table, sin_table, starts,
        local_heads,
    )
    branch, middle, middle_full = attn_out(n, attended, full_out, layer_input, attn_scale)
    layer_output, mlp_grad_full, gate, up, hidden, mlp_gain_part = mlp_forward(
        n, middle_full, full_gate, full_up, full_down, middle, out_grad, row_valid, mlp_scale
    )
    middle_grad, branch_full, gate_grad, up_grad, attn_gain_part = mlp_backward(
        n, mlp_grad_full, full_gate, full_up, full_down, gate, up, branch, out_grad, row_valid,
        attn_scale,
    )

    def flat(rows):
        return rows.reshape(group_size, rows.shape[-1])

    def dp_scatter(part, dimension):
        return lax.psum_scatter(
            part.astype(BF), "dp", scatter_dimension=dimension, tiled=True
        ).astype(F32)

    grad_down = dp_scatter(inner_dot(flat(hidden), flat(mlp_grad_full)), 1)
    grad_gate = dp_scatter(inner_dot(flat(middle_full), flat(gate_grad)), 0)
    grad_up = dp_scatter(inner_dot(flat(middle_full), flat(up_grad)), 0)
    grad_out = dp_scatter(inner_dot(attended, flat(branch_full)), 1)

    mixed_grad = outer_dot(flat(branch_full), full_out).astype(BF)
    query_weighted, key_weighted, value_grad, query_dots, key_dots, query_gain_part, key_gain_part = (
        attention_back(
            qkv_raw, query_low, key_low, value_low, mixed_grad, log_total, query_inv, key_inv,
            query_scale, key_scale, cos_table, sin_table, starts, local_heads,
        )
    )
    query_dots, key_dots, attn_gain_sum, mlp_gain_sum = lax.psum(
        (query_dots[:, 0], key_dots[:, 0], attn_gain_part[0], mlp_gain_part[0]), "mp"
    )
    query_raw_grad = (
        query_inv * query_weighted - query_raw * query_inv**3 * (query_dots / model_width)[:, None]
    ).astype(BF)
    key_raw_grad = (
        key_inv * key_weighted - key_raw * key_inv**3 * (key_dots / model_width)[:, None]
    ).astype(BF)
    qkv_grad = jnp.concatenate([query_raw_grad, key_raw_grad, value_grad], axis=1)
    grad_qkv = dp_scatter(inner_dot(inputs_full, qkv_grad), 0)
    input_grad = input_gradient(n, qkv_grad, full_qkv, middle_grad)

    gain_sums = lax.psum(
        jnp.concatenate([attn_gain_sum, mlp_gain_sum, query_gain_part[0], key_gain_part[0]]), "dp"
    )
    at = lax.axis_index("dp")
    grad_attn_gain = lax.dynamic_slice_in_dim(gain_sums, at * width_part, width_part)
    grad_mlp_gain = lax.dynamic_slice_in_dim(gain_sums, model_width + at * width_part, width_part)

    def head_gain_grad(first):
        whole = gain_sums[first : first + local_width].reshape(local_heads, head_size)
        return lax.dynamic_slice_in_dim(whole, at * gain_part, gain_part, 1)

    return (
        layer_output,
        input_grad,
        grad_qkv[:, :local_width],
        grad_qkv[:, local_width : 2 * local_width],
        grad_qkv[:, 2 * local_width :],
        grad_out,
        grad_gate,
        grad_up,
        grad_down,
        head_gain_grad(2 * model_width),
        head_gain_grad(2 * model_width + local_width),
        grad_attn_gain,
        grad_mlp_gain,
    )


def solution(mesh):
    return jax.shard_map(
        local,
        mesh=mesh,
        in_specs=(
            P(("dp", "mp"), None),
            P("dp", "mp"),
            P("dp", "mp"),
            P("dp", "mp"),
            P("mp", "dp"),
            P("dp", "mp"),
            P("dp", "mp"),
            P("mp", "dp"),
            P("mp", "dp"),
            P("mp", "dp"),
            P("dp"),
            P("dp"),
            P("dp", None),
            P(("dp", "mp"), None),
        ),
        out_specs=(
            P(("dp", "mp"), None),
            P(("dp", "mp"), None),
            P("dp", "mp"),
            P("dp", "mp"),
            P("dp", "mp"),
            P("mp", "dp"),
            P("dp", "mp"),
            P("dp", "mp"),
            P("mp", "dp"),
            P("mp", "dp"),
            P("mp", "dp"),
            P("dp"),
            P("dp"),
        ),
        check_vma=False,
    )
```

time: 1640 us -> 905 us (0.55)
  waiting for transfers between devices: 1200 us -> 137 us
  Pallas kernels: 0 us -> 564 us
  matrix products: 219 us -> 74.3 us
  other arithmetic: 77.6 us -> 25 us
  blocking collectives: 78 us -> 58.5 us
  local copies, waits for them, and re-layouts: 39.8 us -> 20.8 us
    pallas_call x0 -> x7, Pallas kernels: none -> 564 us  [the longest x1 136 us: mlp_backward(): pl.pallas_call(functools.partial(mlp_backward_kernel, n, rows), out_shape...]
    reduce_scatter x11 -> x5, waiting for transfers between devices: 693 us -> 134 us  [dp_scatter(): lax.psum_scatter(part.astype(BF), 'dp', scatter_dimension=dimension, tile...]
    all_gather x11 -> x5, waiting for transfers between devices: 449 us -> 0.08 us  [the longest x1 0.02 us: local(): lax.all_gather(jnp.concatenate([query_weight, key_weight, value_weight],...]
    dot_general x19 -> x1, matrix products: 94.7 us -> 10 us  [plain_dot(): return jnp.dot(former, latter, preferred_element_type=F32)]
    dot_general x7 -> x1, matrix products: 64.6 us -> 6.62 us  [outer_dot(): lax.dot_general(former, latter, (((1,), (1,)), ((), ())), preferred_eleme...]
    unnamed x26 -> x10, waiting for transfers between devices: 56.6 us -> 2.53 us
    all_gather x4 -> x1, blocking collectives: 36.9 us -> 9.01 us  [local(): lax.all_gather(jnp.concatenate([query_gain.reshape(head_part), key_gain.r...]
    psum x1 -> x2, blocking collectives: 15.9 us -> 38.6 us  [the longest x1 22.8 us: local(): lax.psum(jnp.concatenate([attn_gain_sum, mlp_gain_sum, query_gain_part[0]...]
  transfers between devices with their start and end apart: 24 -> 10, of which waited for: 22 -> 2; matrix products, arithmetic and copies ran while one was open for 15% -> 11% of each run, Pallas kernels for 0% -> 33%
where the time goes in v1:
time: 905 us; the launch traced here: 896 us
  Pallas kernels  564 us (62%)
  waiting for transfers between devices  137 us (15%)
  matrix products  74.3 us (8%)
  blocking collectives  58.5 us (6%)
  other arithmetic  25 us (3%)
  local copies, waits for them, and re-layouts  20.8 us (2%)
  between operations  15 us (2%)
    pallas_call x1, Pallas kernels, mlp_backward(): pl.pallas_call(functools.partial(mlp_backward_kernel, n, rows), out_shape...  136 us
    reduce_scatter x5, waiting for transfers between devices, dp_scatter(): lax.psum_scatter(part.astype(BF), 'dp', scatter_dimension=dimension, tile...  134 us
    pallas_call x1, Pallas kernels, mlp_forward(): pl.pallas_call(functools.partial(mlp_forward_kernel, n, rows), out_shape=...  134 us
    pallas_call x1, Pallas kernels, attn_out(): pl.pallas_call(functools.partial(attn_out_kernel, n, rows), out_shape=(ja...  117 us
    pallas_call x1, Pallas kernels, gather_rows(): pl.pallas_call(functools.partial(gather_rows_kernel, n, rows), out_shape=...  73.2 us
    pallas_call x1, Pallas kernels, input_gradient(): pl.pallas_call(functools.partial(input_grad_kernel, n, rows), out_shape=j...  67.9 us
    dot_general x5, matrix products, inner_dot(): lax.dot_general(former, latter, (((0,), (0,)), ((), ())), preferred_eleme...  57.6 us
    psum x1, blocking collectives, local(): lax.psum(jnp.concatenate([attn_gain_sum, mlp_gain_sum, query_gain_part[0]...  22.8 us
  transfers between devices with their start and end apart: 10, of which 2 were waited for; matrix products, arithmetic and copies ran while one was open for 11% of the time, Pallas kernels for 33%

profile of v1, /device:TPU:0, one launch (start us, length us, event | category | flops | bytes accessed | tf_op | source)
XLA Modules:
  0.0 895.8 jit_solution(7425701162110649470)
XLA Ops:
  12.8 73.2 %gather_rows.1 = bf16[4,256,2048]{2,1,0:T(8,128)(2,1)} custom-call(bf16[256,2048]{1,0:T(8,128)(2,1)} %x.1), custom_call_target="tpu_custom_call" | custom-call | tf_op jit(solution)/shard_map/gather_rows/pallas_call | solution.py:302
  87.4 9.0 %all-gather.1 = bf16[8,1,640]{2,1,0:T(2,128)(2,1)S(1)} all-gather(bf16[1,1,640]{2,1,0:T(2,128)(2,1)S(1)} %reshape.156), channel_id=2, replica_groups=mesh['dp'=8,'mp'=4] {'dp'}, dimensions={0}, use_global_device_ids=true | all-gather | bytes 11520 | tf_op jit(solution)/shard_map/all_gather | solution.py:891
  101.9 10.0 %convolution_bitcast_fusion.q_raw.k_raw.v_raw = f32[1024,1536]{1,0:T(8,128)S(1)} fusion(bf16[1024,2048]{1,0:T(8,128)(2,1)} %bitcast.61, bf16[2048,1536]{1,0:T(8,128)(2,1)} %all-gather.8.cloned.1.call-done.weight), kind=kOutput, calls=%fused_computation.5 | convolution fusion | flops 6442450944 | bytes 16777216 | tf_op jit(solution)/shard_map/dot_general | solution.py:26
  115.0 11.0 %all-reduce.1 = (f32[1024]{0:T(1024)S(1)}, f32[1024]{0:T(1024)S(1)}) all-reduce(f32[1024]{0:T(1024)S(1)} %get-tuple-element.118, f32[1024]{0:T(1024)S(1)} %get-tuple-element.117), channel_id=1, replica_groups=mesh['dp'=8,'mp'=4] {'mp'}, use_global_device_ids=true, to_apply=%region_1.2 | all-reduce | flops 2048 | bytes 16384 | tf_op jit(solution)/shard_map/psum | solution.py:918
  126.5 17.6 %attention.1 = (bf16[1024,512]{1,0:T(8,128)(2,1)S(1)}, bf16[1024,512]{1,0:T(8,128)(2,1)S(1)}, bf16[1024,512]{1,0:T(8,128)(2,1)S(1)}, bf16[1024,512]{1,0:T(8,128)(2,1)}, f32[4,1024,1]{2,1,0:T(8,128)}) custom-call(f32[1024,1536]{1,0:T(8,128)} %copy-done.7, f32[1024,1536]{1,0:T(8,128)} %copy-done.7, f32[1024,1536]{1,0:T(8,128)} %copy-done.7, ...), custom_call_target="tpu_custom_call" | custom-call | tf_op jit(solution)/shard_map/attention/pallas_call | solution.py:760
  147.1 116.8 %attn_out.1 = (f32[256,2048]{1,0:T(8,128)}, f32[256,2048]{1,0:T(8,128)}, bf16[4,256,2048]{2,1,0:T(8,128)(2,1)}) custom-call(bf16[1024,512]{1,0:T(8,128)(2,1)} %copy-done.5, bf16[512,2048]{1,0:T(8,128)(2,1)} %all-gather.10.cloned.1.call-done.wo, bf16[256,2048]{1,0:T(8,128)(2,1)} %x.1, f32[1,2048]{1,0:T(1,128)} %bitcast.65), custom_call_target="tpu_custom_call" | custom-call | tf_op jit(solution)/shard_map/attn_out/pallas_call | solution.py:352
  263.9 134.1 %mlp_forward.1 = (bf16[256,2048]{1,0:T(8,128)(2,1)}, bf16[4,256,2048]{2,1,0:T(8,128)(2,1)}, bf16[4,256,2048]{2,1,0:T(8,128)(2,1)}, bf16[4,256,2048]{2,1,0:T(8,12...) custom-call(bf16[4,256,2048]{2,1,0:T(8,128)(2,1)} %get-tuple-element.40.h_full, ...), custom_call_target="tpu_custom_call" | custom-call | tf_op jit(solution)/shard_map/mlp_forward/pallas_call | solution.py:491
  398.1 136.4 %mlp_backward.1 = (f32[256,2048]{1,0:T(8,128)}, bf16[4,256,2048]{2,1,0:T(8,128)(2,1)}, bf16[4,256,2048]{2,1,0:T(8,128)(2,1)}, bf16[4,256,2048]{2,1,0:T(8,128)(2,1)}, f32[1,2048]{1,0:T(1,128)}) custom-call(bf16[4,256,2048]{2,1,0:T(8,128)(2,1)} %get-tuple-element.46.dm_full, bf16[2048,2048]{1,0:T(8,128)(2,1)} %all-gather.12.cloned.1.call-done.wg, ...), custom_call_target="tpu_custom_call" | custom-call | tf_op jit(solution)/shard_map/mlp_backward/pallas_call | solution.py:632
  534.4 6.2 convolution_convert_fusion.1
  540.9 6.6 convolution_convert_fusion.2.out_grad
  547.5 18.2 %attention_back.1 = (f32[1024,512]{1,0:T(8,128)}, f32[1024,512]{1,0:T(8,128)}, bf16[1024,512]{1,0:T(8,128)(2,1)S(1)}, f32[1024,1]{1,0:T(8,128)S(1)}, f32[1024,1]...) custom-call(f32[1024,1536]{1,0:T(8,128)} %copy-done.7, f32[1024,1536]{1,0:T(8,128)} %copy-done.7, ...), custom_call_target="tpu_custom_call" | custom-call | tf_op jit(solution)/shard_map/attention_back/pallas_call | solution.py:838
  569.0 15.8 %all-reduce = (f32[1024]{0:T(1024)S(1)}, f32[1024]{0:T(1024)S(1)}, f32[2048]{0:T(1024)S(1)}, f32[2048]{0:T(1024)S(1)}) all-reduce(f32[1024]{0:T(1024)S(1)} %reduce.1, f32[1024]{0:T(1024)S(1)} %reduce, f32[2048]{0:T(1024)S(1)} %bitcast.73, f32[2048]{0:T(1024)S(1)} %bitcast.74), channel_id=1, replica_groups=mesh['dp'=8,'mp'=4] {'mp'}, use_global_device_ids=true, to_apply=%region_8.9 | all-reduce | flops 6144 | bytes 49152 | tf_op jit(solution)/shard_map/psum | solution.py:956
  584.8 4.2 subtract_convert_fusion.1
  590.0 9.1 %fusion = bf16[2048,1536]{0,1:T(8,128)(2,1)} fusion(bf16[1024,2048]{1,0:T(8,128)(2,1)S(1)} %bitcast.62, bf16[1024,512]{1,0:T(8,128)(2,1)S(1)} %copy-done.4, bf16[1024,512]{1,0:T(8,128)(2,1)S(1)} %get-tuple-element.128, bf16[1024,512]{1,0:T(8,128)(2,1)S(1)} %get-tuple-element.127), kind=kOutput, calls=%fused_computation.4 | convolution fusion | flops 6455033856 | bytes 13631488 | tf_op jit(solution)/shard_map/dot_general | solution.py:30
  599.4 14.1 %bitcast_convert_fusion = bf16[2048,2048]{1,0:T(8,128)(2,1)} fusion(bf16[4,256,2048]{2,1,0:T(8,128)(2,1)} %get-tuple-element.60, bf16[4,256,2048]{2,1,0:T(8,128)(2,1)} %get-tuple-element.46.dm_full), kind=kOutput, calls=%fused_computation | convolution fusion | flops 8594128896 | bytes 16777216 | tf_op jit(solution)/shard_map/dot_general | solution.py:30
  613.6 14.0 %bitcast_convert_fusion.1 = bf16[2048,2048]{1,0:T(8,128)(2,1)} fusion(bf16[4,256,2048]{2,1,0:T(8,128)(2,1)} %get-tuple-element.40.h_full, bf16[4,256,2048]{2,1,0:T(8,128)(2,1)} %get-tuple-element.59), kind=kOutput, calls=%fused_computation.1 | convolution fusion | flops 8594128896 | bytes 16777216 | tf_op jit(solution)/shard_map/dot_general | solution.py:30
  627.9 14.2 %bitcast_convert_fusion.2 = bf16[2048,2048]{1,0:T(8,128)(2,1)} fusion(bf16[4,256,2048]{2,1,0:T(8,128)(2,1)} %get-tuple-element.40.h_full, bf16[4,256,2048]{2,1,0:T(8,128)(2,1)} %get-tuple-element.58), kind=kOutput, calls=%fused_computation.2 | convolution fusion | flops 8594128896 | bytes 16777216 | tf_op jit(solution)/shard_map/dot_general | solution.py:30
  644.9 67.9 %input_gradient.1 = f32[256,2048]{1,0:T(8,128)} custom-call(bf16[1024,1536]{1,0:T(8,128)(2,1)} %pad_maximum_fusion.grads, bf16[2048,1536]{1,0:T(8,128)(2,1)} %all-gather.8.cloned.1.call-done.weight, f32[256,2048]{1,0:T(8,128)} %get-tuple-element.57.base), custom_call_target="tpu_custom_call" | custom-call | tf_op jit(solution)/shard_map/input_gradient/pallas_call | solution.py:697
  712.9 22.8 %psum.55 = f32[5120]{0:T(1024)S(1)} all-reduce(f32[5120]{0:T(1024)S(1)} %pad_maximum_fusion.4), channel_id=1, replica_groups=mesh['dp'=8,'mp'=4] {'dp'}, use_global_device_ids=true, to_apply=%region_16.17 | all-reduce | flops 5120 | bytes 40960 | tf_op jit(solution)/shard_map/psum | solution.py:969
  743.6 2.8 convert_element_type.74
  746.4 62.3 %reduce-scatter.12.cloned.1.call-done = bf16[256,2048]{1,0:T(8,128)(2,1)} async-done(((bf16[2048,2048]{1,0:T(8,128)(2,1)}), bf16[256,2048]{1,0:T(8,128)(2,1)}) %reduce-scatter.12.cloned.1.call-update) | async-done | bytes 1048592 | tf_op jit(solution)/shard_map/reduce_scatter | solution.py:940
  808.8 2.8 convert_element_type.72
  811.6 71.8 %reduce-scatter.10.cloned.1.call-done = bf16[256,2048]{1,0:T(8,128)(2,1)} async-done(((bf16[2048,2048]{1,0:T(8,128)(2,1)}), bf16[256,2048]{1,0:T(8,128)(2,1)}) %reduce-scatter.10.cloned.1.call-update) | async-done | bytes 1048592 | tf_op jit(solution)/shard_map/reduce_scatter | solution.py:940
  883.4 2.8 convert_element_type.70
  (116 shorter events, 36.9 us)
Async XLA Ops:
  7.2 4.9 copy-start.18
  7.2 94.7 %all-gather.8.cloned.1.call-start = ((), (), s32[]{:S(2)}) async-start(), calls=%async_computation.5 | async-start | bytes 7077888 | tf_op jit(solution)/shard_map/all_gather | solution.py:883
  9.3 137.8 %all-gather.10.cloned.1.call-start = ((), (), s32[]{:S(2)}) async-start(), calls=%async_computation.6 | async-start | bytes 2359296 | tf_op jit(solution)/shard_map/all_gather | solution.py:886
  10.1 253.8 %all-gather.12.cloned.1.call-start = ((), (), s32[]{:S(2)}) async-start(), calls=%async_computation.7 | async-start | bytes 9437184 | tf_op jit(solution)/shard_map/all_gather | solution.py:887
  10.8 76.4 %copy-start.16 = (bf16[4,16]{1,0:T(4,128)(2,1)S(1)}, bf16[4,16]{1,0:T(4,128)(2,1)}, u32[]{:S(2)}) copy-start(bf16[4,16]{1,0:T(4,128)(2,1)} %param.22) | copy-start | bytes 388
  10.8 76.4 %copy-start.17 = (bf16[4,16]{1,0:T(4,128)(2,1)S(1)}, bf16[4,16]{1,0:T(4,128)(2,1)}, u32[]{:S(2)}) copy-start(bf16[4,16]{1,0:T(4,128)(2,1)} %param.23) | copy-start | bytes 388
  10.8 76.5 %copy-start.14 = (bf16[256]{0:T(256)(128)(2,1)S(1)}, bf16[256]{0:T(256)(128)(2,1)}, u32[]{:S(2)}) copy-start(bf16[256]{0:T(256)(128)(2,1)} %param.25) | copy-start | bytes 1540
  10.8 76.5 %copy-start.15 = (bf16[256]{0:T(256)(128)(2,1)S(1)}, bf16[256]{0:T(256)(128)(2,1)}, u32[]{:S(2)}) copy-start(bf16[256]{0:T(256)(128)(2,1)} %param.24) | copy-start | bytes 1540
  10.8 253.1 %all-gather.14.cloned.1.call-start = ((), (), s32[]{:S(2)}) async-start(), calls=%async_computation.8 | async-start | bytes 9437184 | tf_op jit(solution)/shard_map/all_gather | solution.py:888
  11.4 252.5 %all-gather.16.cloned.1.call-start = ((), (), s32[]{:S(2)}) async-start(), calls=%async_computation.9 | async-start | bytes 9437184 | tf_op jit(solution)/shard_map/all_gather | solution.py:889
  12.0 725.6 %reduce-scatter.8.cloned.1.call-start = ((), (), s32[]{:S(2)}) async-start(), calls=%async_computation.11 | async-start | bytes 2359296 | tf_op jit(solution)/shard_map/reduce_scatter | solution.py:940
  111.9 2.7 copy-start.7
  145.1 1.0 copy-start.2
  540.7 198.7 %reduce-scatter.6.cloned.1.call-start = ((), (), s32[]{:S(2)}) async-start(), calls=%async_computation.10 | async-start | bytes 7077888 | tf_op jit(solution)/shard_map/reduce_scatter | solution.py:940
  540.9 6.6 copy-start.1
  547.5 21.5 %copy-start.12 = (f32[1,2048]{1,0:T(1,128)S(1)}, f32[1,2048]{1,0:T(1,128)}, u32[]{:S(2)}) copy-start(f32[1,2048]{1,0:T(1,128)} %get-tuple-element.62) | copy-start | bytes 24580
  547.5 21.5 %copy-start.13 = (f32[1,2048]{1,0:T(1,128)S(1)}, f32[1,2048]{1,0:T(1,128)}, u32[]{:S(2)}) copy-start(f32[1,2048]{1,0:T(1,128)} %get-tuple-element.61) | copy-start | bytes 24580
  584.8 5.2 copy-start.4
  584.8 5.2 copy-start.9
  599.1 144.5 %reduce-scatter.14.cloned.1.call-start = ((), (), s32[]{:S(2)}) async-start(), calls=%async_computation.14 | async-start | bytes 9437184 | tf_op jit(solution)/shard_map/reduce_scatter | solution.py:940
  613.5 195.3 %reduce-scatter.12.cloned.1.call-start = ((), (), s32[]{:S(2)}) async-start(), calls=%async_computation.13 | async-start | bytes 9437184 | tf_op jit(solution)/shard_map/reduce_scatter | solution.py:940
  627.6 255.8 %reduce-scatter.10.cloned.1.call-start = ((), (), s32[]{:S(2)}) async-start(), calls=%async_computation.12 | async-start | bytes 9437184 | tf_op jit(solution)/shard_map/reduce_scatter | solution.py:940
  743.6 142.5 %copy-start.11 = (bf16[256,2048]{1,0:T(8,128)(2,1)S(1)}, bf16[256,2048]{1,0:T(8,128)(2,1)}, u32[]{:S(2)}) copy-start(bf16[256,2048]{1,0:T(8,128)(2,1)} %get-tuple-element.164) | copy-start | bytes 3145732
  746.4 140.7 %copy-start.8 = (f32[256,2048]{1,0:T(8,128)S(1)}, f32[256,2048]{1,0:T(8,128)}, u32[]{:S(2)}) copy-start(f32[256,2048]{1,0:T(8,128)} %input_gradient.1) | copy-start | bytes 6291460
  (5 other events, 4.7 us)
Sparse Core Ops, SparseCore 0:
  10.5 48.2 all-gather.7
  60.6 28.1 all-gather.9
  90.7 54.4 all-gather.11
  146.9 54.3 all-gather.13
  203.1 55.9 all-gather.15
  540.8 37.0 reduce-scatter.7
  599.3 59.3 reduce-scatter.5
  662.1 71.5 reduce-scatter.13
  737.5 71.2 reduce-scatter.11
  812.1 71.2 reduce-scatter.9

commit v2 on v1

--- a/solution.py
+++ b/solution.py
@@ -20,6 +20,12 @@
 MIB = 1 << 20
 HBM = pl.BlockSpec(memory_space=pl.ANY)
 VMEM = pl.BlockSpec(memory_space=pltpu.VMEM)
+
+
+def cost(micros):
+    return pl.CostEstimate(
+        flops=micros * 1_000_000_000, bytes_accessed=micros * 3_000_000, transcendentals=0
+    )
 
 
 def plain_dot(former, latter):
@@ -275,9 +281,36 @@
     )
 
 
-def gather_rows_kernel(n, rows, block, full, send_sem, recv_sem, local_sem):
-    me = lax.axis_index("mp")
-    neighbour_barrier(me, n)
+def peer_barrier(axes):
+    barrier = pltpu.get_barrier_semaphore()
+    count = 0
+    for name, index, size in axes:
+        for shift in range(1, size):
+            pl.semaphore_signal(barrier, inc=1, device_id={name: lax.rem(index + shift, size)})
+            count += 1
+    return lambda: pl.semaphore_wait(barrier, count)
+
+
+def exchange(name, index, size, src, recv, send_sem, recv_sem):
+    def copy(shift):
+        peer = lax.rem(index + shift, size)
+        return pltpu.make_async_remote_copy(
+            src_ref=src(peer),
+            dst_ref=recv.at[shift - 1],
+            send_sem=send_sem.at[shift - 1],
+            recv_sem=recv_sem.at[shift - 1],
+            device_id={name: peer},
+        )
+
+    return [copy(shift) for shift in range(1, size)]
+
+
+def gather_rows_kernel(
+    n, n_dp, rows, block, gains, full, gain_parts,
+    send_sem, recv_sem, local_sem, gain_recv, gain_send_sem, gain_recv_sem,
+):
+    me, at = lax.axis_index("mp"), lax.axis_index("dp")
+    peer_barrier((("mp", me, n), ("dp", at, n_dp)))()
     gather = LineGather(
         n,
         me,
@@ -287,27 +320,49 @@
         recv_sem,
         local_sem,
     )
-    for step in range(1, n):
+    for c in range(CHUNKS):
+        gather.step(c, 1)
+    copies = exchange(
+        "dp", at, n_dp, lambda peer: gains, gain_recv, gain_send_sem, gain_recv_sem
+    )
+    for copy in copies:
+        copy.start()
+    for step in range(2, n):
         for c in range(CHUNKS):
             gather.step(c, step)
+    gain_parts[at] = gains[...]
+    for shift, copy in enumerate(copies, 1):
+        copy.wait_recv()
+        gain_parts[lax.rem(at + n_dp - shift, n_dp)] = gain_recv[shift - 1]
     for c in range(CHUNKS):
         gather.last(c)
     for c in range(CHUNKS):
         gather.drain(c)
-
-
-def gather_rows(n, block):
+    for copy in copies:
+        copy.wait_send()
+
+
+def gather_rows(n, n_dp, block, gains):
     rows = block.shape[0] // CHUNKS
     sems = gather_scratch(n, rows, block.shape[1])[1:]
     return pl.pallas_call(
-        functools.partial(gather_rows_kernel, n, rows),
-        out_shape=jax.ShapeDtypeStruct((n,) + block.shape, block.dtype),
-        in_specs=[HBM],
-        out_specs=HBM,
-        scratch_shapes=sems,
+        functools.partial(gather_rows_kernel, n, n_dp, rows),
+        out_shape=(
+            jax.ShapeDtypeStruct((n,) + block.shape, block.dtype),
+            jax.ShapeDtypeStruct((n_dp,) + gains.shape, F32),
+        ),
+        in_specs=[HBM, VMEM],
+        out_specs=(HBM, VMEM),
+        scratch_shapes=sems
+        + [
+            pltpu.VMEM((n_dp - 1,) + gains.shape, F32),
+            pltpu.SemaphoreType.DMA((n_dp - 1,)),
+            pltpu.SemaphoreType.DMA((n_dp - 1,)),
+        ],
         compiler_params=pltpu.CompilerParams(collective_id=0, has_side_effects=True),
         name="gather_rows",
-    )(block)
+        cost_estimate=cost(75),
+    )(block, gains)
 
 
 def attn_out_kernel(
@@ -365,6 +420,7 @@
             collective_id=1, has_side_effects=True, vmem_limit_bytes=56 * MIB
         ),
         name="attn_out",
+        cost_estimate=cost(115),
     )(attended, full_out, layer_input, scale)
 
 
@@ -516,6 +572,7 @@
             collective_id=2, has_side_effects=True, vmem_limit_bytes=60 * MIB
         ),
         name="mlp_forward",
+        cost_estimate=cost(135),
     )(h_full, wg, wu, wd, middle, out_grad, row_valid, scale)
 
 
@@ -658,17 +715,41 @@
             collective_id=3, has_side_effects=True, vmem_limit_bytes=60 * MIB
         ),
         name="mlp_backward",
+        cost_estimate=cost(137),
     )(dm_full, wg, wu, wd, gate, up, branch, out_grad, row_valid, scale)
 
 
-def input_grad_kernel(
-    n, rows, grads, weight, base, out,
+def last_grads_kernel(
+    n, n_dp, rows, grads, weight, base, inputs, att, da, gains,
+    input_grad, qkv_out, out_out, gain_out,
     part, send, recv, rs_send_sem, rs_recv_sem, total, packed,
+    x_buf, da_buf, load_sem,
+    core_send_qkv, core_send_out, core_recv_qkv, core_recv_out, core_send_sem, core_recv_sem,
+    chip_send_qkv, chip_send_out, chip_recv_qkv, chip_recv_out, chip_send_sem, chip_recv_sem,
+    gain_recv, gain_send_sem, gain_recv_sem, mp_recv, mp_send_sem, mp_recv_sem, own_qkv, own_out,
 ):
-    me = lax.axis_index("mp")
-    neighbour_barrier(me, n)
+    me, at = lax.axis_index("mp"), lax.axis_index("dp")
+    entered = peer_barrier((("mp", me, n), ("dp", at, n_dp)))
     width = weight.shape[0]
     block_rows = rows * CHUNKS
+    local_width = att.shape[1]
+    chips = n_dp // 2
+    chip, core = at // 2, lax.rem(at, 2)
+    part_width = width // n_dp
+
+    def place(k):
+        target = lax.rem(chip + 1 + k % chips, chips)
+        return 2 * target + (1 - core if k < chips else core)
+
+    def loads(k):
+        cols = pl.ds(pl.multiple_of(place(k) * part_width, part_width), part_width)
+        return [
+            pltpu.make_async_copy(inputs.at[:, cols], x_buf.at[k % 2], load_sem.at[k % 2, 0]),
+            pltpu.make_async_copy(da.at[:, cols], da_buf.at[k % 2], load_sem.at[k % 2, 1]),
+        ]
+
+    for copy in loads(0):
+        copy.start()
 
     def compute(c):
         for j in range(n):
@@ -686,26 +767,179 @@
     def row_work(c):
         scatter.total(c, total)
         span = chunk_span(c, rows)
-        out[span] = base[span] + total[...]
-
-    run_line(n, CHUNKS, 1, compute, scatter, row_work, None)
-
-
-def input_gradient(n, grads, weight, base):
+        input_grad[span] = base[span] + total[...]
+
+    def core_copies(k):
+        other = 2 * chip + 1 - core
+        return [
+            pltpu.make_async_remote_copy(
+                src_ref=src.at[k],
+                dst_ref=dst.at[k],
+                send_sem=core_send_sem.at[k, which],
+                recv_sem=core_recv_sem.at[k, which],
+                device_id={"dp": other},
+            )
+            for which, (src, dst) in enumerate(
+                ((core_send_qkv, core_recv_qkv), (core_send_out, core_recv_out))
+            )
+        ]
+
+    def chip_copies(k):
+        other = 2 * lax.rem(chip + 1 + k, chips) + core
+        return [
+            pltpu.make_async_remote_copy(
+                src_ref=src.at[k],
+                dst_ref=dst.at[k],
+                send_sem=chip_send_sem.at[k, which],
+                recv_sem=chip_recv_sem.at[k, which],
+                device_id={"dp": other},
+            )
+            for which, (src, dst) in enumerate(
+                ((chip_send_qkv, chip_recv_qkv), (chip_send_out, chip_recv_out))
+            )
+        ]
+
+    def weight_block(k):
+        slot = k % 2
+        for copy in loads(k):
+            copy.wait()
+        if k + 1 < 2 * chips:
+            for copy in loads(k + 1):
+                copy.start()
+        if k >= chips:
+            for copy in core_copies(k - chips):
+                copy.wait_recv()
+
+        @pl.loop(0, 3)
+        def _(tile):
+            cols = pl.ds(pl.multiple_of(tile * local_width, local_width), local_width)
+            block = inner_dot(x_buf[slot], grads[:, cols])
+            if k < chips:
+                core_send_qkv[k, :, cols] = block.astype(BF)
+            else:
+                block = block + core_recv_qkv[k - chips, :, cols].astype(F32)
+                if k < 2 * chips - 1:
+                    chip_send_qkv[k - chips, :, cols] = block.astype(BF)
+                else:
+                    own_qkv[:, cols] = block
+
+        block = inner_dot(att[...], da_buf[slot])
+        if k < chips:
+            core_send_out[k] = block.astype(BF)
+            for copy in core_copies(k):
+                copy.start()
+        else:
+            block = block + core_recv_out[k - chips].astype(F32)
+            if k < 2 * chips - 1:
+                chip_send_out[k - chips] = block.astype(BF)
+                for copy in chip_copies(k - chips):
+                    copy.start()
+            else:
+                own_out[...] = block
+
+    gain_copies = exchange(
+        "dp", at, n_dp, lambda peer: gains.at[peer], gain_recv, gain_send_sem, gain_recv_sem
+    )
+    mp_copies = exchange("mp", me, n, lambda peer: gain_out, mp_recv, mp_send_sem, mp_recv_sem)
+
+    compute(0)
+    entered()
+    scatter.step(0, 0)
+    for copy in gain_copies:
+        copy.start()
+    for c in range(1, CHUNKS):
+        compute(c)
+        scatter.step(c, 0)
+    for k in range(chips):
+        weight_block(k)
+    line = [(step, c) for step in range(1, n) for c in range(CHUNKS)]
+    done = 0
+    for k in range(chips, 2 * chips + 1):
+        if k < 2 * chips:
+            weight_block(k)
+        until = len(line) if k == 2 * chips else (k - chips + 1) * CHUNKS // 2
+        for step, c in line[done:until]:
+            if step < n - 1:
+                scatter.step(c, step)
+            else:
+                row_work(c)
+        done = until
+        if k == chips:
+            gain_out[...] = gains[at]
+            for shift, copy in enumerate(gain_copies, 1):
+                copy.wait_recv()
+                gain_out[...] += gain_recv[shift - 1]
+            for copy in mp_copies:
+                copy.start()
+    for k in range(chips - 1):
+        for copy in chip_copies(k):
+            copy.wait_recv()
+    qkv_out[...] = own_qkv[...]
+    out_out[...] = own_out[...]
+    for k in range(chips - 1):
+        qkv_out[...] += chip_recv_qkv[k].astype(F32)
+        out_out[...] += chip_recv_out[k].astype(F32)
+    for copy in mp_copies:
+        copy.wait_recv()
+        copy.wait_send()
+    lanes = lax.broadcasted_iota(jnp.int32, gain_out.shape, 1)
+    shared = gain_out[...]
+    for shift in range(1, n):
+        shared = shared + mp_recv[shift - 1]
+    gain_out[...] = jnp.where(lanes < 2 * part_width, shared, gain_out[...])
+    for copy in gain_copies:
+        copy.wait_send()
+    for c in range(CHUNKS):
+        scatter.drain(c)
+    for k in range(chips):
+        for copy in core_copies(k):
+            copy.wait_send()
+    for k in range(chips - 1):
+        for copy in chip_copies(k):
+            copy.wait_send()
+
+
+def last_grads(n, n_dp, grads, weight, base, inputs, attended, da_full, gains):
     row_count, width = base.shape
     rows = row_count // CHUNKS
+    size, local_width = attended.shape
+    part_width = width // n_dp
+    chips = n_dp // 2
+    qkv_block = (part_width, 3 * local_width)
+    out_block = (local_width, part_width)
+    gain_block = gains.shape[1:]
     return pl.pallas_call(
-        functools.partial(input_grad_kernel, n, rows),
-        out_shape=jax.ShapeDtypeStruct((row_count, width), F32),
-        in_specs=[VMEM] * 3,
-        out_specs=VMEM,
+        functools.partial(last_grads_kernel, n, n_dp, rows),
+        out_shape=(
+            jax.ShapeDtypeStruct((row_count, width), F32),
+            jax.ShapeDtypeStruct(qkv_block, F32),
+            jax.ShapeDtypeStruct(out_block, F32),
+            jax.ShapeDtypeStruct(gain_block, F32),
+        ),
+        in_specs=[VMEM, VMEM, VMEM, HBM, VMEM, HBM, VMEM],
+        out_specs=(VMEM,) * 4,
         scratch_shapes=scatter_scratch(n, rows, width)
-        + [pltpu.VMEM((n * rows, grads.shape[1]), BF)],
+        + [
+            pltpu.VMEM((n * rows, 3 * local_width), BF),
+            pltpu.VMEM((2, size, part_width), BF),
+            pltpu.VMEM((2, size, part_width), BF),
+            pltpu.SemaphoreType.DMA((2, 2)),
+        ]
+        + [pltpu.VMEM((chips,) + block, BF) for block in (qkv_block, out_block) * 2]
+        + [pltpu.SemaphoreType.DMA((chips, 2))] * 2
+        + [pltpu.VMEM((chips - 1,) + block, BF) for block in (qkv_block, out_block) * 2]
+        + [pltpu.SemaphoreType.DMA((chips - 1, 2))] * 2
+        + [pltpu.VMEM((n_dp - 1,) + gain_block, F32)]
+        + [pltpu.SemaphoreType.DMA((n_dp - 1,))] * 2
+        + [pltpu.VMEM((n - 1,) + gain_block, F32)]
+        + [pltpu.SemaphoreType.DMA((n - 1,))] * 2
+        + [pltpu.VMEM(qkv_block, F32), pltpu.VMEM(out_block, F32)],
         compiler_params=pltpu.CompilerParams(
-            collective_id=4, has_side_effects=True, vmem_limit_bytes=56 * MIB
+            collective_id=4, has_side_effects=True, vmem_limit_bytes=60 * MIB
         ),
-        name="input_gradient",
-    )(grads, weight, base)
+        name="last_grads",
+        cost_estimate=cost(90),
+    )(grads, weight, base, inputs, attended, da_full, gains)
 
 
 def turn(values, cos, sin):
@@ -722,136 +956,194 @@
     return (keys <= places) & (keys >= starts)
 
 
+def columns_to_rows(first, second):
+    lanes = lax.broadcasted_iota(jnp.int32, (first.shape[0], 128), 1)
+    return jnp.transpose(jnp.where(lanes == 0, first, second))[:8]
+
+
+def sum_columns(n, me, first, second, entered, held, recv, turned, send_sem, recv_sem):
+    held[...] = columns_to_rows(first, second)
+    copies = exchange("mp", me, n, lambda peer: held, recv, send_sem, recv_sem)
+    entered()
+    for copy in copies:
+        copy.start()
+    total = held[...]
+    for shift, copy in enumerate(copies, 1):
+        copy.wait_recv()
+        total = total + recv[shift - 1]
+    for copy in copies:
+        copy.wait_send()
+    turned[...] = jnp.zeros_like(turned)
+    turned[:8] = total
+    back = jnp.transpose(turned[...])
+    return back[:, 0:1], back[:, 1:2]
+
+
+def sum_scratch(n, size):
+    return [
+        pltpu.VMEM((8, size), F32),
+        pltpu.VMEM((n - 1, 8, size), F32),
+        pltpu.VMEM((128, size), F32),
+        pltpu.SemaphoreType.DMA((n - 1,)),
+        pltpu.SemaphoreType.DMA((n - 1,)),
+    ]
+
+
 def attention_kernel(
-    q_raw, k_raw, v_raw, q_inv, k_inv, q_gain, k_gain, cos, sin, starts,
-    out, q_low, k_low, v_low, log_total,
+    n, heads, model_width, qkv, q_gain, k_gain, cos, sin, starts,
+    out, q_low, k_low, v_low, log_total, q_inv, k_inv, *sums,
 ):
-    size, head = q_raw.shape
+    me = lax.axis_index("mp")
+    entered = peer_barrier((("mp", me, n),))
+    size = qkv.shape[0]
+    width = qkv.shape[1] // 3
+    head = width // heads
     score_scale = 1.0 / math.sqrt(head)
-    q_low[...] = turn(q_raw[...] * q_inv[...] * q_gain[...], cos[...], sin[...]).astype(BF)
-    k_low[...] = turn(k_raw[...] * k_inv[...] * k_gain[...], cos[...], sin[...]).astype(BF)
-    v_low[...] = v_raw[...].astype(BF)
+
+    def squares(first):
+        return jnp.sum(jnp.square(qkv[:, first : first + width]), axis=1, keepdims=True)
+
+    q_sum, k_sum = sum_columns(n, me, squares(0), squares(width), entered, *sums)
+    q_inv[...] = lax.rsqrt(q_sum / model_width + EPS)
+    k_inv[...] = lax.rsqrt(k_sum / model_width + EPS)
     rows = min(QUERY_ROWS, size)
-    for first in range(0, size, rows):
-        end = first + rows
-        span = slice(first, end)
-        scores = outer_dot(q_low[span], k_low[:end]) * score_scale
-        scores = jnp.where(allowed_keys(starts[span], first, rows, end), scores, MASKED)
-        row_max = jnp.max(scores, axis=1, keepdims=True)
-        exponents = jnp.exp(scores - row_max)
-        row_total = jnp.sum(exponents, axis=1, keepdims=True)
-        probs = (exponents * (1.0 / row_total)).astype(BF)
-        out[span] = plain_dot(probs, v_low[:end]).astype(BF)
-        log_total[span] = row_max + jnp.log(row_total)
-
-
-def head_specs(size, head, heads, count):
-    return [pl.BlockSpec((size, head), lambda h, k=k: (0, k * heads + h)) for k in range(count)]
-
-
-def attention(qkv_raw, q_inv, k_inv, q_gain, k_gain, cos, sin, starts, heads):
+
+    @pl.loop(0, heads)
+    def _(h):
+        def cols(first):
+            return pl.ds(pl.multiple_of(first + h * head, head), head)
+
+        here = cols(0)
+        q_low[:, here] = turn(
+            qkv[:, here] * q_inv[...] * q_gain[:, here], cos[...], sin[...]
+        ).astype(BF)
+        k_low[:, here] = turn(
+            qkv[:, cols(width)] * k_inv[...] * k_gain[:, here], cos[...], sin[...]
+        ).astype(BF)
+        v_low[:, here] = qkv[:, cols(2 * width)].astype(BF)
+        for first in range(0, size, rows):
+            end = first + rows
+            span = slice(first, end)
+            scores = outer_dot(q_low[span, here], k_low[:end, here]) * score_scale
+            scores = jnp.where(allowed_keys(starts[span], first, rows, end), scores, MASKED)
+            row_max = jnp.max(scores, axis=1, keepdims=True)
+            exponents = jnp.exp(scores - row_max)
+            row_total = jnp.sum(exponents, axis=1, keepdims=True)
+            probs = (exponents * (1.0 / row_total)).astype(BF)
+            out[span, here] = plain_dot(probs, v_low[:end, here]).astype(BF)
+            log_total[h, span] = row_max + jnp.log(row_total)
+
+
+def attention(n, heads, model_width, qkv_raw, q_gain, k_gain, cos, sin, starts):
     size = qkv_raw.shape[0]
-    head = cos.shape[1]
-    column = pl.BlockSpec((size, 1), lambda h: (0, 0))
-    table = pl.BlockSpec((size, head), lambda h: (0, 0))
-    gain = pl.BlockSpec((1, head), lambda h: (0, h))
-    by_head = pl.BlockSpec((size, head), lambda h: (0, h))
-    low = jax.ShapeDtypeStruct((size, heads * head), BF)
+    low = jax.ShapeDtypeStruct((size, qkv_raw.shape[1] // 3), BF)
+    column = jax.ShapeDtypeStruct((size, 1), F32)
     return pl.pallas_call(
-        attention_kernel,
-        grid=(heads,),
-        out_shape=(low, low, low, low, jax.ShapeDtypeStruct((heads, size, 1), F32)),
-        in_specs=head_specs(size, head, heads, 3)
-        + [column, column, gain, gain, table, table, column],
-        out_specs=(by_head,) * 4 + (pl.BlockSpec((None, size, 1), lambda h: (h, 0, 0)),),
-        compiler_params=pltpu.CompilerParams(vmem_limit_bytes=48 * MIB),
+        functools.partial(attention_kernel, n, heads, model_width),
+        out_shape=(low,) * 4 + (jax.ShapeDtypeStruct((heads, size, 1), F32), column, column),
+        in_specs=[VMEM] * 6,
+        out_specs=(VMEM,) * 7,
+        scratch_shapes=sum_scratch(n, size),
+        compiler_params=pltpu.CompilerParams(
+            collective_id=5, has_side_effects=True, vmem_limit_bytes=56 * MIB
+        ),
         name="attention",
-    )(qkv_raw, qkv_raw, qkv_raw, q_inv, k_inv, q_gain, k_gain, cos, sin, starts)
+        cost_estimate=cost(25),
+    )(qkv_raw, q_gain, k_gain, cos, sin, starts)
 
 
 def attention_back_kernel(
-    q_raw, k_raw, q_low, k_low, v_low, out_grad, log_total,
+    n, heads, model_width, qkv, q_low, k_low, v_low, out_grad, log_total,
     q_inv, k_inv, q_gain, k_gain, cos, sin, starts,
-    q_weighted, k_weighted, v_grad, q_dots, k_dots, q_gain_grad, k_gain_grad,
-    q_grad, k_sum, v_sum,
+    grads, q_gain_grad, k_gain_grad,
+    q_weighted, k_weighted, q_grad, k_sum, v_sum, q_dots, k_dots, *sums,
 ):
-    size, head = q_raw.shape
+    me = lax.axis_index("mp")
+    entered = peer_barrier((("mp", me, n),))
+    size = qkv.shape[0]
+    width = qkv.shape[1] // 3
+    head = width // heads
     score_scale = 1.0 / math.sqrt(head)
     rows = min(QUERY_ROWS, size)
-    for first in reversed(range(0, size, rows)):
-        end = first + rows
-        span = slice(first, end)
-        scores = outer_dot(q_low[span], k_low[:end]) * score_scale
-        scores = jnp.where(allowed_keys(starts[span], first, rows, end), scores, MASKED)
-        probs = jnp.exp(scores - log_total[span])
-        prob_grad = outer_dot(out_grad[span], v_low[:end])
-        probs_low = probs.astype(BF)
-        weighted = probs * prob_grad
-        score_grad = (
-            weighted - probs * jnp.sum(weighted, axis=1, keepdims=True)
+    q_dots[...] = jnp.zeros_like(q_dots)
+    k_dots[...] = jnp.zeros_like(k_dots)
+
+    @pl.loop(0, heads)
+    def _(h):
+        def cols(first):
+            return pl.ds(pl.multiple_of(first + h * head, head), head)
+
+        here = cols(0)
+        for first in reversed(range(0, size, rows)):
+            end = first + rows
+            span = slice(first, end)
+            scores = outer_dot(q_low[span, here], k_low[:end, here]) * score_scale
+            scores = jnp.where(allowed_keys(starts[span], first, rows, end), scores, MASKED)
+            probs = jnp.exp(scores - log_total[h, span])
+            prob_grad = outer_dot(out_grad[span, here], v_low[:end, here])
+            probs_low = probs.astype(BF)
+            weighted = probs * prob_grad
+            score_grad = (
+                weighted - probs * jnp.sum(weighted, axis=1, keepdims=True)
+            ).astype(BF)
+            q_grad[span] = plain_dot(score_grad, k_low[:end, here]) * score_scale
+            k_extra = inner_dot(score_grad, q_low[span, here])
+            v_extra = inner_dot(probs_low, out_grad[span, here])
+            if end == size:
+                k_sum[...] = k_extra
+                v_sum[...] = v_extra
+            else:
+                k_sum[:end] += k_extra
+                v_sum[:end] += v_extra
+        for first, inv, gain, grad, factor, weighted_out, dots, gain_grad in (
+            (0, q_inv, q_gain, q_grad, None, q_weighted, q_dots, q_gain_grad),
+            (width, k_inv, k_gain, k_sum, score_scale, k_weighted, k_dots, k_gain_grad),
+        ):
+            raw = qkv[:, cols(first)]
+            value = grad[...] if factor is None else grad[...] * factor
+            normed = turn_back(value, cos[...], sin[...])
+            weighted = normed * gain[:, here]
+            weighted_out[:, here] = weighted
+            gain_grad[:, here] = jnp.sum(normed * raw * inv[...], axis=0, keepdims=True)
+            dots[...] += jnp.sum(weighted * raw, axis=1, keepdims=True)
+        grads[:, cols(2 * width)] = v_sum[...].astype(BF)
+
+    q_total, k_total = sum_columns(n, me, q_dots[...], k_dots[...], entered, *sums)
+    for first, inv, weighted, dots in (
+        (0, q_inv, q_weighted, q_total),
+        (width, k_inv, k_weighted, k_total),
+    ):
+        scale = inv[...]
+        factor = scale * scale * scale * (dots / model_width)
+        grads[:, first : first + width] = (
+            scale * weighted[...] - qkv[:, first : first + width] * factor
         ).astype(BF)
-        q_grad[span] = plain_dot(score_grad, k_low[:end]) * score_scale
-        k_extra = inner_dot(score_grad, q_low[span])
-        v_extra = inner_dot(probs_low, out_grad[span])
-        if end == size:
-            k_sum[...] = k_extra
-            v_sum[...] = v_extra
-        else:
-            k_sum[:end] += k_extra
-            v_sum[:end] += v_extra
-    first_head = pl.program_id(0) == 0
-    for raw, inv, gain, grad, factor, weighted_out, dots, gain_grad in (
-        (q_raw, q_inv, q_gain, q_grad, None, q_weighted, q_dots, q_gain_grad),
-        (k_raw, k_inv, k_gain, k_sum, score_scale, k_weighted, k_dots, k_gain_grad),
-    ):
-        value = grad[...] if factor is None else grad[...] * factor
-        normed = turn_back(value, cos[...], sin[...])
-        weighted = normed * gain[...]
-        weighted_out[...] = weighted
-        gain_grad[...] = jnp.sum(normed * raw[...] * inv[...], axis=0, keepdims=True)
-        dot = jnp.sum(weighted * raw[...], axis=1, keepdims=True)
-
-        @pl.when(first_head)
-        def _():
-            dots[...] = dot
-
-        @pl.when(jnp.logical_not(first_head))
-        def _():
-            dots[...] += dot
-
-    v_grad[...] = v_sum[...].astype(BF)
 
 
 def attention_back(
-    qkv_raw, q_low, k_low, v_low, out_grad, log_total, q_inv, k_inv, q_gain, k_gain, cos, sin,
-    starts, heads,
+    n, heads, model_width, qkv_raw, q_low, k_low, v_low, out_grad, log_total, q_inv, k_inv,
+    q_gain, k_gain, cos, sin, starts,
 ):
-    size = qkv_raw.shape[0]
-    head = cos.shape[1]
-    column = pl.BlockSpec((size, 1), lambda h: (0, 0))
-    table = pl.BlockSpec((size, head), lambda h: (0, 0))
-    gain = pl.BlockSpec((1, head), lambda h: (0, h))
-    by_head = pl.BlockSpec((size, head), lambda h: (0, h))
-    wide = jax.ShapeDtypeStruct((size, heads * head), F32)
-    dots = jax.ShapeDtypeStruct((size, 1), F32)
-    gains = jax.ShapeDtypeStruct((1, heads * head), F32)
+    size, width = q_low.shape
+    head = width // heads
+    gains = jax.ShapeDtypeStruct((1, width), F32)
     return pl.pallas_call(
-        attention_back_kernel,
-        grid=(heads,),
-        out_shape=(
-            wide, wide, jax.ShapeDtypeStruct((size, heads * head), BF), dots, dots, gains, gains,
+        functools.partial(attention_back_kernel, n, heads, model_width),
+        out_shape=(jax.ShapeDtypeStruct((size, 3 * width), BF), gains, gains),
+        in_specs=[VMEM] * 13,
+        out_specs=(VMEM,) * 3,
+        scratch_shapes=[pltpu.VMEM((size, width), F32)] * 2
+        + [pltpu.VMEM((size, head), F32)] * 3
+        + [pltpu.VMEM((size, 1), F32)] * 2
+        + sum_scratch(n, size),
+        compiler_params=pltpu.CompilerParams(
+            collective_id=6, has_side_effects=True, vmem_limit_bytes=56 * MIB
         ),
-        in_specs=head_specs(size, head, heads, 2)
-        + [by_head] * 4
-        + [pl.BlockSpec((None, size, 1), lambda h: (h, 0, 0))]
-        + [column, column, gain, gain, table, table, column],
-        out_specs=(by_head, by_head, by_head, column, column, gain, gain),
-        scratch_shapes=[pltpu.VMEM((size, head), F32)] * 3,
-        compiler_params=pltpu.CompilerParams(vmem_limit_bytes=48 * MIB),
         name="attention_back",
+        cost_estimate=cost(30),
     )(
-        qkv_raw, qkv_raw, q_low, k_low, v_low, out_grad, log_total,
-        q_inv, k_inv, q_gain, k_gain, cos, sin, starts,
+        qkv_raw, q_low, k_low, v_low, out_grad, log_total, q_inv, k_inv, q_gain, k_gain,
+        cos, sin, starts,
     )
 
 
@@ -888,95 +1180,87 @@
     full_up = lax.all_gather(up_weight, "dp", axis=0, tiled=True)
     full_down = lax.all_gather(down_weight, "dp", axis=1, tiled=True)
     head_part = local_heads * gain_part
-    gain_parts = lax.all_gather(
-        jnp.concatenate(
-            [query_gain.reshape(head_part), key_gain.reshape(head_part), attn_gain, mlp_gain]
-        ),
-        "dp",
-        axis=0,
-    ).astype(F32)
     width_part = attn_gain.shape[0]
+    own_gains = jnp.concatenate(
+        [attn_gain, mlp_gain, query_gain.reshape(head_part), key_gain.reshape(head_part)]
+    ).astype(F32)[None]
+    inputs_full, gain_parts = gather_rows(n, n_dp, layer_input, own_gains)
+    inputs_full = inputs_full.reshape(group_size, model_width)
+    gain_parts = gain_parts[:, 0]
 
     def head_gain(first):
         piece = gain_parts[:, first : first + head_part].reshape(n_dp, local_heads, gain_part)
         return piece.transpose(1, 0, 2).reshape(1, local_width)
 
-    query_scale = head_gain(0)
-    key_scale = head_gain(head_part)
-    attn_scale = gain_parts[:, 2 * head_part : 2 * head_part + width_part].reshape(1, model_width)
-    mlp_scale = gain_parts[:, 2 * head_part + width_part :].reshape(1, model_width)
+    query_scale = head_gain(2 * width_part)
+    key_scale = head_gain(2 * width_part + head_part)
+    attn_scale = gain_parts[:, :width_part].reshape(1, model_width)
+    mlp_scale = gain_parts[:, width_part : 2 * width_part].reshape(1, model_width)
 
     starts, positions, valid = layout(seq_lens[0], group_size)
     starts = starts[:, None]
     cos_table, sin_table = rotary_tables(positions, head_size)
     row_valid = lax.dynamic_slice_in_dim(valid, me * row_count, row_count, 0).astype(F32)[:, None]
 
-    inputs_full = gather_rows(n, layer_input).reshape(group_size, model_width)
     qkv_raw = plain_dot(inputs_full, full_qkv)
-    query_raw = qkv_raw[:, :local_width]
-    key_raw = qkv_raw[:, local_width : 2 * local_width]
-    query_sums, key_sums = lax.psum(
-        (jnp.sum(query_raw * query_raw, axis=1), jnp.sum(key_raw * key_raw, axis=1)), "mp"
-    )
-    query_inv = lax.rsqrt(query_sums / model_width + EPS)[:, None]
-    key_inv = lax.rsqrt(key_sums / model_width + EPS)[:, None]
-    attended, query_low, key_low, value_low, log_total = attention(
-        qkv_raw, query_inv, key_inv, query_scale, key_scale, cos_table, sin_table, starts,
-        local_heads,
+    attended, query_low, key_low, value_low, log_total, query_inv, key_inv = attention(
+        n, local_heads, model_width, qkv_raw, query_scale, key_scale, cos_table, sin_table, starts
     )
     branch, middle, middle_full = attn_out(n, attended, full_out, layer_input, attn_scale)
     layer_output, mlp_grad_full, gate, up, hidden, mlp_gain_part = mlp_forward(
         n, middle_full, full_gate, full_up, full_down, middle, out_grad, row_valid, mlp_scale
     )
+
+    def flat(rows):
+        return rows.reshape(group_size, rows.shape[-1])
+
+    def dp_scatter(part, dimension):
+        return lax.psum_scatter(part, "dp", scatter_dimension=dimension, tiled=True)
+
+    down_part = inner_dot(flat(hidden), flat(mlp_grad_full)).astype(BF)
+    mlp_grad_full, down_part = lax.optimization_barrier((mlp_grad_full, down_part))
+    grad_down = dp_scatter(down_part, 1)
     middle_grad, branch_full, gate_grad, up_grad, attn_gain_part = mlp_backward(
         n, mlp_grad_full, full_gate, full_up, full_down, gate, up, branch, out_grad, row_valid,
         attn_scale,
     )
-
-    def flat(rows):
-        return rows.reshape(group_size, rows.shape[-1])
-
-    def dp_scatter(part, dimension):
-        return lax.psum_scatter(
-            part.astype(BF), "dp", scatter_dimension=dimension, tiled=True
-        ).astype(F32)
-
-    grad_down = dp_scatter(inner_dot(flat(hidden), flat(mlp_grad_full)), 1)
-    grad_gate = dp_scatter(inner_dot(flat(middle_full), flat(gate_grad)), 0)
-    grad_up = dp_scatter(inner_dot(flat(middle_full), flat(up_grad)), 0)
-    grad_out = dp_scatter(inner_dot(attended, flat(branch_full)), 1)
-
-    mixed_grad = outer_dot(flat(branch_full), full_out).astype(BF)
-    query_weighted, key_weighted, value_grad, query_dots, key_dots, query_gain_part, key_gain_part = (
-        attention_back(
-            qkv_raw, query_low, key_low, value_low, mixed_grad, log_total, query_inv, key_inv,
-            query_scale, key_scale, cos_table, sin_table, starts, local_heads,
-        )
-    )
-    query_dots, key_dots, attn_gain_sum, mlp_gain_sum = lax.psum(
-        (query_dots[:, 0], key_dots[:, 0], attn_gain_part[0], mlp_gain_part[0]), "mp"
-    )
-    query_raw_grad = (
-        query_inv * query_weighted - query_raw * query_inv**3 * (query_dots / model_width)[:, None]
-    ).astype(BF)
-    key_raw_grad = (
-        key_inv * key_weighted - key_raw * key_inv**3 * (key_dots / model_width)[:, None]
-    ).astype(BF)
-    qkv_grad = jnp.concatenate([query_raw_grad, key_raw_grad, value_grad], axis=1)
-    grad_qkv = dp_scatter(inner_dot(inputs_full, qkv_grad), 0)
-    input_grad = input_gradient(n, qkv_grad, full_qkv, middle_grad)
-
-    gain_sums = lax.psum(
-        jnp.concatenate([attn_gain_sum, mlp_gain_sum, query_gain_part[0], key_gain_part[0]]), "dp"
-    )
-    at = lax.axis_index("dp")
-    grad_attn_gain = lax.dynamic_slice_in_dim(gain_sums, at * width_part, width_part)
-    grad_mlp_gain = lax.dynamic_slice_in_dim(gain_sums, model_width + at * width_part, width_part)
-
-    def head_gain_grad(first):
-        whole = gain_sums[first : first + local_width].reshape(local_heads, head_size)
-        return lax.dynamic_slice_in_dim(whole, at * gain_part, gain_part, 1)
-
+    branch_full = flat(branch_full)
+    gate_part = inner_dot(flat(middle_full), flat(gate_grad)).astype(BF)
+    branch_full, gate_part, grad_down = lax.optimization_barrier(
+        (branch_full, gate_part, grad_down)
+    )
+    grad_gate = dp_scatter(gate_part, 0)
+
+    mixed_grad = outer_dot(branch_full, full_out).astype(BF)
+    qkv_grad, query_gain_part, key_gain_part = attention_back(
+        n, local_heads, model_width, qkv_raw, query_low, key_low, value_low, mixed_grad, log_total,
+        query_inv, key_inv, query_scale, key_scale, cos_table, sin_table, starts,
+    )
+    up_part = inner_dot(flat(middle_full), flat(up_grad)).astype(BF)
+    qkv_grad, up_part, grad_gate = lax.optimization_barrier((qkv_grad, up_part, grad_gate))
+    grad_up = dp_scatter(up_part, 0)
+
+    def by_part(row):
+        return row.reshape(n_dp, -1)
+
+    def by_head_part(row):
+        pieces = row.reshape(local_heads, n_dp, gain_part).transpose(1, 0, 2)
+        return pieces.reshape(n_dp, head_part)
+
+    gain_grads = jnp.concatenate(
+        [
+            by_part(attn_gain_part),
+            by_part(mlp_gain_part),
+            by_head_part(query_gain_part),
+            by_head_part(key_gain_part),
+        ],
+        axis=1,
+    )[:, None]
+    input_grad, grad_qkv, grad_out, gain_sums = last_grads(
+        n, n_dp, qkv_grad, full_qkv, middle_grad, inputs_full, attended, branch_full, gain_grads
+    )
+    gain_sums = gain_sums[0]
+    heads_at = 2 * width_part
     return (
         layer_output,
         input_grad,
@@ -984,13 +1268,13 @@
         grad_qkv[:, local_width : 2 * local_width],
         grad_qkv[:, 2 * local_width :],
         grad_out,
-        grad_gate,
-        grad_up,
-        grad_down,
-        head_gain_grad(2 * model_width),
-        head_gain_grad(2 * model_width + local_width),
-        grad_attn_gain,
-        grad_mlp_gain,
+        grad_gate.astype(F32),
+        grad_up.astype(F32),
+        grad_down.astype(F32),
+        gain_sums[heads_at : heads_at + head_part].reshape(local_heads, gain_part),
+        gain_sums[heads_at + head_part :].reshape(local_heads, gain_part),
+        gain_sums[:width_part],
+        gain_sums[width_part:heads_at],
     )
 
 

time: 905 us -> 769 us (0.85)
  waiting for transfers between devices: 137 us -> 33 us
  blocking collectives: 58.5 us -> 0 us
  Pallas kernels: 564 us -> 620 us
  matrix products: 74.3 us -> 60.4 us
    reduce_scatter x5 -> x3, waiting for transfers between devices: 134 us -> 26.8 us  [dp_scatter(): return lax.psum_scatter(part, 'dp', scatter_dimension=dimension, tiled=True)]
    pallas_call x4, Pallas kernels: 177 us -> 228 us  [the longest x1 96.2 us: last_grads(): pl.pallas_call(functools.partial(last_grads_kernel, n, n_dp, rows), out_s...]
    psum x3 -> x0, blocking collectives: 49.5 us -> none  [the longest x1 22.8 us: local(): lax.psum(jnp.concatenate([attn_gain_sum, mlp_gain_sum, query_gain_part[0]...]
    dot_general x5 -> x3, matrix products: 57.6 us -> 42.5 us  [inner_dot(): lax.dot_general(former, latter, (((0,), (0,)), ((), ())), preferred_eleme...]
    unnamed x48 -> x39, local copies, waits for them, and re-layouts: 15 us -> 5.23 us
  transfers between devices with their start and end apart: 10 -> 8, of which waited for: 2 -> 3; matrix products, arithmetic and copies ran while one was open for 11% -> 9% of each run, Pallas kernels for 33% -> 63%
where the time goes in v2:
time: 769 us; the launch traced here: 760 us
  Pallas kernels  620 us (81%)
  matrix products  60.4 us (8%)
  waiting for transfers between devices  33 us (4%)
  other arithmetic  16.3 us (2%)
  local copies, waits for them, and re-layouts  15.4 us (2%)
  between operations  14.8 us (2%)
    pallas_call x1, Pallas kernels, mlp_forward(): pl.pallas_call(functools.partial(mlp_forward_kernel, n, rows), out_shape=...  140 us
    pallas_call x1, Pallas kernels, mlp_backward(): pl.pallas_call(functools.partial(mlp_backward_kernel, n, rows), out_shape...  135 us
    pallas_call x1, Pallas kernels, attn_out(): pl.pallas_call(functools.partial(attn_out_kernel, n, rows), out_shape=(ja...  117 us
    pallas_call x1, Pallas kernels, last_grads(): pl.pallas_call(functools.partial(last_grads_kernel, n, n_dp, rows), out_s...  96.2 us
    pallas_call x1, Pallas kernels, gather_rows(): pl.pallas_call(functools.partial(gather_rows_kernel, n, n_dp, rows), out_...  76.1 us
    dot_general x3, matrix products, inner_dot(): lax.dot_general(former, latter, (((0,), (0,)), ((), ())), preferred_eleme...  42.5 us
    pallas_call x1, Pallas kernels, attention_back(): pl.pallas_call(functools.partial(attention_back_kernel, n, heads, model_w...  29.1 us
    reduce_scatter x3, waiting for transfers between devices, dp_scatter(): return lax.psum_scatter(part, 'dp', scatter_dimension=dimension, tiled=True)  26.8 us
  transfers between devices with their start and end apart: 8, of which 3 were waited for; matrix products, arithmetic and copies ran while one was open for 9% of the time, Pallas kernels for 63%

profile of v2, /device:TPU:0, one launch (start us, length us, event | category | flops | bytes accessed | tf_op | source)
XLA Modules:
  0.0 760.5 jit_solution(16633123961735112254)
XLA Ops:
  7.3 2.0 pad_maximum_fusion
  13.7 76.1 %gather_rows.1 = (bf16[4,256,2048]{2,1,0:T(8,128)(2,1)}, f32[8,1,640]{2,1,0:T(1,128)}) custom-call(bf16[256,2048]{1,0:T(8,128)(2,1)} %x.1, f32[1,640]{1,0:T(1,128)} %maximum_convert_fusion.gains), custom_call_target="tpu_custom_call" | custom-call | flops 74999996416 | bytes 225000000 | tf_op jit(solution)/shard_map/gather_rows/pallas_call | solution.py:348
  96.7 1.9 fusion
  98.7 1.3 pad_maximum_fusion.1
  100.0 11.8 %fusion.7.qkv = f32[1024,1536]{1,0:T(8,128)} fusion(bf16[1024,2048]{1,0:T(8,128)(2,1)} %bitcast.69, bf16[2048,1536]{1,0:T(8,128)(2,1)} %all-gather.6.cloned.1.call-done.weight), kind=kOutput, calls=%fused_computation.35 | convolution fusion | flops 6442450944 | bytes 16777216 | tf_op jit(solution)/shard_map/dot_general | solution.py:32
  111.7 26.8 %attention.1 = (bf16[1024,512]{1,0:T(8,128)(2,1)}, bf16[1024,512]{1,0:T(8,128)(2,1)}, bf16[1024,512]{1,0:T(8,128)(2,1)}, bf16[1024,512]{1,0:T(8,128)(2,1)}, f32[...) custom-call(f32[1024,1536]{1,0:T(8,128)} %fusion.7.qkv, f32[1,512]{1,0:T(1,128)} %reshape.197.q_gain, ...), custom_call_target="tpu_custom_call" | custom-call | flops 24999999488 | bytes 75000000 | tf_op jit(solution)/shard_map/attention/pallas_call | solution.py:1041
  138.5 116.9 %attn_out.1 = (f32[256,2048]{1,0:T(8,128)}, f32[256,2048]{1,0:T(8,128)}, bf16[4,256,2048]{2,1,0:T(8,128)(2,1)}) custom-call(bf16[1024,512]{1,0:T(8,128)(2,1)} %get-tuple-element.53.att, bf16[512,2048]{1,0:T(8,128)(2,1)} %all-gather.8.cloned.1.call-done.wo, bf16[256,2048]{1,0:T(8,128)(2,1)} %x.1, f32[1,2048]{1,0:T(1,128)} %bitcast.61), custom_call_target="tpu_custom_call" | custom-call | flops 115000000512 | bytes 345000000 | tf_op jit(solution)/shard_map/attn_out/pallas_call | solution.py:407
  255.5 3.6 all-gather.14.cloned.1.call-done.wd
  259.1 140.3 %mlp_forward.1 = (bf16[256,2048]{1,0:T(8,128)(2,1)}, bf16[4,256,2048]{2,1,0:T(8,128)(2,1)}, bf16[4,256,2048]{2,1,0:T(8,128)(2,1)}, bf16[4,256,2048]{2,1,0:T(8,12...) custom-call(bf16[4,256,2048]{2,1,0:T(8,128)(2,1)} %get-tuple-element.54.h_full, ...), custom_call_target="tpu_custom_call" | custom-call | flops 134999998464 | bytes 405000000 | tf_op jit(solution)/shard_map/mlp_forward/pallas_call | solution.py:547
  399.4 14.0 %bitcast_convert_fusion.2 = bf16[2048,2048]{1,0:T(8,128)(2,1)} fusion(bf16[4,256,2048]{2,1,0:T(8,128)(2,1)} %get-tuple-element.61, bf16[4,256,2048]{2,1,0:T(8,128)(2,1)} %get-tuple-element.62.dm_full), kind=kOutput, calls=%fused_computation.2 | convolution fusion | flops 8594128896 | bytes 16777216 | tf_op jit(solution)/shard_map/dot_general | solution.py:36
  413.5 134.8 %mlp_backward.1 = (f32[256,2048]{1,0:T(8,128)}, bf16[4,256,2048]{2,1,0:T(8,128)(2,1)}, bf16[4,256,2048]{2,1,0:T(8,128)(2,1)}, bf16[4,256,2048]{2,1,0:T(8,128)(2,1)}, f32[1,2048]{1,0:T(1,128)}) custom-call(bf16[4,256,2048]{2,1,0:T(8,128)(2,1)} %get-tuple-element.62.dm_full, bf16[2048,2048]{1,0:T(8,128)(2,1)} %all-gather.10.cloned.1.call-done.wg, ...), custom_call_target="tpu_custom_call" | custom-call | flops 137000001536 | bytes 411000000 | tf_op jit(solution)/shard_map/mlp_backward/pallas_call | solution.py:689
  548.3 14.0 %bitcast_convert_fusion.1 = bf16[2048,2048]{1,0:T(8,128)(2,1)} fusion(bf16[4,256,2048]{2,1,0:T(8,128)(2,1)} %get-tuple-element.54.h_full, bf16[4,256,2048]{2,1,0:T(8,128)(2,1)} %get-tuple-element.67), kind=kOutput, calls=%fused_computation.1 | convolution fusion | flops 8594128896 | bytes 16777216 | tf_op jit(solution)/shard_map/dot_general | solution.py:36
  562.4 14.5 %bitcast_convert_fusion = bf16[2048,2048]{1,0:T(8,128)(2,1)} fusion(bf16[4,256,2048]{2,1,0:T(8,128)(2,1)} %get-tuple-element.54.h_full, bf16[4,256,2048]{2,1,0:T(8,128)(2,1)} %get-tuple-element.74), kind=kOutput, calls=%fused_computation | convolution fusion | flops 8594128896 | bytes 16777216 | tf_op jit(solution)/shard_map/dot_general | solution.py:36
  576.9 6.1 convolution_convert_fusion.out_grad
  583.0 29.1 %attention_back.1 = (bf16[1024,1536]{1,0:T(8,128)(2,1)}, f32[1,512]{1,0:T(1,128)}, f32[1,512]{1,0:T(1,128)}) custom-call(f32[1024,1536]{1,0:T(8,128)} %fusion.7.qkv, bf16[1024,512]{1,0:T(8,128)(2,1)} %get-tuple-element.57.q_low, bf16[1024,512]{1,0:T(8,128)(2,1)} %get-tuple-element.58.k_low, bf16[1024,512]{1,0:T(8,128)(2,1)} %get-tuple-element.59.v_low, ...), custom_call_target="tpu_custom_call" | custom-call | flops 30000001024 | bytes 90000000 | tf_op jit(solution)/shard_map/attention_back/pallas_call | solution.py:1130
  612.2 22.6 %reduce-scatter.6.cloned.1.call-done = bf16[256,2048]{1,0:T(8,128)(2,1)} async-done(((bf16[2048,2048]{1,0:T(8,128)(2,1)}), bf16[256,2048]{1,0:T(8,128)(2,1)}) %reduce-scatter.6.cloned.1.call-update) | async-done | bytes 1048592 | tf_op jit(solution)/shard_map/reduce_scatter | solution.py:1218
  639.3 1.5 convert_element_type.53
  640.8 96.2 %last_grads.1 = (f32[256,2048]{1,0:T(8,128)}, f32[256,1536]{1,0:T(8,128)}, f32[512,256]{1,0:T(8,128)}, f32[1,640]{1,0:T(1,128)}) custom-call(bf16[1024,1536]{1,0:T(8,128)(2,1)} %get-tuple-element.76.grads, bf16[2048,1536]{1,0:T(8,128)(2,1)} %all-gather.6.cloned.1.call-done.weight, f32[256,2048]{1,0:T(8,128)} %get-tuple-element.77.base, ...), custom_call_target="tpu_custom_call" | custom-call | flops 89999998976 | bytes 270000000 | tf_op jit(solution)/shard_map/last_grads/pallas_call | solution.py:911
  739.1 1.6 convert_element_type.51
  740.7 1.2 fusion.6
  741.9 1.2 fusion.4
  743.1 4.2 reduce-scatter.8.cloned.1.call-done
  747.3 2.8 convert_element_type.52
  751.1 1.3 copy.76
  (100 shorter events, 19.7 us)
Async XLA Ops:
  7.2 4.9 copy-start.13
  7.2 5.6 copy-start.14
  7.2 5.6 copy-start.15
  7.2 5.7 copy-start.11
  7.2 5.7 copy-start.12
  7.2 92.7 %all-gather.6.cloned.1.call-start = ((), (), s32[]{:S(2)}) async-start(), calls=%async_computation.3 | async-start | bytes 7077888 | tf_op jit(solution)/shard_map/all_gather | solution.py:1175
  9.3 129.2 %all-gather.8.cloned.1.call-start = ((), (), s32[]{:S(2)}) async-start(), calls=%async_computation.4 | async-start | bytes 2359296 | tf_op jit(solution)/shard_map/all_gather | solution.py:1178
  10.1 245.4 %all-gather.10.cloned.1.call-start = ((), (), s32[]{:S(2)}) async-start(), calls=%async_computation.5 | async-start | bytes 9437184 | tf_op jit(solution)/shard_map/all_gather | solution.py:1179
  10.8 244.7 %all-gather.12.cloned.1.call-start = ((), (), s32[]{:S(2)}) async-start(), calls=%async_computation.6 | async-start | bytes 9437184 | tf_op jit(solution)/shard_map/all_gather | solution.py:1180
  11.4 247.7 %all-gather.14.cloned.1.call-start = ((), (), s32[]{:S(2)}) async-start(), calls=%async_computation.7 | async-start | bytes 9437184 | tf_op jit(solution)/shard_map/all_gather | solution.py:1181
  12.0 550.3 %reduce-scatter.4.cloned.1.call-start = ((), (), s32[]{:S(2)}) async-start(), calls=%async_computation.8 | async-start | bytes 9437184 | tf_op jit(solution)/shard_map/reduce_scatter | solution.py:1218
  413.4 221.4 %reduce-scatter.6.cloned.1.call-start = ((), (), s32[]{:S(2)}) async-start(), calls=%async_computation.9 | async-start | bytes 9437184 | tf_op jit(solution)/shard_map/reduce_scatter | solution.py:1218
  562.3 185.0 %reduce-scatter.8.cloned.1.call-start = ((), (), s32[]{:S(2)}) async-start(), calls=%async_computation.10 | async-start | bytes 9437184 | tf_op jit(solution)/shard_map/reduce_scatter | solution.py:1218
  562.4 14.5 %copy-start.10 = (bf16[512,2048]{1,0:T(8,128)(2,1)S(1)}, bf16[512,2048]{1,0:T(8,128)(2,1)}, u32[]{:S(2)}) copy-start(bf16[512,2048]{1,0:T(8,128)(2,1)} %all-gather.8.cloned.1.call-done.wo) | copy-start | bytes 6291460
  634.8 0.7 copy-start.7
  634.8 1.4 copy-start.6
  634.8 2.1 copy-start.9
  634.8 2.9 copy-start.8
  634.8 4.5 copy-start.2
  640.8 98.4 %copy-start.3 = (bf16[256,2048]{1,0:T(8,128)(2,1)S(1)}, bf16[256,2048]{1,0:T(8,128)(2,1)}, u32[]{:S(2)}) copy-start(bf16[256,2048]{1,0:T(8,128)(2,1)} %reduce-scatter.6.cloned.1.call-done) | copy-start | bytes 3145732
  739.1 2.8 copy-start.1
  739.1 11.0 %copy-start.4 = (bf16[256,2048]{1,0:T(8,128)(2,1)S(1)}, bf16[256,2048]{1,0:T(8,128)(2,1)}, u32[]{:S(2)}) copy-start(bf16[256,2048]{1,0:T(8,128)(2,1)} %get-tuple-element.120) | copy-start | bytes 3145732
  741.9 9.2 %copy-start = (f32[256,2048]{1,0:T(8,128)S(1)}, f32[256,2048]{1,0:T(8,128)}, u32[]{:S(2)}) copy-start(f32[256,2048]{1,0:T(8,128)} %get-tuple-element.121) | copy-start | bytes 6291460
  747.3 5.1 copy-start.5
Sparse Core Ops, SparseCore 0:
  10.5 48.2 all-gather.5
  60.7 28.1 all-gather.7
  90.8 54.3 all-gather.9
  147.0 54.4 all-gather.11
  203.2 55.8 all-gather.13
  413.6 70.2 reduce-scatter.3
  562.5 72.3 reduce-scatter.5
  638.3 108.9 reduce-scatter.7

commit v3 on v2

--- a/solution.py
+++ b/solution.py
@@ -13,7 +13,9 @@
 MASKED = -1000000000.0
 CHUNKS = 4
 STAGGER = 2
-TILE = 256
+EDGES = False
+FILL = 2
+TILE = 512
 QUERY_ROWS = 256
 BF = jnp.bfloat16
 F32 = jnp.float32
@@ -148,9 +150,9 @@
 
 
 class LineScatter:
-    def __init__(self, n, me, rows, part, send, recv, send_sem, recv_sem):
+    def __init__(self, n, me, rows, part, recv, send_sem, recv_sem):
         self.n, self.me, self.rows = n, me, rows
-        self.part, self.send, self.recv = part, send, recv
+        self.part, self.recv = part, recv
         self.send_sem, self.recv_sem = send_sem, recv_sem
 
     def piece(self, c, owner):
@@ -169,26 +171,27 @@
     def sides(self):
         return ((0, self.me), (1, self.n - 1 - self.me))
 
+    def owner(self, way, step):
+        return self.n - 1 - step + self.me if way == 0 else step - (self.n - 1 - self.me)
+
+    def edge(self, c, step):
+        for way, place in self.sides():
+
+            @pl.when(place == 0)
+            def _(way=way):
+                self.copy(c, step, way, self.piece(c, self.owner(way, step))).start()
+
     def step(self, c, step):
-        n = self.n
         for way, place in self.sides():
-            owner = n - 1 - step + self.me if way == 0 else step - (n - 1 - self.me)
-
-            @pl.when(place == 0)
-            def _(way=way, owner=owner):
-                self.copy(c, step, way, self.piece(c, owner)).start()
-
-            if step > 0:
-
-                @pl.when((place > 0) & (place <= min(step, n - 2)))
-                def _(way=way, owner=owner):
-                    slot = self.send.at[c, step - 1, way]
-                    self.copy(c, step - 1, way, slot).wait_recv()
-                    slot[...] = (
-                        self.piece(c, owner)[...].astype(F32)
-                        + self.recv[c, step - 1, way].astype(F32)
-                    ).astype(BF)
-                    self.copy(c, step, way, slot).start()
+
+            @pl.when((place > 0) & (place <= min(step, self.n - 2)))
+            def _(way=way):
+                piece = self.piece(c, self.owner(way, step))
+                self.copy(c, step - 1, way, piece).wait_recv()
+                piece[...] = (
+                    piece[...].astype(F32) + self.recv[c, step - 1, way].astype(F32)
+                ).astype(BF)
+                self.copy(c, step, way, piece).start()
 
     def total(self, c, out):
         n = self.n
@@ -210,15 +213,23 @@
                     self.copy(c, step, way, self.recv.at[c, step, way]).wait_send()
 
 
-def run_line(n, chunks, stagger, compute, scatter, row_work, gather):
+def run_line(n, chunks, stagger, compute, scatter, row_work, gather, filler=None):
     last_step = 2 * n - 2 if gather is not None else n - 1
     events = sorted(
-        (step + stagger * c, c, step) for c in range(chunks) for step in range(last_step + 1)
-    )
+        (step + stagger * c - (0.5 if step == 0 else 0), c, step)
+        for c in range(chunks)
+        for step in range(last_step + 1)
+    )
+    computed = 0
     for _, c, step in events:
-        if step < n - 1:
-            if step == 0:
-                compute(c)
+        if step == 0:
+            compute(c)
+            for ahead in range(n - 1 if EDGES else 1):
+                scatter.edge(c, ahead)
+            computed += 1
+        elif step < n - 1:
+            if not EDGES:
+                scatter.edge(c, step)
             scatter.step(c, step)
         elif step == n - 1:
             row_work(c)
@@ -228,10 +239,128 @@
             gather.step(c, step - n + 2)
         else:
             gather.last(c)
+        if filler is not None and computed == chunks:
+            filler()
     for c in range(chunks):
         scatter.drain(c)
         if gather is not None:
             gather.drain(c)
+
+
+def flipped(chip, bit):
+    return chip + bit - 2 * bit * lax.rem(chip // bit, 2)
+
+
+def bits_of(number):
+    return [1 << k for k in range(number.bit_length()) if number >> k & 1]
+
+
+def relative_chip(chip, relative):
+    for bit in bits_of(relative):
+        chip = flipped(chip, bit)
+    return chip
+
+
+def relative_order(chips):
+    return sorted(range(chips), key=lambda r: (-len(bits_of(r)), r))
+
+
+class PlaneReduce:
+    def __init__(self, at, chips, rows, views, sems, out):
+        self.chip, self.core = at // 2, lax.rem(at, 2)
+        self.chips, self.rows, self.out = chips, rows, out
+        self.core_send, self.core_recv, self.held, self.message = views
+        self.core_send_sem, self.core_recv_sem, self.send_sem, self.recv_sem = sems
+
+    def first_bit(self, relative, half):
+        bits = bits_of(relative)
+        return bits[0] if half == 0 else bits[-1]
+
+    def before(self, relative, half):
+        return [
+            r for r in range(1, self.chips) if r - self.first_bit(r, half) == relative
+        ]
+
+    def owner(self, relative, same_core):
+        return 2 * relative_chip(self.chip, relative) + (
+            self.core if same_core else 1 - self.core
+        )
+
+    def half_rows(self, half):
+        return pl.ds(half * (self.rows // 2), self.rows // 2)
+
+    def core_copy(self, relative):
+        return pltpu.make_async_remote_copy(
+            src_ref=self.core_send(relative),
+            dst_ref=self.core_recv(relative),
+            send_sem=self.core_send_sem.at[relative],
+            recv_sem=self.core_recv_sem.at[relative],
+            device_id={"dp": 2 * self.chip + 1 - self.core},
+        )
+
+    def message_copy(self, relative, half):
+        span = self.half_rows(half)
+        target = flipped(self.chip, self.first_bit(relative, half))
+        return pltpu.make_async_remote_copy(
+            src_ref=self.held(relative).at[span],
+            dst_ref=self.message(relative).at[span],
+            send_sem=self.send_sem.at[relative, half],
+            recv_sem=self.recv_sem.at[relative, half],
+            device_id={"dp": 2 * target + self.core},
+        )
+
+    def push(self, relative, half):
+        span = self.half_rows(half)
+        for r in self.before(relative, half):
+            self.message_copy(r, half).wait_recv()
+            held = self.held(relative)
+            held[span] = (
+                held[span].astype(F32) + self.message(r)[span].astype(F32)
+            ).astype(BF)
+        self.message_copy(relative, half).start()
+
+    def finish(self):
+        for half in range(2):
+            span = self.half_rows(half)
+            for r in self.before(0, half):
+                self.message_copy(r, half).wait_recv()
+                self.out[span] += self.message(r)[span].astype(F32)
+
+    def drain_core(self, relative):
+        self.core_copy(relative).wait_send()
+
+    def drain(self):
+        for r in range(1, self.chips):
+            for half in range(2):
+                self.message_copy(r, half).wait_send()
+
+
+def plane_sems(chips):
+    return [pltpu.SemaphoreType.DMA((chips,))] * 2 + [pltpu.SemaphoreType.DMA((chips, 2))] * 2
+
+
+def stage_barrier(me, n, at, chips):
+    barrier = pltpu.get_barrier_semaphore()
+
+    @pl.when(me > 0)
+    def _():
+        pl.semaphore_signal(barrier, inc=1, device_id={"mp": me - 1})
+
+    @pl.when(me < n - 1)
+    def _():
+        pl.semaphore_signal(barrier, inc=1, device_id={"mp": me + 1})
+
+    count = signal_partners(barrier, at, chips)
+    pl.semaphore_wait(barrier, count + jnp.minimum(me, 1) + jnp.minimum(n - 1 - me, 1))
+
+
+def signal_partners(sem, at, chips):
+    chip, core = at // 2, lax.rem(at, 2)
+    pl.semaphore_signal(sem, inc=1, device_id={"dp": 2 * chip + 1 - core})
+    bits = [1 << k for k in range(chips.bit_length() - 1)]
+    for bit in bits:
+        pl.semaphore_signal(sem, inc=1, device_id={"dp": 2 * flipped(chip, bit) + core})
+    return 1 + len(bits)
 
 
 def inverse_rms(rows):
@@ -248,7 +377,6 @@
 def scatter_scratch(n, rows, width):
     return [
         pltpu.VMEM((CHUNKS, n * rows, width), BF),
-        pltpu.VMEM((CHUNKS, max(n - 2, 1), 2, rows, width), BF),
         pltpu.VMEM((CHUNKS, n - 1, 2, rows, width), BF),
         pltpu.SemaphoreType.DMA((CHUNKS, n - 1, 2)),
         pltpu.SemaphoreType.DMA((CHUNKS, n - 1, 2)),
@@ -367,7 +495,7 @@
 
 def attn_out_kernel(
     n, rows, att, wo, x, scale, branch, middle, full,
-    part, send, recv, rs_send_sem, rs_recv_sem, total, own, ag_send_sem, ag_recv_sem, local_sem,
+    part, recv, rs_send_sem, rs_recv_sem, total, own, ag_send_sem, ag_recv_sem, local_sem,
     packed,
 ):
     me = lax.axis_index("mp")
@@ -381,12 +509,12 @@
                 j * block_rows + c * rows : j * block_rows + (c + 1) * rows
             ]
 
-        @pl.loop(0, width // (2 * TILE))
+        @pl.loop(0, width // TILE)
         def _(tile):
-            cols = pl.ds(pl.multiple_of(tile * 2 * TILE, 2 * TILE), 2 * TILE)
+            cols = pl.ds(pl.multiple_of(tile * TILE, TILE), TILE)
             part[c, :, cols] = plain_dot(packed[...], wo[:, cols]).astype(BF)
 
-    scatter = LineScatter(n, me, rows, part, send, recv, rs_send_sem, rs_recv_sem)
+    scatter = LineScatter(n, me, rows, part, recv, rs_send_sem, rs_recv_sem)
     gather = make_gather(n, me, rows, own, full, ag_send_sem, ag_recv_sem, local_sem)
 
     def row_work(c):
@@ -446,7 +574,7 @@
 def mlp_forward_kernel(
     n, rows, h_full, wg, wu, wd, middle, upstream_in, row_valid, scale,
     output, dm_full, gate_out, up_out, hidden_out, gain_out,
-    part, send, recv, rs_send_sem, rs_recv_sem, total, own, ag_send_sem, ag_recv_sem, local_sem,
+    part, recv, rs_send_sem, rs_recv_sem, total, own, ag_send_sem, ag_recv_sem, local_sem,
     vg, vu, vd, wsem, h_buf, h_sem, gate_buf, up_buf, hidden_buf, out_sem,
 ):
     me = lax.axis_index("mp")
@@ -517,7 +645,7 @@
             cols = pl.ds(pl.multiple_of(tile * TILE, TILE), TILE)
             part[c, :, cols] = plain_dot(hidden_buf[slot], vd[:, cols]).astype(BF)
 
-    scatter = LineScatter(n, me, rows, part, send, recv, rs_send_sem, rs_recv_sem)
+    scatter = LineScatter(n, me, rows, part, recv, rs_send_sem, rs_recv_sem)
     gather = make_gather(n, me, rows, own, dm_full, ag_send_sem, ag_recv_sem, local_sem)
 
     def row_work(c):
@@ -577,13 +705,18 @@
 
 
 def mlp_backward_kernel(
-    n, rows, dm_full, wg, wu, wd, gate_in, up_in, branch, upstream_in, row_valid, scale,
-    middle_grad, da_full, gate_grad, up_grad, gain_out,
-    part, send, recv, rs_send_sem, rs_recv_sem, total, own, ag_send_sem, ag_recv_sem, local_sem,
-    vg, vu, vd, wsem, dm_buf, gate_buf, up_buf, in_sem, dgate_buf, dup_buf, out_sem,
+    n, n_dp, rows, dm_full, h_full, wg, wu, wd, gate_in, up_in, branch, upstream_in, row_valid,
+    scale,
+    middle_grad, da_full, gain_out, gate_out, up_out,
+    part, recv, rs_send_sem, rs_recv_sem, total, own, ag_send_sem, ag_recv_sem, local_sem,
+    vg, vu, vd, wsem, dm_buf, gate_buf, up_buf, in_sem, dgate, dup, mg_buf, mg_sem,
+    h_buf, h_sem, extra, ready, *plane,
 ):
-    me = lax.axis_index("mp")
+    me, at = lax.axis_index("mp"), lax.axis_index("dp")
     width, hidden_width = wg.shape
+    chips = n_dp // 2
+    part_width = width // n_dp
+    size = n * rows * CHUNKS
 
     def in_copies(c, j):
         span = pl.ds(j * rows, rows)
@@ -606,27 +739,13 @@
     for tile in range(gate_tiles.count):
         gate_tiles.copy(tile).start()
         up_tiles.copy(tile).start()
-    neighbour_barrier(me, n)
-
-    def save_copies(c, j):
-        slot = c % 2
-        span = pl.ds(j * rows, rows)
-        return [
-            pltpu.make_async_copy(
-                buf.at[slot, span], out.at[j, chunk_span(c, rows)], out_sem.at[slot, k, j]
-            )
-            for k, (buf, out) in enumerate(((dgate_buf, gate_grad), (dup_buf, up_grad)))
-        ]
+    stage_barrier(me, n, at, chips)
 
     def compute(c):
-        slot = c % 2
+        here = pl.ds(c * n * rows, n * rows)
         for j in range(n):
             for copy in in_copies(c, j):
                 copy.wait()
-        if c >= 2:
-            for j in range(n):
-                for copy in save_copies(c - 2, j):
-                    copy.wait()
 
         @pl.loop(0, hidden_width // TILE)
         def _(tile):
@@ -637,18 +756,15 @@
             gate = gate_buf[:, cols].astype(F32)
             up = up_buf[:, cols].astype(F32)
             sigmoid = jax.nn.sigmoid(gate)
-            dgate_buf[slot, :, cols] = (
+            dgate[here, cols] = (
                 hidden_grad * up * sigmoid * (1.0 + gate * (1.0 - sigmoid))
             ).astype(BF)
-            dup_buf[slot, :, cols] = (hidden_grad * gate * sigmoid).astype(BF)
+            dup[here, cols] = (hidden_grad * gate * sigmoid).astype(BF)
 
         if c + 1 < CHUNKS:
             for j in range(n):
                 for copy in in_copies(c + 1, j):
                     copy.start()
-        for j in range(n):
-            for copy in save_copies(c, j):
-                copy.start()
 
         @pl.loop(0, width // TILE)
         def _(tile):
@@ -657,46 +773,174 @@
                 up_tiles.copy(tile).wait()
             cols = pl.ds(pl.multiple_of(tile * TILE, TILE), TILE)
             part[c, :, cols] = (
-                outer_dot(dgate_buf[slot], vg[cols, :]) + outer_dot(dup_buf[slot], vu[cols, :])
+                outer_dot(dgate[here], vg[cols, :]) + outer_dot(dup[here], vu[cols, :])
             ).astype(BF)
 
-    scatter = LineScatter(n, me, rows, part, send, recv, rs_send_sem, rs_recv_sem)
+        if c + 1 == CHUNKS:
+            for copy in h_copies(0):
+                copy.start()
+            signal_partners(ready, at, chips)
+
+    scatter = LineScatter(n, me, rows, part, recv, rs_send_sem, rs_recv_sem)
     gather = make_gather(n, me, rows, own, da_full, ag_send_sem, ag_recv_sem, local_sem)
+
+    def mg_copy(c):
+        return pltpu.make_async_copy(
+            mg_buf.at[c % 2], middle_grad.at[chunk_span(c, rows)], mg_sem.at[c % 2]
+        )
 
     def row_work(c):
         scatter.total(c, total)
         span = chunk_span(c, rows)
         upstream = upstream_in[span].astype(F32) * row_valid[span] + total[...]
-        middle_grad[span] = upstream
+        if c >= 2:
+            mg_copy(c - 2).wait()
+        mg_buf[c % 2] = upstream
+        mg_copy(c).start()
         value = branch[span]
         grad, gain = norm_back(value, inverse_rms(value), scale[...], upstream)
         own[c] = grad.astype(BF)
         gain_out[...] = gain if c == 0 else gain_out[...] + gain
 
-    run_line(n, CHUNKS, STAGGER, compute, scatter, row_work, gather)
+    block_width = pl.ds(0, hidden_width)
+
+    def slot(index):
+        for ref in (vg, vu, vd):
+            count = ref.shape[0] // part_width
+            if index < count:
+                return ref.at[pl.ds(index * part_width, part_width), block_width]
+            index -= count
+        return extra.at[index]
+
+    base = [chips, chips + 3 * chips]
+    reduces = []
+    for which, out in enumerate((gate_out, up_out)):
+        first = base[which]
+        views = (
+            lambda r: slot(r),
+            lambda r, first=first: slot(first + r),
+            lambda r, first=first: slot(first + chips + r),
+            lambda r, first=first: slot(first + 2 * chips + r - 1),
+        )
+        reduces.append(
+            PlaneReduce(at, chips, part_width, views, plane[4 * which : 4 * which + 4], out)
+        )
+    order = relative_order(chips)
+    jobs = [
+        (which, same_core, r)
+        for which in range(2)
+        for same_core in (False, True)
+        for r in order
+    ]
+
+    def h_copies(index):
+        which, same_core, r = jobs[index]
+        first = reduces[which].owner(r, same_core) * part_width
+        cols = pl.ds(pl.multiple_of(first, part_width), part_width)
+        return [
+            pltpu.make_async_copy(
+                h_full.at[j, :, cols],
+                h_buf.at[index % 2, j],
+                h_sem.at[index % 2, j],
+            )
+            for j in range(n)
+        ]
+
+    def weight_block(index):
+        which, same_core, r = jobs[index]
+        reduce = reduces[which]
+        grad = (dgate, dup)[which]
+        if index == 0:
+            pl.semaphore_wait(ready, 1 + len(bits_of(chips - 1)))
+        for copy in h_copies(index):
+            copy.wait()
+        if index + 1 < len(jobs):
+            for copy in h_copies(index + 1):
+                copy.start()
+        if same_core:
+            reduce.core_copy(r).wait_recv()
+        elif which == 1:
+            reduces[0].drain_core(r)
+        left = jnp.concatenate(
+            [
+                h_buf[index % 2, j, c * rows : (c + 1) * rows]
+                for c in range(CHUNKS)
+                for j in range(n)
+            ],
+            axis=0,
+        )
+
+        @pl.loop(0, hidden_width // TILE)
+        def _(tile):
+            cols = pl.ds(pl.multiple_of(tile * TILE, TILE), TILE)
+            block = inner_dot(left, grad[:, cols])
+            if not same_core:
+                reduce.core_send(r)[:, cols] = block.astype(BF)
+            else:
+                block = block + reduce.core_recv(r)[:, cols].astype(F32)
+                if r > 0:
+                    reduce.held(r)[:, cols] = block.astype(BF)
+                else:
+                    reduce.out[:, cols] = block
+
+        if not same_core:
+            reduce.core_copy(r).start()
+
+    work = []
+    for index, (which, same_core, r) in enumerate(jobs):
+        work.append(lambda index=index: weight_block(index))
+        if same_core and r > 0:
+            for half in range(2):
+                if not reduces[which].before(r, half):
+                    work.append(lambda w=which, r=r, half=half: reduces[w].push(r, half))
+                    work[-2:] = [lambda f=work[-2], g=work[-1]: (f(), g())]
+        if same_core and r == order[-1]:
+            for late in order:
+                for half in range(2):
+                    if late > 0 and reduces[which].before(late, half):
+                        work.append(lambda w=which, r=late, half=half: reduces[w].push(r, half))
+    pending = iter(work)
+
+    def filler():
+        for _ in range(FILL):
+            job = next(pending, None)
+            if job is not None:
+                job()
+
+    run_line(n, CHUNKS, STAGGER, compute, scatter, row_work, gather, filler)
+    for job in pending:
+        job()
+    for reduce in reduces:
+        reduce.finish()
+        reduce.drain()
+    for r in range(chips):
+        reduces[1].drain_core(r)
     for c in range(max(CHUNKS - 2, 0), CHUNKS):
-        for j in range(n):
-            for copy in save_copies(c, j):
-                copy.wait()
-
-
-def mlp_backward(n, dm_full, wg, wu, wd, gate, up, branch, out_grad, row_valid, scale):
+        mg_copy(c).wait()
+
+
+def mlp_backward(n, n_dp, dm_full, h_full, wg, wu, wd, gate, up, branch, out_grad, row_valid, scale):
     row_count, width = branch.shape
     hidden_width = wg.shape[1]
     rows = row_count // CHUNKS
-    saved = jax.ShapeDtypeStruct((n, row_count, hidden_width), BF)
+    size = n * row_count
+    chips = n_dp // 2
+    part_width = width // n_dp
+    block = (part_width, hidden_width)
     most = max(width, hidden_width) // TILE
+    slots = (2 * width + hidden_width) // part_width
+    extra = max(7 * chips - 1 - slots, 1)
     return pl.pallas_call(
-        functools.partial(mlp_backward_kernel, n, rows),
+        functools.partial(mlp_backward_kernel, n, n_dp, rows),
         out_shape=(
             jax.ShapeDtypeStruct((row_count, width), F32),
             jax.ShapeDtypeStruct((n, row_count, width), BF),
-            saved,
-            saved,
             jax.ShapeDtypeStruct((1, width), F32),
+            jax.ShapeDtypeStruct(block, F32),
+            jax.ShapeDtypeStruct(block, F32),
         ),
-        in_specs=[HBM] * 6 + [VMEM] * 4,
-        out_specs=(VMEM, HBM, HBM, HBM, VMEM),
+        in_specs=[HBM] * 7 + [VMEM] * 4,
+        out_specs=(HBM, HBM, VMEM, VMEM, VMEM),
         scratch_shapes=scatter_scratch(n, rows, width)
         + gather_scratch(n, rows, width)
         + [
@@ -709,24 +953,31 @@
             pltpu.VMEM((n * rows, hidden_width), BF),
             pltpu.SemaphoreType.DMA((3, n)),
         ]
-        + [pltpu.VMEM((2, n * rows, hidden_width), BF)] * 2
-        + [pltpu.SemaphoreType.DMA((2, 2, n))],
+        + [pltpu.VMEM((size, hidden_width), BF)] * 2
+        + [
+            pltpu.VMEM((2, rows, width), F32),
+            pltpu.SemaphoreType.DMA((2,)),
+            pltpu.VMEM((2, n, row_count, part_width), BF),
+            pltpu.SemaphoreType.DMA((2, n)),
+            pltpu.VMEM((extra,) + block, BF),
+            pltpu.SemaphoreType.REGULAR,
+        ]
+        + plane_sems(chips) * 2,
         compiler_params=pltpu.CompilerParams(
-            collective_id=3, has_side_effects=True, vmem_limit_bytes=60 * MIB
+            collective_id=3, has_side_effects=True, vmem_limit_bytes=63 * MIB
         ),
         name="mlp_backward",
-        cost_estimate=cost(137),
-    )(dm_full, wg, wu, wd, gate, up, branch, out_grad, row_valid, scale)
+        cost_estimate=cost(145),
+    )(dm_full, h_full, wg, wu, wd, gate, up, branch, out_grad, row_valid, scale)
 
 
 def last_grads_kernel(
     n, n_dp, rows, grads, weight, base, inputs, att, da, gains,
     input_grad, qkv_out, out_out, gain_out,
-    part, send, recv, rs_send_sem, rs_recv_sem, total, packed,
+    part, recv, rs_send_sem, rs_recv_sem, total, packed,
     x_buf, da_buf, load_sem,
-    core_send_qkv, core_send_out, core_recv_qkv, core_recv_out, core_send_sem, core_recv_sem,
-    chip_send_qkv, chip_send_out, chip_recv_qkv, chip_recv_out, chip_send_sem, chip_recv_sem,
-    gain_recv, gain_send_sem, gain_recv_sem, mp_recv, mp_send_sem, mp_recv_sem, own_qkv, own_out,
+    send_qkv, recv_qkv, held_qkv, message_qkv, send_out, recv_out, held_out, message_out,
+    gain_recv, gain_send_sem, gain_recv_sem, mp_recv, mp_send_sem, mp_recv_sem, *plane,
 ):
     me, at = lax.axis_index("mp"), lax.axis_index("dp")
     entered = peer_barrier((("mp", me, n), ("dp", at, n_dp)))
@@ -734,15 +985,29 @@
     block_rows = rows * CHUNKS
     local_width = att.shape[1]
     chips = n_dp // 2
-    chip, core = at // 2, lax.rem(at, 2)
     part_width = width // n_dp
-
-    def place(k):
-        target = lax.rem(chip + 1 + k % chips, chips)
-        return 2 * target + (1 - core if k < chips else core)
+    order = relative_order(chips)
+    jobs = [(same_core, r) for same_core in (False, True) for r in order]
+
+    def views(send, recv, held, message):
+        return (
+            lambda r: send.at[r],
+            lambda r: recv.at[r],
+            lambda r: held.at[r - 1],
+            lambda r: message.at[r - 1],
+        )
+
+    by_qkv = PlaneReduce(
+        at, chips, part_width, views(send_qkv, recv_qkv, held_qkv, message_qkv), plane[:4], qkv_out
+    )
+    by_out = PlaneReduce(
+        at, chips, local_width, views(send_out, recv_out, held_out, message_out), plane[4:], out_out
+    )
 
     def loads(k):
-        cols = pl.ds(pl.multiple_of(place(k) * part_width, part_width), part_width)
+        same_core, r = jobs[k]
+        first = by_qkv.owner(r, same_core) * part_width
+        cols = pl.ds(pl.multiple_of(first, part_width), part_width)
         return [
             pltpu.make_async_copy(inputs.at[:, cols], x_buf.at[k % 2], load_sem.at[k % 2, 0]),
             pltpu.make_async_copy(da.at[:, cols], da_buf.at[k % 2], load_sem.at[k % 2, 1]),
@@ -762,123 +1027,96 @@
             cols = pl.ds(pl.multiple_of(tile * TILE, TILE), TILE)
             part[c, :, cols] = outer_dot(packed[...], weight[cols, :]).astype(BF)
 
-    scatter = LineScatter(n, me, rows, part, send, recv, rs_send_sem, rs_recv_sem)
+    scatter = LineScatter(n, me, rows, part, recv, rs_send_sem, rs_recv_sem)
 
     def row_work(c):
         scatter.total(c, total)
         span = chunk_span(c, rows)
         input_grad[span] = base[span] + total[...]
 
-    def core_copies(k):
-        other = 2 * chip + 1 - core
-        return [
-            pltpu.make_async_remote_copy(
-                src_ref=src.at[k],
-                dst_ref=dst.at[k],
-                send_sem=core_send_sem.at[k, which],
-                recv_sem=core_recv_sem.at[k, which],
-                device_id={"dp": other},
-            )
-            for which, (src, dst) in enumerate(
-                ((core_send_qkv, core_recv_qkv), (core_send_out, core_recv_out))
-            )
-        ]
-
-    def chip_copies(k):
-        other = 2 * lax.rem(chip + 1 + k, chips) + core
-        return [
-            pltpu.make_async_remote_copy(
-                src_ref=src.at[k],
-                dst_ref=dst.at[k],
-                send_sem=chip_send_sem.at[k, which],
-                recv_sem=chip_recv_sem.at[k, which],
-                device_id={"dp": other},
-            )
-            for which, (src, dst) in enumerate(
-                ((chip_send_qkv, chip_recv_qkv), (chip_send_out, chip_recv_out))
-            )
-        ]
-
     def weight_block(k):
+        same_core, r = jobs[k]
         slot = k % 2
         for copy in loads(k):
             copy.wait()
-        if k + 1 < 2 * chips:
+        if k + 1 < len(jobs):
             for copy in loads(k + 1):
                 copy.start()
-        if k >= chips:
-            for copy in core_copies(k - chips):
-                copy.wait_recv()
+        if same_core:
+            by_qkv.core_copy(r).wait_recv()
+            by_out.core_copy(r).wait_recv()
+
+        def keep(reduce, block, cols):
+            if not same_core:
+                reduce.core_send(r)[:, cols] = block.astype(BF)
+                return
+            block = block + reduce.core_recv(r)[:, cols].astype(F32)
+            if r > 0:
+                reduce.held(r)[:, cols] = block.astype(BF)
+            else:
+                reduce.out[:, cols] = block
 
         @pl.loop(0, 3)
         def _(tile):
             cols = pl.ds(pl.multiple_of(tile * local_width, local_width), local_width)
-            block = inner_dot(x_buf[slot], grads[:, cols])
-            if k < chips:
-                core_send_qkv[k, :, cols] = block.astype(BF)
-            else:
-                block = block + core_recv_qkv[k - chips, :, cols].astype(F32)
-                if k < 2 * chips - 1:
-                    chip_send_qkv[k - chips, :, cols] = block.astype(BF)
-                else:
-                    own_qkv[:, cols] = block
-
-        block = inner_dot(att[...], da_buf[slot])
-        if k < chips:
-            core_send_out[k] = block.astype(BF)
-            for copy in core_copies(k):
-                copy.start()
-        else:
-            block = block + core_recv_out[k - chips].astype(F32)
-            if k < 2 * chips - 1:
-                chip_send_out[k - chips] = block.astype(BF)
-                for copy in chip_copies(k - chips):
-                    copy.start()
-            else:
-                own_out[...] = block
+            keep(by_qkv, inner_dot(x_buf[slot], grads[:, cols]), cols)
+
+        keep(by_out, inner_dot(att[...], da_buf[slot]), slice(None))
+        for reduce in (by_qkv, by_out):
+            if not same_core:
+                reduce.core_copy(r).start()
+            elif r > 0:
+                for half in range(2):
+                    if not reduce.before(r, half):
+                        reduce.push(r, half)
 
     gain_copies = exchange(
         "dp", at, n_dp, lambda peer: gains.at[peer], gain_recv, gain_send_sem, gain_recv_sem
     )
     mp_copies = exchange("mp", me, n, lambda peer: gain_out, mp_recv, mp_send_sem, mp_recv_sem)
-
-    compute(0)
-    entered()
-    scatter.step(0, 0)
-    for copy in gain_copies:
-        copy.start()
-    for c in range(1, CHUNKS):
-        compute(c)
-        scatter.step(c, 0)
-    for k in range(chips):
-        weight_block(k)
-    line = [(step, c) for step in range(1, n) for c in range(CHUNKS)]
-    done = 0
-    for k in range(chips, 2 * chips + 1):
-        if k < 2 * chips:
-            weight_block(k)
-        until = len(line) if k == 2 * chips else (k - chips + 1) * CHUNKS // 2
-        for step, c in line[done:until]:
+    line = iter([(step, c) for c in range(CHUNKS) for step in range(1, n)])
+
+    def line_steps(count):
+        for _ in range(count):
+            step, c = next(line, (None, None))
+            if step is None:
+                return
             if step < n - 1:
                 scatter.step(c, step)
             else:
                 row_work(c)
-        done = until
-        if k == chips:
-            gain_out[...] = gains[at]
-            for shift, copy in enumerate(gain_copies, 1):
-                copy.wait_recv()
-                gain_out[...] += gain_recv[shift - 1]
-            for copy in mp_copies:
-                copy.start()
-    for k in range(chips - 1):
-        for copy in chip_copies(k):
-            copy.wait_recv()
-    qkv_out[...] = own_qkv[...]
-    out_out[...] = own_out[...]
-    for k in range(chips - 1):
-        qkv_out[...] += chip_recv_qkv[k].astype(F32)
-        out_out[...] += chip_recv_out[k].astype(F32)
+
+    def send_edges(c):
+        for step in range(n - 1):
+            scatter.edge(c, step)
+
+    compute(0)
+    entered()
+    send_edges(0)
+    for copy in gain_copies:
+        copy.start()
+    blocks = iter(range(len(jobs)))
+    for c in range(1, CHUNKS):
+        weight_block(next(blocks))
+        compute(c)
+        send_edges(c)
+    for k in blocks:
+        weight_block(k)
+        line_steps(2)
+    late = [(r, half) for r in order for half in range(2) if r > 0 and by_qkv.before(r, half)]
+    for r, half in late:
+        for reduce in (by_qkv, by_out):
+            reduce.push(r, half)
+        line_steps(1)
+    gain_out[...] = gains[at]
+    for shift, copy in enumerate(gain_copies, 1):
+        copy.wait_recv()
+        gain_out[...] += gain_recv[shift - 1]
+    for copy in mp_copies:
+        copy.start()
+    line_steps(n * CHUNKS)
+    for reduce in (by_qkv, by_out):
+        reduce.finish()
     for copy in mp_copies:
         copy.wait_recv()
         copy.wait_send()
@@ -891,12 +1129,10 @@
         copy.wait_send()
     for c in range(CHUNKS):
         scatter.drain(c)
-    for k in range(chips):
-        for copy in core_copies(k):
-            copy.wait_send()
-    for k in range(chips - 1):
-        for copy in chip_copies(k):
-            copy.wait_send()
+    for reduce in (by_qkv, by_out):
+        for r in range(chips):
+            reduce.drain_core(r)
+        reduce.drain()
 
 
 def last_grads(n, n_dp, grads, weight, base, inputs, attended, da_full, gains):
@@ -925,20 +1161,21 @@
             pltpu.VMEM((2, size, part_width), BF),
             pltpu.SemaphoreType.DMA((2, 2)),
         ]
-        + [pltpu.VMEM((chips,) + block, BF) for block in (qkv_block, out_block) * 2]
-        + [pltpu.SemaphoreType.DMA((chips, 2))] * 2
-        + [pltpu.VMEM((chips - 1,) + block, BF) for block in (qkv_block, out_block) * 2]
-        + [pltpu.SemaphoreType.DMA((chips - 1, 2))] * 2
+        + [
+            pltpu.VMEM((count,) + block, BF)
+            for block in (qkv_block, out_block)
+            for count in (chips, chips, chips - 1, chips - 1)
+        ]
         + [pltpu.VMEM((n_dp - 1,) + gain_block, F32)]
         + [pltpu.SemaphoreType.DMA((n_dp - 1,))] * 2
         + [pltpu.VMEM((n - 1,) + gain_block, F32)]
         + [pltpu.SemaphoreType.DMA((n - 1,))] * 2
-        + [pltpu.VMEM(qkv_block, F32), pltpu.VMEM(out_block, F32)],
+        + plane_sems(chips) * 2,
         compiler_params=pltpu.CompilerParams(
             collective_id=4, has_side_effects=True, vmem_limit_bytes=60 * MIB
         ),
         name="last_grads",
-        cost_estimate=cost(90),
+        cost_estimate=cost(80),
     )(grads, weight, base, inputs, attended, da_full, gains)
 
 
@@ -1220,25 +1457,18 @@
     down_part = inner_dot(flat(hidden), flat(mlp_grad_full)).astype(BF)
     mlp_grad_full, down_part = lax.optimization_barrier((mlp_grad_full, down_part))
     grad_down = dp_scatter(down_part, 1)
-    middle_grad, branch_full, gate_grad, up_grad, attn_gain_part = mlp_backward(
-        n, mlp_grad_full, full_gate, full_up, full_down, gate, up, branch, out_grad, row_valid,
-        attn_scale,
+    middle_grad, branch_full, attn_gain_part, grad_gate, grad_up = mlp_backward(
+        n, n_dp, mlp_grad_full, middle_full, full_gate, full_up, full_down, gate, up, branch,
+        out_grad, row_valid, attn_scale,
     )
     branch_full = flat(branch_full)
-    gate_part = inner_dot(flat(middle_full), flat(gate_grad)).astype(BF)
-    branch_full, gate_part, grad_down = lax.optimization_barrier(
-        (branch_full, gate_part, grad_down)
-    )
-    grad_gate = dp_scatter(gate_part, 0)
+    branch_full, grad_down = lax.optimization_barrier((branch_full, grad_down))
 
     mixed_grad = outer_dot(branch_full, full_out).astype(BF)
     qkv_grad, query_gain_part, key_gain_part = attention_back(
         n, local_heads, model_width, qkv_raw, query_low, key_low, value_low, mixed_grad, log_total,
         query_inv, key_inv, query_scale, key_scale, cos_table, sin_table, starts,
     )
-    up_part = inner_dot(flat(middle_full), flat(up_grad)).astype(BF)
-    qkv_grad, up_part, grad_gate = lax.optimization_barrier((qkv_grad, up_part, grad_gate))
-    grad_up = dp_scatter(up_part, 0)
 
     def by_part(row):
         return row.reshape(n_dp, -1)
@@ -1268,8 +1498,8 @@
         grad_qkv[:, local_width : 2 * local_width],
         grad_qkv[:, 2 * local_width :],
         grad_out,
-        grad_gate.astype(F32),
-        grad_up.astype(F32),
+        grad_gate,
+        grad_up,
         grad_down.astype(F32),
         gain_sums[heads_at : heads_at + head_part].reshape(local_heads, gain_part),
         gain_sums[heads_at + head_part :].reshape(local_heads, gain_part),

time: 769 us -> 730 us (0.949)
  matrix products: 60.4 us -> 32 us
  waiting for transfers between devices: 33 us -> 4.77 us
  Pallas kernels: 620 us -> 635 us
    pallas_call x1, Pallas kernels: 135 us -> 164 us  [mlp_backward(): pl.pallas_call(functools.partial(mlp_backward_kernel, n, n_dp, rows), out...]
    dot_general x3 -> x1, matrix products: 42.5 us -> 14.1 us  [inner_dot(): lax.dot_general(former, latter, (((0,), (0,)), ((), ())), preferred_eleme...]
    reduce_scatter x3 -> x1, waiting for transfers between devices: 26.8 us -> 0.02 us  [dp_scatter(): return lax.psum_scatter(part, 'dp', scatter_dimension=dimension, tiled=True)]
    pallas_call x1, Pallas kernels: 96.2 us -> 86.8 us  [last_grads(): pl.pallas_call(functools.partial(last_grads_kernel, n, n_dp, rows), out_s...]
  transfers between devices with their start and end apart: 8 -> 6, of which waited for: 3 -> 1; matrix products, arithmetic and copies ran while one was open for 9% -> 4% of each run, Pallas kernels for 63% -> 53%
where the time goes in v3:
time: 730 us; the launch traced here: 721 us
  Pallas kernels  635 us (87%)
  matrix products  32 us (4%)
  local copies, waits for them, and re-layouts  20.9 us (3%)
  between operations  14.8 us (2%)
  other arithmetic  13.9 us (2%)
    pallas_call x1, Pallas kernels, mlp_backward(): pl.pallas_call(functools.partial(mlp_backward_kernel, n, n_dp, rows), out...  164 us
    pallas_call x1, Pallas kernels, mlp_forward(): pl.pallas_call(functools.partial(mlp_forward_kernel, n, rows), out_shape=...  137 us
    pallas_call x1, Pallas kernels, attn_out(): pl.pallas_call(functools.partial(attn_out_kernel, n, rows), out_shape=(ja...  118 us
    pallas_call x1, Pallas kernels, last_grads(): pl.pallas_call(functools.partial(last_grads_kernel, n, n_dp, rows), out_s...  86.8 us
    pallas_call x1, Pallas kernels, gather_rows(): pl.pallas_call(functools.partial(gather_rows_kernel, n, n_dp, rows), out_...  76.1 us
    pallas_call x1, Pallas kernels, attention(): pl.pallas_call(functools.partial(attention_kernel, n, heads, model_width)...  26.8 us
    pallas_call x1, Pallas kernels, attention_back(): pl.pallas_call(functools.partial(attention_back_kernel, n, heads, model_w...  26 us
  transfers between devices with their start and end apart: 6, of which 1 were waited for; matrix products, arithmetic and copies ran while one was open for 4% of the time, Pallas kernels for 53%

profile of v3, /device:TPU:0, one launch (start us, length us, event | category | flops | bytes accessed | tf_op | source)
XLA Modules:
  0.0 721.5 jit_solution(6032420139637799472)
XLA Ops:
  7.3 2.0 pad_maximum_fusion
  13.7 76.1 %gather_rows.1 = (bf16[4,256,2048]{2,1,0:T(8,128)(2,1)}, f32[8,1,640]{2,1,0:T(1,128)}) custom-call(bf16[256,2048]{1,0:T(8,128)(2,1)} %x.1, f32[1,640]{1,0:T(1,128)} %maximum_convert_fusion.gains), custom_call_target="tpu_custom_call" | custom-call | flops 74999996416 | bytes 225000000 | tf_op jit(solution)/shard_map/gather_rows/pallas_call | solution.py:476
  96.8 1.9 fusion
  98.7 1.3 pad_maximum_fusion.1
  100.0 11.8 %fusion.7.qkv = f32[1024,1536]{1,0:T(8,128)} fusion(bf16[1024,2048]{1,0:T(8,128)(2,1)} %bitcast.61, bf16[2048,1536]{1,0:T(8,128)(2,1)} %all-gather.6.cloned.1.call-done.weight), kind=kOutput, calls=%fused_computation.33 | convolution fusion | flops 6442450944 | bytes 16777216 | tf_op jit(solution)/shard_map/dot_general | solution.py:34
  111.8 26.8 %attention.1 = (bf16[1024,512]{1,0:T(8,128)(2,1)}, bf16[1024,512]{1,0:T(8,128)(2,1)}, bf16[1024,512]{1,0:T(8,128)(2,1)}, bf16[1024,512]{1,0:T(8,128)(2,1)}, f32[...) custom-call(f32[1024,1536]{1,0:T(8,128)} %fusion.7.qkv, f32[1,512]{1,0:T(1,128)} %reshape.193.q_gain, ...), custom_call_target="tpu_custom_call" | custom-call | flops 24999999488 | bytes 75000000 | tf_op jit(solution)/shard_map/attention/pallas_call | solution.py:1278
  138.6 118.2 %attn_out.1 = (f32[256,2048]{1,0:T(8,128)}, f32[256,2048]{1,0:T(8,128)}, bf16[4,256,2048]{2,1,0:T(8,128)(2,1)}) custom-call(bf16[1024,512]{1,0:T(8,128)(2,1)} %get-tuple-element.49.att, bf16[512,2048]{1,0:T(8,128)(2,1)} %all-gather.8.cloned.1.call-done.wo, bf16[256,2048]{1,0:T(8,128)(2,1)} %x.1, f32[1,2048]{1,0:T(1,128)} %bitcast.53), custom_call_target="tpu_custom_call" | custom-call | flops 115000000512 | bytes 345000000 | tf_op jit(solution)/shard_map/attn_out/pallas_call | solution.py:535
  256.9 2.2 all-gather.14.cloned.1.call-done.wd
  259.1 137.3 %mlp_forward.1 = (bf16[256,2048]{1,0:T(8,128)(2,1)}, bf16[4,256,2048]{2,1,0:T(8,128)(2,1)}, bf16[4,256,2048]{2,1,0:T(8,128)(2,1)}, bf16[4,256,2048]{2,1,0:T(8,12...) custom-call(bf16[4,256,2048]{2,1,0:T(8,128)(2,1)} %get-tuple-element.50.h_full, ...), custom_call_target="tpu_custom_call" | custom-call | flops 134999998464 | bytes 405000000 | tf_op jit(solution)/shard_map/mlp_forward/pallas_call | solution.py:675
  396.4 14.1 %bitcast_convert_fusion = bf16[2048,2048]{1,0:T(8,128)(2,1)} fusion(bf16[4,256,2048]{2,1,0:T(8,128)(2,1)} %get-tuple-element.57, bf16[4,256,2048]{2,1,0:T(8,128)(2,1)} %get-tuple-element.58.dm_full), kind=kOutput, calls=%fused_computation | convolution fusion | flops 8594128896 | bytes 16777216 | tf_op jit(solution)/shard_map/dot_general | solution.py:38
  410.5 163.6 %mlp_backward.1 = (f32[256,2048]{1,0:T(8,128)}, bf16[4,256,2048]{2,1,0:T(8,128)(2,1)}, f32[1,2048]{1,0:T(1,128)}, f32[256,2048]{1,0:T(8,128)}, f32[256,2048]{1,0:T(8,128)}) custom-call(bf16[4,256,2048]{2,1,0:T(8,128)(2,1)} %get-tuple-element.58.dm_full, bf16[4,256,2048]{2,1,0:T(8,128)(2,1)} %get-tuple-element.50.h_full, ...), custom_call_target="tpu_custom_call" | custom-call | flops 145000005632 | bytes 435000000 | tf_op jit(solution)/shard_map/mlp_backward/pallas_call | solution.py:933
  574.6 1.4 reduce.23
  576.7 6.2 convolution_convert_fusion.out_grad
  582.9 26.0 %attention_back.1 = (bf16[1024,1536]{1,0:T(8,128)(2,1)}, f32[1,512]{1,0:T(1,128)}, f32[1,512]{1,0:T(1,128)}) custom-call(f32[1024,1536]{1,0:T(8,128)} %fusion.7.qkv, bf16[1024,512]{1,0:T(8,128)(2,1)} %get-tuple-element.53.q_low, bf16[1024,512]{1,0:T(8,128)(2,1)} %get-tuple-element.54.k_low, bf16[1024,512]{1,0:T(8,128)(2,1)} %get-tuple-element.55.v_low, ...), custom_call_target="tpu_custom_call" | custom-call | flops 30000001024 | bytes 90000000 | tf_op jit(solution)/shard_map/attention_back/pallas_call | solution.py:1367
  609.0 1.3 reduce.21
  610.5 1.3 reduce.20
  612.7 86.8 %last_grads.1 = (f32[256,2048]{1,0:T(8,128)}, f32[256,1536]{1,0:T(8,128)}, f32[512,256]{1,0:T(8,128)}, f32[1,640]{1,0:T(1,128)}) custom-call(bf16[1024,1536]{1,0:T(8,128)(2,1)} %get-tuple-element.68.grads, bf16[2048,1536]{1,0:T(8,128)(2,1)} %all-gather.6.cloned.1.call-done.weight, f32[256,2048]{1,0:T(8,128)} %get-tuple-element.69.base, ...), custom_call_target="tpu_custom_call" | custom-call | flops 80000000000 | bytes 240000000 | tf_op jit(solution)/shard_map/last_grads/pallas_call | solution.py:1147
  700.3 1.2 fusion.6
  701.5 2.7 fusion.4
  705.5 1.5 convert_element_type.37
  707.0 2.5 copy.69
  709.4 1.3 copy.70
  711.6 1.3 copy.72
  712.9 1.3 copy.73
  (82 shorter events, 16.5 us)
Async XLA Ops:
  7.2 4.9 copy-start.8
  7.2 5.6 copy-start.9
  7.2 5.6 copy-start.10
  7.2 5.7 copy-start.6
  7.2 5.7 copy-start.7
  7.2 92.7 %all-gather.6.cloned.1.call-start = ((), (), s32[]{:S(2)}) async-start(), calls=%async_computation.1 | async-start | bytes 7077888 | tf_op jit(solution)/shard_map/all_gather | solution.py:1412
  9.3 129.2 %all-gather.8.cloned.1.call-start = ((), (), s32[]{:S(2)}) async-start(), calls=%async_computation.2 | async-start | bytes 2359296 | tf_op jit(solution)/shard_map/all_gather | solution.py:1415
  10.1 246.7 %all-gather.10.cloned.1.call-start = ((), (), s32[]{:S(2)}) async-start(), calls=%async_computation.3 | async-start | bytes 9437184 | tf_op jit(solution)/shard_map/all_gather | solution.py:1416
  10.8 246.0 %all-gather.12.cloned.1.call-start = ((), (), s32[]{:S(2)}) async-start(), calls=%async_computation.4 | async-start | bytes 9437184 | tf_op jit(solution)/shard_map/all_gather | solution.py:1417
  11.4 247.7 %all-gather.14.cloned.1.call-start = ((), (), s32[]{:S(2)}) async-start(), calls=%async_computation.5 | async-start | bytes 9437184 | tf_op jit(solution)/shard_map/all_gather | solution.py:1418
  12.0 564.7 %reduce-scatter.2.cloned.1.call-start = ((), (), s32[]{:S(2)}) async-start(), calls=%async_computation.6 | async-start | bytes 9437184 | tf_op jit(solution)/shard_map/reduce_scatter | solution.py:1455
  410.5 165.5 %copy-start.5 = (f32[1,2048]{1,0:T(1,128)S(1)}, f32[1,2048]{1,0:T(1,128)}, u32[]{:S(2)}) copy-start(f32[1,2048]{1,0:T(1,128)} %get-tuple-element.71) | copy-start | bytes 24580
  612.7 92.8 %copy-start.3 = (bf16[2048,256]{1,0:T(8,128)(2,1)S(1)}, bf16[2048,256]{1,0:T(8,128)(2,1)}, u32[]{:S(2)}) copy-start(bf16[2048,256]{1,0:T(8,128)(2,1)} %reduce-scatter.2.cloned.1.call-done) | copy-start | bytes 3145732
  701.5 7.9 %copy-start.2 = (f32[256,2048]{1,0:T(8,128)S(1)}, f32[256,2048]{1,0:T(8,128)}, u32[]{:S(2)}) copy-start(f32[256,2048]{1,0:T(8,128)} %get-tuple-element.113) | copy-start | bytes 6291460
  705.5 5.3 copy-start.4
  707.0 4.6 copy-start.1
  709.4 3.4 copy-start
Sparse Core Ops, SparseCore 0:
  10.5 48.2 all-gather.5
  60.7 28.1 all-gather.7
  90.8 54.4 all-gather.9
  147.0 54.3 all-gather.11
  203.1 55.9 all-gather.13
  410.6 68.7 reduce-scatter.1

commit v4 on v3

--- a/solution.py
+++ b/solution.py
@@ -15,6 +15,7 @@
 STAGGER = 2
 EDGES = False
 FILL = 2
+PERIOD = 8
 TILE = 512
 QUERY_ROWS = 256
 BF = jnp.bfloat16
@@ -141,6 +142,9 @@
 
     def drain(self, c):
         self.local_copy(c).wait()
+        self.drain_sends(c)
+
+    def drain_sends(self, c):
         for step in range(1, self.n):
             for way, place in self.sides():
 
@@ -571,24 +575,44 @@
             self.copy(tile).start()
 
 
-def mlp_forward_kernel(
-    n, rows, h_full, wg, wu, wd, middle, upstream_in, row_valid, scale,
-    output, dm_full, gate_out, up_out, hidden_out, gain_out,
+def mlp_kernel(
+    n, n_dp, rows, h_full, wg, wu, wd, middle, branch, upstream_in, row_valid, mlp_scale, attn_scale,
+    output, dm_full, hidden_out, mlp_gain, middle_grad, da_full, attn_gain, gate_out, up_out,
     part, recv, rs_send_sem, rs_recv_sem, total, own, ag_send_sem, ag_recv_sem, local_sem,
-    vg, vu, vd, wsem, h_buf, h_sem, gate_buf, up_buf, hidden_buf, out_sem,
+    vg, vu, vd, wsem, in_buf, in_sem, gate_all, up_all, hidden_buf, hidden_sem,
+    row_buf, row_sem, mg_buf, mg_sem, h_buf, h_sem, extra, ready, *plane,
 ):
-    me = lax.axis_index("mp")
+    me, at = lax.axis_index("mp"), lax.axis_index("dp")
     width, hidden_width = wg.shape
-
-    def h_copy(c, j):
+    chips = n_dp // 2
+    part_width = width // n_dp
+
+    def in_copies(phase, c):
+        source = h_full if phase == 0 else dm_full
+        return [
+            pltpu.make_async_copy(
+                source.at[j, chunk_span(c, rows)],
+                in_buf.at[c % 2, pl.ds(j * rows, rows)],
+                in_sem.at[c % 2, j],
+            )
+            for j in range(n)
+        ]
+
+    def start(copies):
+        for copy in copies:
+            copy.start()
+
+    def wait(copies):
+        for copy in copies:
+            copy.wait()
+
+    def row_copy(phase, c):
+        source = middle if phase == 0 else branch
         return pltpu.make_async_copy(
-            h_full.at[j, chunk_span(c, rows)],
-            h_buf.at[c % 2, pl.ds(j * rows, rows)],
-            h_sem.at[c % 2, j],
+            source.at[chunk_span(c, rows)], row_buf.at[c % 2], row_sem.at[c % 2]
         )
 
-    for j in range(n):
-        h_copy(0, j).start()
+    start(in_copies(0, 0))
     gate_tiles = WeightTiles(wg, vg, wsem.at[0], 1, TILE)
     up_tiles = WeightTiles(wu, vu, wsem.at[1], 1, TILE)
     down_tiles = WeightTiles(wd, vd, wsem.at[2], 1, TILE)
@@ -596,31 +620,33 @@
         gate_tiles.copy(tile).start()
         up_tiles.copy(tile).start()
     down_tiles.start()
-    neighbour_barrier(me, n)
-
-    def save_copies(c, j):
-        slot = c % 2
-        span = pl.ds(j * rows, rows)
+    row_copy(0, 0).start()
+    stage_barrier(me, n, at, chips)
+
+    scatter = LineScatter(n, me, rows, part, recv, rs_send_sem, rs_recv_sem)
+    gathers = [
+        make_gather(n, me, rows, own, full, ag_send_sem, ag_recv_sem, local_sem)
+        for full in (dm_full, da_full)
+    ]
+
+    def hidden_copies(c):
         return [
             pltpu.make_async_copy(
-                buf.at[slot, span], out.at[j, chunk_span(c, rows)], out_sem.at[slot, k, j]
+                hidden_buf.at[c % 2, pl.ds(j * rows, rows)],
+                hidden_out.at[j, chunk_span(c, rows)],
+                hidden_sem.at[c % 2, j],
             )
-            for k, (buf, out) in enumerate(
-                ((gate_buf, gate_out), (up_buf, up_out), (hidden_buf, hidden_out))
-            )
+            for j in range(n)
         ]
 
-    def compute(c):
+    def forward(c):
+        here = pl.ds(c * n * rows, n * rows)
         slot = c % 2
-        for j in range(n):
-            h_copy(c, j).wait()
+        wait(in_copies(0, c))
         if c + 1 < CHUNKS:
-            for j in range(n):
-                h_copy(c + 1, j).start()
+            start(in_copies(0, c + 1))
         if c >= 2:
-            for j in range(n):
-                for copy in save_copies(c - 2, j):
-                    copy.wait()
+            wait(hidden_copies(c - 2))
 
         @pl.loop(0, hidden_width // TILE)
         def _(tile):
@@ -628,15 +654,13 @@
                 gate_tiles.copy(tile).wait()
                 up_tiles.copy(tile).wait()
             cols = pl.ds(pl.multiple_of(tile * TILE, TILE), TILE)
-            gate = plain_dot(h_buf[slot], vg[:, cols])
-            up = plain_dot(h_buf[slot], vu[:, cols])
-            gate_buf[slot, :, cols] = gate.astype(BF)
-            up_buf[slot, :, cols] = up.astype(BF)
+            gate = plain_dot(in_buf[slot], vg[:, cols])
+            up = plain_dot(in_buf[slot], vu[:, cols])
+            gate_all[here, cols] = gate.astype(BF)
+            up_all[here, cols] = up.astype(BF)
             hidden_buf[slot, :, cols] = (gate * jax.nn.sigmoid(gate) * up).astype(BF)
 
-        for j in range(n):
-            for copy in save_copies(c, j):
-                copy.start()
+        start(hidden_copies(c))
 
         @pl.loop(0, width // TILE)
         def _(tile):
@@ -645,166 +669,77 @@
             cols = pl.ds(pl.multiple_of(tile * TILE, TILE), TILE)
             part[c, :, cols] = plain_dot(hidden_buf[slot], vd[:, cols]).astype(BF)
 
-    scatter = LineScatter(n, me, rows, part, recv, rs_send_sem, rs_recv_sem)
-    gather = make_gather(n, me, rows, own, dm_full, ag_send_sem, ag_recv_sem, local_sem)
-
-    def row_work(c):
-        scatter.total(c, total)
-        span = chunk_span(c, rows)
-        value = total[...]
-        inverse = inverse_rms(value)
-        output[span] = (middle[span] + value * inverse * scale[...]).astype(BF)
-        upstream = upstream_in[span].astype(F32) * row_valid[span]
-        grad, gain = norm_back(value, inverse, scale[...], upstream)
-        own[c] = grad.astype(BF)
-        gain_out[...] = gain if c == 0 else gain_out[...] + gain
-
-    run_line(n, CHUNKS, STAGGER, compute, scatter, row_work, gather)
-    for c in range(max(CHUNKS - 2, 0), CHUNKS):
-        for j in range(n):
-            for copy in save_copies(c, j):
-                copy.wait()
-
-
-def mlp_forward(n, h_full, wg, wu, wd, middle, out_grad, row_valid, scale):
-    row_count, width = middle.shape
-    hidden_width = wg.shape[1]
-    rows = row_count // CHUNKS
-    saved = jax.ShapeDtypeStruct((n, row_count, hidden_width), BF)
-    most = max(width, hidden_width) // TILE
-    return pl.pallas_call(
-        functools.partial(mlp_forward_kernel, n, rows),
-        out_shape=(
-            jax.ShapeDtypeStruct((row_count, width), BF),
-            jax.ShapeDtypeStruct((n, row_count, width), BF),
-            saved,
-            saved,
-            saved,
-            jax.ShapeDtypeStruct((1, width), F32),
-        ),
-        in_specs=[HBM] * 4 + [VMEM] * 4,
-        out_specs=(VMEM, HBM, HBM, HBM, HBM, VMEM),
-        scratch_shapes=scatter_scratch(n, rows, width)
-        + gather_scratch(n, rows, width)
-        + [
-            pltpu.VMEM(wg.shape, BF),
-            pltpu.VMEM(wu.shape, BF),
-            pltpu.VMEM(wd.shape, BF),
-            pltpu.SemaphoreType.DMA((3, most)),
-            pltpu.VMEM((2, n * rows, width), BF),
-            pltpu.SemaphoreType.DMA((2, n)),
-        ]
-        + [pltpu.VMEM((2, n * rows, hidden_width), BF)] * 3
-        + [pltpu.SemaphoreType.DMA((2, 3, n))],
-        compiler_params=pltpu.CompilerParams(
-            collective_id=2, has_side_effects=True, vmem_limit_bytes=60 * MIB
-        ),
-        name="mlp_forward",
-        cost_estimate=cost(135),
-    )(h_full, wg, wu, wd, middle, out_grad, row_valid, scale)
-
-
-def mlp_backward_kernel(
-    n, n_dp, rows, dm_full, h_full, wg, wu, wd, gate_in, up_in, branch, upstream_in, row_valid,
-    scale,
-    middle_grad, da_full, gain_out, gate_out, up_out,
-    part, recv, rs_send_sem, rs_recv_sem, total, own, ag_send_sem, ag_recv_sem, local_sem,
-    vg, vu, vd, wsem, dm_buf, gate_buf, up_buf, in_sem, dgate, dup, mg_buf, mg_sem,
-    h_buf, h_sem, extra, ready, *plane,
-):
-    me, at = lax.axis_index("mp"), lax.axis_index("dp")
-    width, hidden_width = wg.shape
-    chips = n_dp // 2
-    part_width = width // n_dp
-    size = n * rows * CHUNKS
-
-    def in_copies(c, j):
-        span = pl.ds(j * rows, rows)
-        return [
-            pltpu.make_async_copy(
-                source.at[j, chunk_span(c, rows)], buf.at[span], in_sem.at[k, j]
-            )
-            for k, (source, buf) in enumerate(
-                ((dm_full, dm_buf), (gate_in, gate_buf), (up_in, up_buf))
-            )
-        ]
-
-    for j in range(n):
-        for copy in in_copies(0, j):
-            copy.start()
-    down_tiles = WeightTiles(wd, vd, wsem.at[0], 0, TILE)
-    gate_tiles = WeightTiles(wg, vg, wsem.at[1], 0, TILE)
-    up_tiles = WeightTiles(wu, vu, wsem.at[2], 0, TILE)
-    down_tiles.start()
-    for tile in range(gate_tiles.count):
-        gate_tiles.copy(tile).start()
-        up_tiles.copy(tile).start()
-    stage_barrier(me, n, at, chips)
-
-    def compute(c):
+    def backward(c):
         here = pl.ds(c * n * rows, n * rows)
-        for j in range(n):
-            for copy in in_copies(c, j):
-                copy.wait()
+        scatter.drain(c)
+        gathers[0].drain_sends(c)
+        wait(in_copies(1, c))
 
         @pl.loop(0, hidden_width // TILE)
         def _(tile):
-            if c == 0:
-                down_tiles.copy(tile).wait()
             cols = pl.ds(pl.multiple_of(tile * TILE, TILE), TILE)
-            hidden_grad = outer_dot(dm_buf[...], vd[cols, :])
-            gate = gate_buf[:, cols].astype(F32)
-            up = up_buf[:, cols].astype(F32)
+            hidden_grad = outer_dot(in_buf[c % 2], vd[cols, :])
+            gate = gate_all[here, cols].astype(F32)
+            up = up_all[here, cols].astype(F32)
             sigmoid = jax.nn.sigmoid(gate)
-            dgate[here, cols] = (
+            gate_all[here, cols] = (
                 hidden_grad * up * sigmoid * (1.0 + gate * (1.0 - sigmoid))
             ).astype(BF)
-            dup[here, cols] = (hidden_grad * gate * sigmoid).astype(BF)
-
-        if c + 1 < CHUNKS:
-            for j in range(n):
-                for copy in in_copies(c + 1, j):
-                    copy.start()
+            up_all[here, cols] = (hidden_grad * gate * sigmoid).astype(BF)
 
         @pl.loop(0, width // TILE)
         def _(tile):
-            if c == 0:
-                gate_tiles.copy(tile).wait()
-                up_tiles.copy(tile).wait()
             cols = pl.ds(pl.multiple_of(tile * TILE, TILE), TILE)
             part[c, :, cols] = (
-                outer_dot(dgate[here], vg[cols, :]) + outer_dot(dup[here], vu[cols, :])
+                outer_dot(gate_all[here], vg[cols, :]) + outer_dot(up_all[here], vu[cols, :])
             ).astype(BF)
 
         if c + 1 == CHUNKS:
-            for copy in h_copies(0):
-                copy.start()
+            start(h_copies(0))
             signal_partners(ready, at, chips)
-
-    scatter = LineScatter(n, me, rows, part, recv, rs_send_sem, rs_recv_sem)
-    gather = make_gather(n, me, rows, own, da_full, ag_send_sem, ag_recv_sem, local_sem)
 
     def mg_copy(c):
         return pltpu.make_async_copy(
             mg_buf.at[c % 2], middle_grad.at[chunk_span(c, rows)], mg_sem.at[c % 2]
         )
 
-    def row_work(c):
+    def next_row_copy(phase, c):
+        if c + 1 < CHUNKS:
+            row_copy(phase, c + 1).start()
+        elif phase == 0:
+            row_copy(1, 0).start()
+
+    def forward_rows(c):
         scatter.total(c, total)
         span = chunk_span(c, rows)
+        row_copy(0, c).wait()
+        next_row_copy(0, c)
+        value = total[...]
+        inverse = inverse_rms(value)
+        output[span] = (row_buf[c % 2] + value * inverse * mlp_scale[...]).astype(BF)
+        upstream = upstream_in[span].astype(F32) * row_valid[span]
+        grad, gain = norm_back(value, inverse, mlp_scale[...], upstream)
+        own[c] = grad.astype(BF)
+        mlp_gain[...] = gain if c == 0 else mlp_gain[...] + gain
+
+    def backward_rows(c):
+        scatter.total(c, total)
+        span = chunk_span(c, rows)
+        row_copy(1, c).wait()
+        next_row_copy(1, c)
         upstream = upstream_in[span].astype(F32) * row_valid[span] + total[...]
         if c >= 2:
             mg_copy(c - 2).wait()
         mg_buf[c % 2] = upstream
         mg_copy(c).start()
-        value = branch[span]
-        grad, gain = norm_back(value, inverse_rms(value), scale[...], upstream)
+        value = row_buf[c % 2]
+        grad, gain = norm_back(value, inverse_rms(value), attn_scale[...], upstream)
         own[c] = grad.astype(BF)
-        gain_out[...] = gain if c == 0 else gain_out[...] + gain
+        attn_gain[...] = gain if c == 0 else attn_gain[...] + gain
 
     block_width = pl.ds(0, hidden_width)
 
-    def slot(index):
+    def slot_at(index):
         for ref in (vg, vu, vd):
             count = ref.shape[0] // part_width
             if index < count:
@@ -812,15 +747,14 @@
             index -= count
         return extra.at[index]
 
-    base = [chips, chips + 3 * chips]
     reduces = []
     for which, out in enumerate((gate_out, up_out)):
-        first = base[which]
+        first = chips + 3 * chips * which
         views = (
-            lambda r: slot(r),
-            lambda r, first=first: slot(first + r),
-            lambda r, first=first: slot(first + chips + r),
-            lambda r, first=first: slot(first + 2 * chips + r - 1),
+            lambda r: slot_at(r),
+            lambda r, first=first: slot_at(first + r),
+            lambda r, first=first: slot_at(first + chips + r),
+            lambda r, first=first: slot_at(first + 2 * chips + r - 1),
         )
         reduces.append(
             PlaneReduce(at, chips, part_width, views, plane[4 * which : 4 * which + 4], out)
@@ -839,9 +773,7 @@
         cols = pl.ds(pl.multiple_of(first, part_width), part_width)
         return [
             pltpu.make_async_copy(
-                h_full.at[j, :, cols],
-                h_buf.at[index % 2, j],
-                h_sem.at[index % 2, j],
+                h_full.at[j, :, cols], h_buf.at[index % 2, j], h_sem.at[index % 2, j]
             )
             for j in range(n)
         ]
@@ -849,14 +781,12 @@
     def weight_block(index):
         which, same_core, r = jobs[index]
         reduce = reduces[which]
-        grad = (dgate, dup)[which]
+        grad = (gate_all, up_all)[which]
         if index == 0:
             pl.semaphore_wait(ready, 1 + len(bits_of(chips - 1)))
-        for copy in h_copies(index):
-            copy.wait()
+        wait(h_copies(index))
         if index + 1 < len(jobs):
-            for copy in h_copies(index + 1):
-                copy.start()
+            start(h_copies(index + 1))
         if same_core:
             reduce.core_copy(r).wait_recv()
         elif which == 1:
@@ -885,31 +815,58 @@
 
         if not same_core:
             reduce.core_copy(r).start()
+        elif r > 0:
+            for half in range(2):
+                if not reduce.before(r, half):
+                    reduce.push(r, half)
 
     work = []
     for index, (which, same_core, r) in enumerate(jobs):
-        work.append(lambda index=index: weight_block(index))
-        if same_core and r > 0:
-            for half in range(2):
-                if not reduces[which].before(r, half):
-                    work.append(lambda w=which, r=r, half=half: reduces[w].push(r, half))
-                    work[-2:] = [lambda f=work[-2], g=work[-1]: (f(), g())]
+        work.append(functools.partial(weight_block, index))
         if same_core and r == order[-1]:
             for late in order:
                 for half in range(2):
                     if late > 0 and reduces[which].before(late, half):
-                        work.append(lambda w=which, r=late, half=half: reduces[w].push(r, half))
+                        work.append(functools.partial(reduces[which].push, late, half))
     pending = iter(work)
 
-    def filler():
-        for _ in range(FILL):
-            job = next(pending, None)
-            if job is not None:
-                job()
-
-    run_line(n, CHUNKS, STAGGER, compute, scatter, row_work, gather, filler)
+    last_step = 2 * n - 2
+    events = sorted(
+        (max(PERIOD, last_step + 1) * phase + step + STAGGER * c - (0.5 if step == 0 else 0), phase, c, step)
+        for phase in range(2)
+        for c in range(CHUNKS)
+        for step in range(last_step + 1)
+    )
+    filling = False
+    for _, phase, c, step in events:
+        gather = gathers[phase]
+        if step == 0:
+            (forward, backward)[phase](c)
+            filling = filling or (phase == 1 and c + 1 == CHUNKS)
+        if step < n - 1:
+            scatter.edge(c, step)
+            if step > 0:
+                scatter.step(c, step)
+        elif step == n - 1:
+            (forward_rows, backward_rows)[phase](c)
+            gather.step(c, 1)
+        elif step < last_step:
+            gather.step(c, step - n + 2)
+        else:
+            gather.last(c)
+            if phase == 0:
+                gather.local_copy(c).wait()
+                start(in_copies(1, c))
+        if filling:
+            for _ in range(FILL):
+                job = next(pending, None)
+                if job is not None:
+                    job()
     for job in pending:
         job()
+    for c in range(CHUNKS):
+        scatter.drain(c)
+        gathers[1].drain(c)
     for reduce in reduces:
         reduce.finish()
         reduce.drain()
@@ -917,9 +874,10 @@
         reduces[1].drain_core(r)
     for c in range(max(CHUNKS - 2, 0), CHUNKS):
         mg_copy(c).wait()
-
-
-def mlp_backward(n, n_dp, dm_full, h_full, wg, wu, wd, gate, up, branch, out_grad, row_valid, scale):
+        wait(hidden_copies(c))
+
+
+def mlp(n, n_dp, h_full, wg, wu, wd, middle, branch, out_grad, row_valid, mlp_scale, attn_scale):
     row_count, width = branch.shape
     hidden_width = wg.shape[1]
     rows = row_count // CHUNKS
@@ -929,18 +887,22 @@
     block = (part_width, hidden_width)
     most = max(width, hidden_width) // TILE
     slots = (2 * width + hidden_width) // part_width
-    extra = max(7 * chips - 1 - slots, 1)
+    extra = 7 * chips - 1 - slots
     return pl.pallas_call(
-        functools.partial(mlp_backward_kernel, n, n_dp, rows),
+        functools.partial(mlp_kernel, n, n_dp, rows),
         out_shape=(
+            jax.ShapeDtypeStruct((row_count, width), BF),
+            jax.ShapeDtypeStruct((n, row_count, width), BF),
+            jax.ShapeDtypeStruct((n, row_count, hidden_width), BF),
+            jax.ShapeDtypeStruct((1, width), F32),
             jax.ShapeDtypeStruct((row_count, width), F32),
             jax.ShapeDtypeStruct((n, row_count, width), BF),
             jax.ShapeDtypeStruct((1, width), F32),
             jax.ShapeDtypeStruct(block, F32),
             jax.ShapeDtypeStruct(block, F32),
         ),
-        in_specs=[HBM] * 7 + [VMEM] * 4,
-        out_specs=(HBM, HBM, VMEM, VMEM, VMEM),
+        in_specs=[HBM] * 6 + [VMEM] * 4,
+        out_specs=(VMEM, HBM, HBM, VMEM, HBM, HBM, VMEM, VMEM, VMEM),
         scratch_shapes=scatter_scratch(n, rows, width)
         + gather_scratch(n, rows, width)
         + [
@@ -948,27 +910,28 @@
             pltpu.VMEM(wu.shape, BF),
             pltpu.VMEM(wd.shape, BF),
             pltpu.SemaphoreType.DMA((3, most)),
-            pltpu.VMEM((n * rows, width), BF),
-            pltpu.VMEM((n * rows, hidden_width), BF),
-            pltpu.VMEM((n * rows, hidden_width), BF),
-            pltpu.SemaphoreType.DMA((3, n)),
-        ]
-        + [pltpu.VMEM((size, hidden_width), BF)] * 2
-        + [
+            pltpu.VMEM((2, n * rows, width), BF),
+            pltpu.SemaphoreType.DMA((2, n)),
+            pltpu.VMEM((size, hidden_width), BF),
+            pltpu.VMEM((size, hidden_width), BF),
+            pltpu.VMEM((2, n * rows, hidden_width), BF),
+            pltpu.SemaphoreType.DMA((2, n)),
+            pltpu.VMEM((2, rows, width), F32),
+            pltpu.SemaphoreType.DMA((2,)),
             pltpu.VMEM((2, rows, width), F32),
             pltpu.SemaphoreType.DMA((2,)),
             pltpu.VMEM((2, n, row_count, part_width), BF),
             pltpu.SemaphoreType.DMA((2, n)),
-            pltpu.VMEM((extra,) + block, BF),
+            pltpu.VMEM((extra,) + block if extra > 0 else (1, 16, 128), BF),
             pltpu.SemaphoreType.REGULAR,
         ]
         + plane_sems(chips) * 2,
         compiler_params=pltpu.CompilerParams(
-            collective_id=3, has_side_effects=True, vmem_limit_bytes=63 * MIB
+            collective_id=2, has_side_effects=True, vmem_limit_bytes=63 * MIB
         ),
-        name="mlp_backward",
-        cost_estimate=cost(145),
-    )(dm_full, h_full, wg, wu, wd, gate, up, branch, out_grad, row_valid, scale)
+        name="mlp",
+        cost_estimate=cost(260),
+    )(h_full, wg, wu, wd, middle, branch, out_grad, row_valid, mlp_scale, attn_scale)
 
 
 def last_grads_kernel(
@@ -1444,25 +1407,21 @@
         n, local_heads, model_width, qkv_raw, query_scale, key_scale, cos_table, sin_table, starts
     )
     branch, middle, middle_full = attn_out(n, attended, full_out, layer_input, attn_scale)
-    layer_output, mlp_grad_full, gate, up, hidden, mlp_gain_part = mlp_forward(
-        n, middle_full, full_gate, full_up, full_down, middle, out_grad, row_valid, mlp_scale
+    (
+        layer_output, mlp_grad_full, hidden, mlp_gain_part, middle_grad, branch_full,
+        attn_gain_part, grad_gate, grad_up,
+    ) = mlp(
+        n, n_dp, middle_full, full_gate, full_up, full_down, middle, branch, out_grad, row_valid,
+        mlp_scale, attn_scale,
     )
 
     def flat(rows):
         return rows.reshape(group_size, rows.shape[-1])
 
-    def dp_scatter(part, dimension):
-        return lax.psum_scatter(part, "dp", scatter_dimension=dimension, tiled=True)
-
+    branch_full = flat(branch_full)
     down_part = inner_dot(flat(hidden), flat(mlp_grad_full)).astype(BF)
-    mlp_grad_full, down_part = lax.optimization_barrier((mlp_grad_full, down_part))
-    grad_down = dp_scatter(down_part, 1)
-    middle_grad, branch_full, attn_gain_part, grad_gate, grad_up = mlp_backward(
-        n, n_dp, mlp_grad_full, middle_full, full_gate, full_up, full_down, gate, up, branch,
-        out_grad, row_valid, attn_scale,
-    )
-    branch_full = flat(branch_full)
-    branch_full, grad_down = lax.optimization_barrier((branch_full, grad_down))
+    branch_full, down_part = lax.optimization_barrier((branch_full, down_part))
+    grad_down = lax.psum_scatter(down_part, "dp", scatter_dimension=1, tiled=True)
 
     mixed_grad = outer_dot(branch_full, full_out).astype(BF)
     qkv_grad, query_gain_part, key_gain_part = attention_back(

time: 730 us -> 688 us (0.942)
  Pallas kernels: 635 us -> 592 us
    pallas_call x2 -> x1, Pallas kernels: 301 us -> 255 us  [mlp(): pl.pallas_call(functools.partial(mlp_kernel, n, n_dp, rows), out_shape=(j...]
  transfers between devices with their start and end apart: 6 -> 6, of which waited for: 1 -> 1; matrix products, arithmetic and copies ran while one was open for 4% -> 6% of each run, Pallas kernels for 53% -> 50%
where the time goes in v4:
time: 688 us; the launch traced here: 679 us
  Pallas kernels  592 us (86%)
  matrix products  31.4 us (5%)
  local copies, waits for them, and re-layouts  21 us (3%)
  between operations  14.8 us (2%)
  other arithmetic  14.5 us (2%)
    pallas_call x1, Pallas kernels, mlp(): pl.pallas_call(functools.partial(mlp_kernel, n, n_dp, rows), out_shape=(j...  255 us
    pallas_call x1, Pallas kernels, attn_out(): pl.pallas_call(functools.partial(attn_out_kernel, n, rows), out_shape=(ja...  118 us
    pallas_call x1, Pallas kernels, last_grads(): pl.pallas_call(functools.partial(last_grads_kernel, n, n_dp, rows), out_s...  86 us
    pallas_call x1, Pallas kernels, gather_rows(): pl.pallas_call(functools.partial(gather_rows_kernel, n, n_dp, rows), out_...  76.1 us
    pallas_call x1, Pallas kernels, attention_back(): pl.pallas_call(functools.partial(attention_back_kernel, n, heads, model_w...  30.1 us
    pallas_call x1, Pallas kernels, attention(): pl.pallas_call(functools.partial(attention_kernel, n, heads, model_width)...  26.8 us
    dot_general x1, matrix products, inner_dot(): lax.dot_general(former, latter, (((0,), (0,)), ((), ())), preferred_eleme...  14.1 us
  transfers between devices with their start and end apart: 6, of which 1 were waited for; matrix products, arithmetic and copies ran while one was open for 6% of the time, Pallas kernels for 50%

profile of v4, /device:TPU:0, one launch (start us, length us, event | category | flops | bytes accessed | tf_op | source)
XLA Modules:
  0.0 678.9 jit_solution(15572519510519761554)
XLA Ops:
  7.3 2.0 pad_maximum_fusion
  13.7 76.1 %gather_rows.1 = (bf16[4,256,2048]{2,1,0:T(8,128)(2,1)}, f32[8,1,640]{2,1,0:T(1,128)}) custom-call(bf16[256,2048]{1,0:T(8,128)(2,1)} %x.1, f32[1,640]{1,0:T(1,128)} %maximum_convert_fusion.gains), custom_call_target="tpu_custom_call" | custom-call | flops 74999996416 | bytes 225000000 | tf_op jit(solution)/shard_map/gather_rows/pallas_call | solution.py:480
  92.1 1.0 copy.42.starts
  96.7 1.9 fusion
  98.7 1.3 pad_maximum_fusion.1
  100.0 11.7 %fusion.7.qkv = f32[1024,1536]{1,0:T(8,128)} fusion(bf16[1024,2048]{1,0:T(8,128)(2,1)} %bitcast.61, bf16[2048,1536]{1,0:T(8,128)(2,1)} %all-gather.6.cloned.1.call-done.weight), kind=kOutput, calls=%fused_computation.33 | convolution fusion | flops 6442450944 | bytes 16777216 | tf_op jit(solution)/shard_map/dot_general | solution.py:35
  111.7 26.8 %attention.1 = (bf16[1024,512]{1,0:T(8,128)(2,1)}, bf16[1024,512]{1,0:T(8,128)(2,1)}, bf16[1024,512]{1,0:T(8,128)(2,1)}, bf16[1024,512]{1,0:T(8,128)(2,1)}, f32[...) custom-call(f32[1024,1536]{1,0:T(8,128)} %fusion.7.qkv, f32[1,512]{1,0:T(1,128)} %reshape.193.q_gain, ...), custom_call_target="tpu_custom_call" | custom-call | flops 24999999488 | bytes 75000000 | tf_op jit(solution)/shard_map/attention/pallas_call | solution.py:1241
  138.5 118.3 %attn_out.1 = (f32[256,2048]{1,0:T(8,128)}, f32[256,2048]{1,0:T(8,128)}, bf16[4,256,2048]{2,1,0:T(8,128)(2,1)}) custom-call(bf16[1024,512]{1,0:T(8,128)(2,1)} %get-tuple-element.45.att, bf16[512,2048]{1,0:T(8,128)(2,1)} %all-gather.8.cloned.1.call-done.wo, bf16[256,2048]{1,0:T(8,128)(2,1)} %x.1, f32[1,2048]{1,0:T(1,128)} %bitcast.53), custom_call_target="tpu_custom_call" | custom-call | flops 115000000512 | bytes 345000000 | tf_op jit(solution)/shard_map/attn_out/pallas_call | solution.py:539
  256.8 2.2 all-gather.14.cloned.1.call-done.wd
  259.1 255.1 %mlp.1 = (bf16[256,2048]{1,0:T(8,128)(2,1)}, bf16[4,256,2048]{2,1,0:T(8,128)(2,1)}, bf16[4,256,2048]{2,1,0:T(8,128)(2,1)}, f32[1,2048]{1,0:T(1,128)}, f32[256,20...) custom-call(bf16[4,256,2048]{2,1,0:T(8,128)(2,1)} %get-tuple-element, ...), custom_call_target="tpu_custom_call" | custom-call | flops 260000006144 | bytes 780000000 | tf_op jit(solution)/shard_map/mlp/pallas_call | solution.py:891
  514.2 14.1 %bitcast_convert_fusion = bf16[2048,2048]{1,0:T(8,128)(2,1)} fusion(bf16[4,256,2048]{2,1,0:T(8,128)(2,1)} %get-tuple-element.54, bf16[4,256,2048]{2,1,0:T(8,128)(2,1)} %get-tuple-element.55), kind=kOutput, calls=%fused_computation | convolution fusion | flops 8594128896 | bytes 16777216 | tf_op jit(solution)/shard_map/dot_general | solution.py:39
  528.3 1.6 copy-done.7
  529.9 5.5 convolution_convert_fusion.out_grad
  535.4 30.1 %attention_back.1 = (bf16[1024,1536]{1,0:T(8,128)(2,1)}, f32[1,512]{1,0:T(1,128)}, f32[1,512]{1,0:T(1,128)}) custom-call(f32[1024,1536]{1,0:T(8,128)} %fusion.7.qkv, bf16[1024,512]{1,0:T(8,128)(2,1)} %get-tuple-element.50.q_low, bf16[1024,512]{1,0:T(8,128)(2,1)} %get-tuple-element.51.k_low, bf16[1024,512]{1,0:T(8,128)(2,1)} %get-tuple-element.52.v_low, ...), custom_call_target="tpu_custom_call" | custom-call | flops 30000001024 | bytes 90000000 | tf_op jit(solution)/shard_map/attention_back/pallas_call | solution.py:1330
  566.0 1.3 reduce.21
  567.5 1.3 reduce.20
  571.1 86.0 %last_grads.1 = (f32[256,2048]{1,0:T(8,128)}, f32[256,1536]{1,0:T(8,128)}, f32[512,256]{1,0:T(8,128)}, f32[1,640]{1,0:T(1,128)}) custom-call(bf16[1024,1536]{1,0:T(8,128)(2,1)} %get-tuple-element.60.grads, bf16[2048,1536]{1,0:T(8,128)(2,1)} %all-gather.6.cloned.1.call-done.weight, f32[256,2048]{1,0:T(8,128)} %get-tuple-element.61.base, ...), custom_call_target="tpu_custom_call" | custom-call | flops 80000000000 | bytes 240000000 | tf_op jit(solution)/shard_map/last_grads/pallas_call | solution.py:1110
  659.2 1.2 fusion.6
  660.5 2.7 fusion.4
  663.2 2.8 convert_element_type.37
  665.9 1.0 copy.67
  666.9 1.3 copy.68
  669.0 1.3 copy.70
  670.4 1.3 copy.71
  (85 shorter events, 16.1 us)
Async XLA Ops:
  7.2 4.9 copy-start.10
  7.2 5.6 copy-start.11
  7.2 5.6 copy-start.12
  7.2 5.7 copy-start.8
  7.2 5.7 copy-start.9
  7.2 92.7 %all-gather.6.cloned.1.call-start = ((), (), s32[]{:S(2)}) async-start(), calls=%async_computation.1 | async-start | bytes 7077888 | tf_op jit(solution)/shard_map/all_gather | solution.py:1375
  9.3 129.2 %all-gather.8.cloned.1.call-start = ((), (), s32[]{:S(2)}) async-start(), calls=%async_computation.2 | async-start | bytes 2359296 | tf_op jit(solution)/shard_map/all_gather | solution.py:1378
  10.1 246.7 %all-gather.10.cloned.1.call-start = ((), (), s32[]{:S(2)}) async-start(), calls=%async_computation.3 | async-start | bytes 9437184 | tf_op jit(solution)/shard_map/all_gather | solution.py:1379
  10.8 246.0 %all-gather.12.cloned.1.call-start = ((), (), s32[]{:S(2)}) async-start(), calls=%async_computation.4 | async-start | bytes 9437184 | tf_op jit(solution)/shard_map/all_gather | solution.py:1380
  11.4 247.7 %all-gather.14.cloned.1.call-start = ((), (), s32[]{:S(2)}) async-start(), calls=%async_computation.5 | async-start | bytes 9437184 | tf_op jit(solution)/shard_map/all_gather | solution.py:1381
  12.0 651.2 %reduce-scatter.2.cloned.1.call-start = ((), (), s32[]{:S(2)}) async-start(), calls=%async_computation.6 | async-start | bytes 9437184 | tf_op jit(solution)/shard_map/reduce_scatter | solution.py:1424
  528.3 1.6 copy-start.7
  535.4 33.6 %copy-start.6 = (f32[1,2048]{1,0:T(1,128)S(1)}, f32[1,2048]{1,0:T(1,128)}, u32[]{:S(2)}) copy-start(f32[1,2048]{1,0:T(1,128)} %get-tuple-element.62) | copy-start | bytes 24580
  535.4 34.3 %copy-start.5 = (f32[1,2048]{1,0:T(1,128)S(1)}, f32[1,2048]{1,0:T(1,128)}, u32[]{:S(2)}) copy-start(f32[1,2048]{1,0:T(1,128)} %get-tuple-element.63) | copy-start | bytes 24580
  657.1 8.8 %copy-start.3 = (bf16[256,2048]{1,0:T(8,128)(2,1)S(1)}, bf16[256,2048]{1,0:T(8,128)(2,1)}, u32[]{:S(2)}) copy-start(bf16[256,2048]{1,0:T(8,128)(2,1)} %get-tuple-element.104) | copy-start | bytes 3145732
  660.5 6.4 copy-start.2
  663.2 5.1 copy-start.4
  665.9 3.1 copy-start.1
  666.9 3.4 copy-start
Sparse Core Ops, SparseCore 0:
  10.5 48.2 all-gather.5
  60.7 28.1 all-gather.7
  90.8 54.3 all-gather.9
  146.9 54.3 all-gather.11
  203.1 55.9 all-gather.13
  528.4 70.2 reduce-scatter.1

commit v5 on v4

--- a/solution.py
+++ b/solution.py
@@ -437,16 +437,89 @@
     return [copy(shift) for shift in range(1, size)]
 
 
-def gather_rows_kernel(
-    n, n_dp, rows, block, gains, full, gain_parts,
+class PlaneGather:
+    def __init__(self, at, chips, rows, slot, sems):
+        self.chip, self.core = at // 2, lax.rem(at, 2)
+        self.chips, self.rows, self.slot = chips, rows, slot
+        self.core_send_sem, self.core_recv_sem, self.send_sem, self.recv_sem = sems
+        self.arrived = set()
+
+    def last_bit(self, relative, half):
+        bits = bits_of(relative)
+        return bits[-1] if half == 0 else bits[0]
+
+    def place(self, relative, same_core=True):
+        return self.slot(
+            2 * relative_chip(self.chip, relative) + (self.core if same_core else 1 - self.core)
+        )
+
+    def copy(self, relative, half):
+        bit = self.last_bit(relative, half)
+        view = self.place(relative - bit).at[pl.ds(half * (self.rows // 2), self.rows // 2)]
+        return pltpu.make_async_remote_copy(
+            src_ref=view,
+            dst_ref=view,
+            send_sem=self.send_sem.at[relative, half],
+            recv_sem=self.recv_sem.at[relative, half],
+            device_id={"dp": 2 * flipped(self.chip, bit) + self.core},
+        )
+
+    def core_copy(self, relative, same_core):
+        view = self.place(relative, same_core)
+        return pltpu.make_async_remote_copy(
+            src_ref=view,
+            dst_ref=view,
+            send_sem=self.core_send_sem.at[relative],
+            recv_sem=self.core_recv_sem.at[relative],
+            device_id={"dp": 2 * self.chip + 1 - self.core},
+        )
+
+    def ensure(self, relative, half):
+        if relative > 0 and (relative, half) not in self.arrived:
+            self.arrived.add((relative, half))
+            self.copy(relative, half).wait_recv()
+
+    def send(self, passed_on):
+        for count in range(1, self.chips.bit_length()):
+            for r in range(1, self.chips):
+                for half in range(2):
+                    if len(bits_of(r)) == count and (count > 1) == passed_on:
+                        self.ensure(r - self.last_bit(r, half), half)
+                        self.copy(r, half).start()
+        if not passed_on:
+            self.core_copy(0, True).start()
+
+    def swap(self, relatives):
+        for r in relatives:
+            for half in range(2):
+                self.ensure(r, half)
+            self.core_copy(r, True).start()
+
+    def finish(self):
+        for r in range(self.chips):
+            self.core_copy(r, False).wait_recv()
+
+    def drain(self):
+        for r in range(self.chips):
+            self.core_copy(r, True).wait_send()
+            for half in range(2):
+                if r > 0:
+                    self.copy(r, half).wait_send()
+
+
+def front_kernel(
+    n, n_dp, rows, model_width, x, wq, wk, wv, wo, gains,
+    full, qkv, full_qkv, full_out, gain_parts, q_inv, k_inv,
     send_sem, recv_sem, local_sem, gain_recv, gain_send_sem, gain_recv_sem,
+    vqkv, vout, save_sem, x_buf, x_sem, squares,
+    held, sum_recv, turned, sum_send_sem, sum_recv_sem, *plane,
 ):
     me, at = lax.axis_index("mp"), lax.axis_index("dp")
     peer_barrier((("mp", me, n), ("dp", at, n_dp)))()
     gather = LineGather(
         n,
         me,
-        lambda c: block.at[chunk_span(c, rows)],
+        lambda c: x.at[chunk_span(c, rows)],
         lambda index, c: full.at[index, chunk_span(c, rows)],
         send_sem,
         recv_sem,
@@ -454,47 +527,151 @@
     )
     for c in range(CHUNKS):
         gather.step(c, 1)
+    chips = n_dp // 2
+    part_width, width = wq.shape
+    row_count = rows * CHUNKS
+
+    def part(owner):
+        return pl.ds(pl.multiple_of(owner * part_width, part_width), part_width)
+
+    by_qkv = PlaneGather(at, chips, part_width, lambda owner: vqkv.at[part(owner)], plane[:4])
+    by_out = PlaneGather(at, chips, width, lambda owner: vout.at[:, part(owner)], plane[4:])
+    for k, weight in enumerate((wq, wk, wv)):
+        vqkv[part(at), k * width : (k + 1) * width] = weight[...]
+    by_qkv.send(False)
+    vout[:, part(at)] = wo[...]
+    by_out.send(False)
     copies = exchange(
         "dp", at, n_dp, lambda peer: gains, gain_recv, gain_send_sem, gain_recv_sem
     )
     for copy in copies:
         copy.start()
+
+    def block(index, source):
+        load = pltpu.make_async_copy(source, x_buf, x_sem)
+        load.start()
+        load.wait()
+        here = pl.ds(pl.multiple_of(index * row_count, row_count), row_count)
+
+        @pl.loop(0, 3)
+        def _(tile):
+            cols = pl.ds(pl.multiple_of(tile * width, width), width)
+            value = plain_dot(x_buf[...], vqkv[:, cols])
+            qkv[here, cols] = value
+            squares[tile] = jnp.sum(value * value, axis=1, keepdims=True)
+
+        held[:, here] = columns_to_rows(squares[0], squares[1])
+
+    def blocks_at(step):
+        @pl.loop(0, 2)
+        def _(side):
+            index = me - step + 2 * step * side
+
+            @pl.when((index >= 0) & (index < n))
+            def _():
+                block(index, full.at[index])
+
+    saves = [
+        pltpu.make_async_copy(vqkv, full_qkv, save_sem.at[0]),
+        pltpu.make_async_copy(vout, full_out, save_sem.at[1]),
+    ]
+    early = [r for r in range(1, chips) if len(bits_of(r)) == 1]
+    late = [r for r in range(1, chips) if len(bits_of(r)) > 1]
+
+    def weights_here():
+        by_qkv.finish()
+        saves[0].start()
+        block(me, x)
+
+    hooks = [
+        lambda: by_qkv.send(True),
+        None,
+        None,
+        lambda: by_qkv.swap(early),
+        lambda: (by_qkv.swap(late), by_out.send(True)),
+        lambda: by_out.swap(early + late),
+        weights_here,
+    ]
+    ready = 1
     for step in range(2, n):
         for c in range(CHUNKS):
             gather.step(c, step)
+            if hooks:
+                hook = hooks.pop(0)
+                if hook is not None:
+                    hook()
+        if not hooks:
+            while ready < step:
+                blocks_at(ready)
+                ready += 1
+    for hook in hooks:
+        if hook is not None:
+            hook()
+    while ready < n - 1:
+        blocks_at(ready)
+        ready += 1
     gain_parts[at] = gains[...]
     for shift, copy in enumerate(copies, 1):
         copy.wait_recv()
         gain_parts[lax.rem(at + n_dp - shift, n_dp)] = gain_recv[shift - 1]
+    by_out.finish()
+    saves[1].start()
     for c in range(CHUNKS):
         gather.last(c)
+    blocks_at(n - 1)
+    q_sum, k_sum = sum_held(n, me, held, sum_recv, turned, sum_send_sem, sum_recv_sem)
+    q_inv[...] = lax.rsqrt(q_sum / model_width + EPS)
+    k_inv[...] = lax.rsqrt(k_sum / model_width + EPS)
     for c in range(CHUNKS):
         gather.drain(c)
     for copy in copies:
         copy.wait_send()
-
-
-def gather_rows(n, n_dp, block, gains):
-    rows = block.shape[0] // CHUNKS
-    sems = gather_scratch(n, rows, block.shape[1])[1:]
+    for gathered in (by_qkv, by_out):
+        gathered.drain()
+    for copy in saves:
+        copy.wait()
+
+
+def front(n, n_dp, block, wq, wk, wv, wo, gains):
+    row_count, model_width = block.shape
+    rows = row_count // CHUNKS
+    size = n * row_count
+    width = wq.shape[1]
+    chips = n_dp // 2
+    column = jax.ShapeDtypeStruct((size, 1), F32)
     return pl.pallas_call(
-        functools.partial(gather_rows_kernel, n, n_dp, rows),
+        functools.partial(front_kernel, n, n_dp, rows, model_width),
         out_shape=(
             jax.ShapeDtypeStruct((n,) + block.shape, block.dtype),
+            jax.ShapeDtypeStruct((size, 3 * width), F32),
+            jax.ShapeDtypeStruct((model_width, 3 * width), BF),
+            jax.ShapeDtypeStruct((width, model_width), BF),
             jax.ShapeDtypeStruct((n_dp,) + gains.shape, F32),
+            column,
+            column,
         ),
-        in_specs=[HBM, VMEM],
-        out_specs=(HBM, VMEM),
-        scratch_shapes=sems
+        in_specs=[HBM] + [VMEM] * 5,
+        out_specs=(HBM, VMEM, HBM, HBM, VMEM, VMEM, VMEM),
+        scratch_shapes=gather_scratch(n, rows, model_width)[1:]
         + [
             pltpu.VMEM((n_dp - 1,) + gains.shape, F32),
             pltpu.SemaphoreType.DMA((n_dp - 1,)),
             pltpu.SemaphoreType.DMA((n_dp - 1,)),
-        ],
-        compiler_params=pltpu.CompilerParams(collective_id=0, has_side_effects=True),
-        name="gather_rows",
-        cost_estimate=cost(75),
-    )(block, gains)
+            pltpu.VMEM((model_width, 3 * width), BF),
+            pltpu.VMEM((width, model_width), BF),
+            pltpu.SemaphoreType.DMA((2,)),
+            pltpu.VMEM((row_count, model_width), BF),
+            pltpu.SemaphoreType.DMA,
+            pltpu.VMEM((3, row_count, 1), F32),
+        ]
+        + sum_scratch(n, size)
+        + plane_sems(chips) * 2,
+        compiler_params=pltpu.CompilerParams(
+            collective_id=0, has_side_effects=True, vmem_limit_bytes=48 * MIB
+        ),
+        name="front",
+        cost_estimate=cost(80),
+    )(block, wq, wk, wv, wo, gains)
 
 
 def attn_out_kernel(
@@ -1161,10 +1338,8 @@
     return jnp.transpose(jnp.where(lanes == 0, first, second))[:8]
 
 
-def sum_columns(n, me, first, second, entered, held, recv, turned, send_sem, recv_sem):
-    held[...] = columns_to_rows(first, second)
+def sum_held(n, me, held, recv, turned, send_sem, recv_sem):
     copies = exchange("mp", me, n, lambda peer: held, recv, send_sem, recv_sem)
-    entered()
     for copy in copies:
         copy.start()
     total = held[...]
@@ -1190,66 +1365,51 @@
 
 
 def attention_kernel(
-    n, heads, model_width, qkv, q_gain, k_gain, cos, sin, starts,
-    out, q_low, k_low, v_low, log_total, q_inv, k_inv, *sums,
+    q_raw, k_raw, v_raw, q_inv, k_inv, q_gain, k_gain, cos, sin, starts,
+    out, q_low, k_low, v_low, log_total,
 ):
-    me = lax.axis_index("mp")
-    entered = peer_barrier((("mp", me, n),))
-    size = qkv.shape[0]
-    width = qkv.shape[1] // 3
-    head = width // heads
+    size, head = q_raw.shape
     score_scale = 1.0 / math.sqrt(head)
-
-    def squares(first):
-        return jnp.sum(jnp.square(qkv[:, first : first + width]), axis=1, keepdims=True)
-
-    q_sum, k_sum = sum_columns(n, me, squares(0), squares(width), entered, *sums)
-    q_inv[...] = lax.rsqrt(q_sum / model_width + EPS)
-    k_inv[...] = lax.rsqrt(k_sum / model_width + EPS)
+    q_low[...] = turn(q_raw[...] * q_inv[...] * q_gain[...], cos[...], sin[...]).astype(BF)
+    k_low[...] = turn(k_raw[...] * k_inv[...] * k_gain[...], cos[...], sin[...]).astype(BF)
+    v_low[...] = v_raw[...].astype(BF)
     rows = min(QUERY_ROWS, size)
-
-    @pl.loop(0, heads)
-    def _(h):
-        def cols(first):
-            return pl.ds(pl.multiple_of(first + h * head, head), head)
-
-        here = cols(0)
-        q_low[:, here] = turn(
-            qkv[:, here] * q_inv[...] * q_gain[:, here], cos[...], sin[...]
-        ).astype(BF)
-        k_low[:, here] = turn(
-            qkv[:, cols(width)] * k_inv[...] * k_gain[:, here], cos[...], sin[...]
-        ).astype(BF)
-        v_low[:, here] = qkv[:, cols(2 * width)].astype(BF)
-        for first in range(0, size, rows):
-            end = first + rows
-            span = slice(first, end)
-            scores = outer_dot(q_low[span, here], k_low[:end, here]) * score_scale
-            scores = jnp.where(allowed_keys(starts[span], first, rows, end), scores, MASKED)
-            row_max = jnp.max(scores, axis=1, keepdims=True)
-            exponents = jnp.exp(scores - row_max)
-            row_total = jnp.sum(exponents, axis=1, keepdims=True)
-            probs = (exponents * (1.0 / row_total)).astype(BF)
-            out[span, here] = plain_dot(probs, v_low[:end, here]).astype(BF)
-            log_total[h, span] = row_max + jnp.log(row_total)
-
-
-def attention(n, heads, model_width, qkv_raw, q_gain, k_gain, cos, sin, starts):
+    for first in range(0, size, rows):
+        end = first + rows
+        span = slice(first, end)
+        scores = outer_dot(q_low[span], k_low[:end]) * score_scale
+        scores = jnp.where(allowed_keys(starts[span], first, rows, end), scores, MASKED)
+        row_max = jnp.max(scores, axis=1, keepdims=True)
+        exponents = jnp.exp(scores - row_max)
+        row_total = jnp.sum(exponents, axis=1, keepdims=True)
+        probs = (exponents * (1.0 / row_total)).astype(BF)
+        out[span] = plain_dot(probs, v_low[:end]).astype(BF)
+        log_total[span] = row_max + jnp.log(row_total)
+
+
+def head_specs(size, head, heads, count):
+    return [pl.BlockSpec((size, head), lambda h, k=k: (0, k * heads + h)) for k in range(count)]
+
+
+def attention(qkv_raw, q_inv, k_inv, q_gain, k_gain, cos, sin, starts, heads):
     size = qkv_raw.shape[0]
-    low = jax.ShapeDtypeStruct((size, qkv_raw.shape[1] // 3), BF)
-    column = jax.ShapeDtypeStruct((size, 1), F32)
+    head = cos.shape[1]
+    column = pl.BlockSpec((size, 1), lambda h: (0, 0))
+    table = pl.BlockSpec((size, head), lambda h: (0, 0))
+    gain = pl.BlockSpec((1, head), lambda h: (0, h))
+    by_head = pl.BlockSpec((size, head), lambda h: (0, h))
+    low = jax.ShapeDtypeStruct((size, heads * head), BF)
     return pl.pallas_call(
-        functools.partial(attention_kernel, n, heads, model_width),
-        out_shape=(low,) * 4 + (jax.ShapeDtypeStruct((heads, size, 1), F32), column, column),
-        in_specs=[VMEM] * 6,
-        out_specs=(VMEM,) * 7,
-        scratch_shapes=sum_scratch(n, size),
-        compiler_params=pltpu.CompilerParams(
-            collective_id=5, has_side_effects=True, vmem_limit_bytes=56 * MIB
-        ),
+        attention_kernel,
+        grid=(heads,),
+        out_shape=(low, low, low, low, jax.ShapeDtypeStruct((heads, size, 1), F32)),
+        in_specs=head_specs(size, head, heads, 3)
+        + [column, column, gain, gain, table, table, column],
+        out_specs=(by_head,) * 4 + (pl.BlockSpec((None, size, 1), lambda h: (h, 0, 0)),),
+        compiler_params=pltpu.CompilerParams(vmem_limit_bytes=48 * MIB),
         name="attention",
-        cost_estimate=cost(25),
-    )(qkv_raw, q_gain, k_gain, cos, sin, starts)
+        cost_estimate=cost(18),
+    )(qkv_raw, qkv_raw, qkv_raw, q_inv, k_inv, q_gain, k_gain, cos, sin, starts)
 
 
 def attention_back_kernel(
@@ -1308,7 +1468,10 @@
             dots[...] += jnp.sum(weighted * raw, axis=1, keepdims=True)
         grads[:, cols(2 * width)] = v_sum[...].astype(BF)
 
-    q_total, k_total = sum_columns(n, me, q_dots[...], k_dots[...], entered, *sums)
+    held = sums[0]
+    held[...] = columns_to_rows(q_dots[...], k_dots[...])
+    entered()
+    q_total, k_total = sum_held(n, me, *sums)
     for first, inv, weighted, dots in (
         (0, q_inv, q_weighted, q_total),
         (width, k_inv, k_weighted, k_total),
@@ -1372,10 +1535,6 @@
     head_size = gain_part * n_dp
     local_width = local_heads * head_size
 
-    full_qkv = lax.all_gather(
-        jnp.concatenate([query_weight, key_weight, value_weight], axis=1), "dp", axis=0, tiled=True
-    )
-    full_out = lax.all_gather(out_weight, "dp", axis=1, tiled=True)
     full_gate = lax.all_gather(gate_weight, "dp", axis=0, tiled=True)
     full_up = lax.all_gather(up_weight, "dp", axis=0, tiled=True)
     full_down = lax.all_gather(down_weight, "dp", axis=1, tiled=True)
@@ -1384,7 +1543,9 @@
     own_gains = jnp.concatenate(
         [attn_gain, mlp_gain, query_gain.reshape(head_part), key_gain.reshape(head_part)]
     ).astype(F32)[None]
-    inputs_full, gain_parts = gather_rows(n, n_dp, layer_input, own_gains)
+    inputs_full, qkv_raw, full_qkv, full_out, gain_parts, query_inv, key_inv = front(
+        n, n_dp, layer_input, query_weight, key_weight, value_weight, out_weight, own_gains
+    )
     inputs_full = inputs_full.reshape(group_size, model_width)
     gain_parts = gain_parts[:, 0]
 
@@ -1402,9 +1563,9 @@
     cos_table, sin_table = rotary_tables(positions, head_size)
     row_valid = lax.dynamic_slice_in_dim(valid, me * row_count, row_count, 0).astype(F32)[:, None]
 
-    qkv_raw = plain_dot(inputs_full, full_qkv)
-    attended, query_low, key_low, value_low, log_total, query_inv, key_inv = attention(
-        n, local_heads, model_width, qkv_raw, query_scale, key_scale, cos_table, sin_table, starts
+    attended, query_low, key_low, value_low, log_total = attention(
+        qkv_raw, query_inv, key_inv, query_scale, key_scale, cos_table, sin_table, starts,
+        local_heads,
     )
     branch, middle, middle_full = attn_out(n, attended, full_out, layer_input, attn_scale)
     (

time: 688 us -> 679 us (0.987)
  matrix products: 31.4 us -> 20 us
  local copies, waits for them, and re-layouts: 21 us -> 30.3 us
    dot_general x1 -> x0, matrix products: 11.7 us -> none  [plain_dot(): return jnp.dot(former, latter, preferred_element_type=F32)]
    pallas_call x2, Pallas kernels: 103 us -> 112 us  [the longest x1 93.9 us: front(): pl.pallas_call(functools.partial(front_kernel, n, n_dp, rows, model_width...]
    unnamed x35 -> x59, local copies, waits for them, and re-layouts: 9.28 us -> 17.8 us
  transfers between devices with their start and end apart: 6 -> 4, of which waited for: 1 -> 0; matrix products, arithmetic and copies ran while one was open for 6% -> 4% of each run, Pallas kernels for 50% -> 51%
where the time goes in v5:
time: 679 us; the launch traced here: 670 us
  Pallas kernels  592 us (87%)
  local copies, waits for them, and re-layouts  30.3 us (4%)
  matrix products  20 us (3%)
  between operations  14.2 us (2%)
  other arithmetic  10.9 us (2%)
    pallas_call x1, Pallas kernels, mlp(): pl.pallas_call(functools.partial(mlp_kernel, n, n_dp, rows), out_shape=(j...  249 us
    pallas_call x1, Pallas kernels, attn_out(): pl.pallas_call(functools.partial(attn_out_kernel, n, rows), out_shape=(ja...  117 us
    pallas_call x1, Pallas kernels, front(): pl.pallas_call(functools.partial(front_kernel, n, n_dp, rows, model_width...  93.9 us
    pallas_call x1, Pallas kernels, last_grads(): pl.pallas_call(functools.partial(last_grads_kernel, n, n_dp, rows), out_s...  85.7 us
    pallas_call x1, Pallas kernels, attention_back(): pl.pallas_call(functools.partial(attention_back_kernel, n, heads, model_w...  28.6 us
    pallas_call x1, Pallas kernels, attention(): pl.pallas_call(attention_kernel, grid=(heads,), out_shape=(low, low, low,...  17.9 us
    unnamed x59, local copies, waits for them, and re-layouts  17.8 us
    dot_general x1, matrix products, inner_dot(): lax.dot_general(former, latter, (((0,), (0,)), ((), ())), preferred_eleme...  14.5 us
  transfers between devices with their start and end apart: 4, of which 0 were waited for; matrix products, arithmetic and copies ran while one was open for 4% of the time, Pallas kernels for 51%

profile of v5, /device:TPU:0, one launch (start us, length us, event | category | flops | bytes accessed | tf_op | source)
XLA Modules:
  0.0 669.8 jit_solution(11870810854700473486)
XLA Ops:
  12.4 1.2 copy-done.5
  17.4 93.9 %front.1 = (bf16[4,256,2048]{2,1,0:T(8,128)(2,1)}, f32[1024,1536]{1,0:T(8,128)}, bf16[2048,1536]{1,0:T(8,128)(2,1)}, bf16[512,2048]{1,0:T(8,128)(2,1)S(1)}, f32[...) custom-call(bf16[256,2048]{1,0:T(8,128)(2,1)S(1)} %copy-done.5, ...), custom_call_target="tpu_custom_call" | custom-call | flops 80000000000 | bytes 240000000 | tf_op jit(solution)/shard_map/front/pallas_call | solution.py:642
  111.3 1.3 copy-done.10
  117.8 1.9 fusion
  120.0 17.9 %attention.1 = (bf16[1024,512]{1,0:T(8,128)(2,1)S(1)}, bf16[1024,512]{1,0:T(8,128)(2,1)S(1)}, bf16[1024,512]{1,0:T(8,128)(2,1)S(1)}, bf16[1024,512]{1,0:T(8,128)(2,1)}, f32[4,1024,1]{2,1,0:T(8,128)}) custom-call(f32[1024,1536]{1,0:T(8,128)} %get-tuple-element.46.q_raw.k_raw.v_raw.qkv, f32[1024,1536]{1,0:T(8,128)} %get-tuple-element.46.q_raw.k_raw.v_raw.qkv, ...), custom_call_target="tpu_custom_call" | custom-call | flops 17999998976 | bytes 54000000 | tf_op jit(solution)/shard_map/attention/pallas_call | solution.py:1402
  138.1 1.0 copy-done.12
  139.0 1.0 copy-done.13
  140.0 1.0 copy-done.14
  141.0 116.6 %attn_out.1 = (f32[256,2048]{1,0:T(8,128)}, f32[256,2048]{1,0:T(8,128)}, bf16[4,256,2048]{2,1,0:T(8,128)(2,1)}) custom-call(bf16[1024,512]{1,0:T(8,128)(2,1)} %copy-done.12, bf16[512,2048]{1,0:T(8,128)(2,1)} %copy-done.10, bf16[256,2048]{1,0:T(8,128)(2,1)} %x.3, f32[1,2048]{1,0:T(1,128)} %bitcast.51), custom_call_target="tpu_custom_call" | custom-call | flops 115000000512 | bytes 345000000 | tf_op jit(solution)/shard_map/attn_out/pallas_call | solution.py:716
  257.6 249.3 %mlp.1 = (bf16[256,2048]{1,0:T(8,128)(2,1)}, bf16[4,256,2048]{2,1,0:T(8,128)(2,1)}, bf16[4,256,2048]{2,1,0:T(8,128)(2,1)}, f32[1,2048]{1,0:T(1,128)}, f32[256,20...) custom-call(bf16[4,256,2048]{2,1,0:T(8,128)(2,1)} %get-tuple-element, ...), custom_call_target="tpu_custom_call" | custom-call | flops 260000006144 | bytes 780000000 | tf_op jit(solution)/shard_map/mlp/pallas_call | solution.py:1068
  507.0 14.5 %bitcast_convert_fusion = bf16[2048,2048]{1,0:T(8,128)(2,1)} fusion(bf16[4,256,2048]{2,1,0:T(8,128)(2,1)} %get-tuple-element.60, bf16[4,256,2048]{2,1,0:T(8,128)(2,1)} %get-tuple-element.61), kind=kOutput, calls=%fused_computation | convolution fusion | flops 8594128896 | bytes 16777216 | tf_op jit(solution)/shard_map/dot_general | solution.py:39
  521.5 1.6 copy-done.11
  523.0 5.5 convolution_convert_fusion.out_grad
  528.6 28.6 %attention_back.1 = (bf16[1024,1536]{1,0:T(8,128)(2,1)}, f32[1,512]{1,0:T(1,128)}, f32[1,512]{1,0:T(1,128)}) custom-call(f32[1024,1536]{1,0:T(8,128)} %get-tuple-element.46.q_raw.k_raw.v_raw.qkv, bf16[1024,512]{1,0:T(8,128)(2,1)} %copy-done.13, bf16[1024,512]{1,0:T(8,128)(2,1)} %copy-done.14, bf16[1024,512]{1,0:T(8,128)(2,1)} %get-tuple-element.58.v_low, ...), custom_call_target="tpu_custom_call" | custom-call | flops 30000001024 | bytes 90000000 | tf_op jit(solution)/shard_map/attention_back/pallas_call | solution.py:1493
  557.7 1.3 reduce.21
  559.2 1.3 reduce.20
  562.8 85.7 %last_grads.1 = (f32[256,2048]{1,0:T(8,128)}, f32[256,1536]{1,0:T(8,128)}, f32[512,256]{1,0:T(8,128)}, f32[1,640]{1,0:T(1,128)}) custom-call(bf16[1024,1536]{1,0:T(8,128)(2,1)} %get-tuple-element.64.grads, bf16[2048,1536]{1,0:T(8,128)(2,1)} %get-tuple-element.65.weight, f32[256,2048]{1,0:T(8,128)} %get-tuple-element.66.base, bf16[1024,2048]{1,0:T(8,128)(2,1)} %bitcast.59, ...), custom_call_target="tpu_custom_call" | custom-call | flops 80000000000 | bytes 240000000 | tf_op jit(solution)/shard_map/last_grads/pallas_call | solution.py:1287
  650.6 1.2 fusion.6
  651.9 2.7 fusion.4
  654.6 2.8 convert_element_type.37
  657.3 1.0 copy.67
  658.3 1.3 copy.68
  660.4 1.3 copy.70
  661.7 1.3 copy.71
  (101 shorter events, 20.3 us)
Async XLA Ops:
  7.2 250.4 %all-gather.4.cloned.1.call-start = ((), (), s32[]{:S(2)}) async-start(), calls=%async_computation.1 | async-start | bytes 9437184 | tf_op jit(solution)/shard_map/all_gather | solution.py:1538
  7.9 249.7 %all-gather.6.cloned.1.call-start = ((), (), s32[]{:S(2)}) async-start(), calls=%async_computation.2 | async-start | bytes 9437184 | tf_op jit(solution)/shard_map/all_gather | solution.py:1539
  8.7 249.0 %all-gather.8.cloned.1.call-start = ((), (), s32[]{:S(2)}) async-start(), calls=%async_computation.3 | async-start | bytes 9437184 | tf_op jit(solution)/shard_map/all_gather | solution.py:1540
  9.4 645.2 %reduce-scatter.2.cloned.1.call-start = ((), (), s32[]{:S(2)}) async-start(), calls=%async_computation.4 | async-start | bytes 9437184 | tf_op jit(solution)/shard_map/reduce_scatter | solution.py:1585
  12.4 1.2 copy-start.5
  17.4 95.2 %copy-start.24 = (s32[1,2]{1,0:T(1,128)S(1)}, s32[1,2]{1,0:T(1,128)}, u32[]{:S(2)}) copy-start(s32[1,2]{1,0:T(1,128)} %param.26) | copy-start | bytes 28
  111.3 1.3 copy-start.10
  112.6 25.3 %copy-start.15 = (f32[1024,1]{1,0:T(8,128)}, f32[1024,1]{1,0:T(8,128)S(1)}, u32[]{:S(2)}) copy-start(f32[1024,1]{1,0:T(8,128)S(1)} %get-tuple-element.47.q_inv) | copy-start | bytes 12292
  112.6 25.3 %copy-start.16 = (f32[1024,1]{1,0:T(8,128)}, f32[1024,1]{1,0:T(8,128)S(1)}, u32[]{:S(2)}) copy-start(f32[1024,1]{1,0:T(8,128)S(1)} %get-tuple-element.48.k_inv) | copy-start | bytes 12292
  114.6 23.4 %copy-start.2 = (s32[1024,1]{1,0:T(8,128)}, s32[1024,1]{1,0:T(8,128)S(1)}, u32[]{:S(2)}) copy-start(s32[1024,1]{1,0:T(8,128)S(1)} %copy.42.starts) | copy-start | bytes 12292
  114.8 23.2 %copy-start.3 = (f32[1,512]{1,0:T(1,128)}, f32[1,512]{1,0:T(1,128)S(1)}, u32[]{:S(2)}) copy-start(f32[1,512]{1,0:T(1,128)S(1)} %reshape.192.q_gain) | copy-start | bytes 6148
  115.0 23.0 %copy-start.4 = (f32[1,512]{1,0:T(1,128)}, f32[1,512]{1,0:T(1,128)S(1)}, u32[]{:S(2)}) copy-start(f32[1,512]{1,0:T(1,128)S(1)} %reshape.194.k_gain) | copy-start | bytes 6148
  120.0 18.0 %copy-start = (f32[1024,128]{1,0:T(8,128)}, f32[1024,128]{1,0:T(8,128)S(1)}, u32[]{:S(2)}) copy-start(f32[1024,128]{1,0:T(8,128)S(1)} %get-tuple-element.95.cos) | copy-start | bytes 1572868
  120.0 18.0 %copy-start.1 = (f32[1024,128]{1,0:T(8,128)}, f32[1024,128]{1,0:T(8,128)S(1)}, u32[]{:S(2)}) copy-start(f32[1024,128]{1,0:T(8,128)S(1)} %get-tuple-element.96.sin) | copy-start | bytes 1572868
  138.0 1.0 copy-start.12
  140.0 1.0 copy-start.14
  521.5 1.6 copy-start.11
  528.6 32.1 %copy-start.23 = (f32[1,2048]{1,0:T(1,128)S(1)}, f32[1,2048]{1,0:T(1,128)}, u32[]{:S(2)}) copy-start(f32[1,2048]{1,0:T(1,128)} %get-tuple-element.68) | copy-start | bytes 24580
  528.6 32.8 %copy-start.22 = (f32[1,2048]{1,0:T(1,128)S(1)}, f32[1,2048]{1,0:T(1,128)}, u32[]{:S(2)}) copy-start(f32[1,2048]{1,0:T(1,128)} %get-tuple-element.69) | copy-start | bytes 24580
  648.5 8.9 %copy-start.20 = (bf16[256,2048]{1,0:T(8,128)(2,1)S(1)}, bf16[256,2048]{1,0:T(8,128)(2,1)}, u32[]{:S(2)}) copy-start(bf16[256,2048]{1,0:T(8,128)(2,1)} %get-tuple-element.110) | copy-start | bytes 3145732
  651.9 6.4 copy-start.19
  654.6 5.1 copy-start.21
  657.3 3.1 copy-start.18
  658.3 3.4 copy-start.17
  (5 other events, 4.8 us)
Sparse Core Ops, SparseCore 0:
  9.9 83.4 all-gather.3
  95.2 53.8 all-gather.5
  151.0 55.9 all-gather.7
  521.6 69.9 reduce-scatter.1

commit v6 on v5

--- a/solution.py
+++ b/solution.py
@@ -16,6 +16,7 @@
 EDGES = False
 FILL = 2
 PERIOD = 8
+HOOKS = (3, 7, 10, 13, 16)
 TILE = 512
 QUERY_ROWS = 256
 BF = jnp.bfloat16
@@ -508,11 +509,11 @@
 
 
 def front_kernel(
-    n, n_dp, rows, model_width, x, wq, wk, wv, wo, gains,
-    full, qkv, full_qkv, full_out, gain_parts, q_inv, k_inv,
+    n, n_dp, rows, model_width, x, wq, wk, wv, wo, gains, wg,
+    full, qkv, full_qkv, full_out, gain_parts, q_inv, k_inv, full_gate,
     send_sem, recv_sem, local_sem, gain_recv, gain_send_sem, gain_recv_sem,
     vqkv, vout, save_sem, x_buf, x_sem, squares,
-    held, sum_recv, turned, sum_send_sem, sum_recv_sem, *plane,
+    held, sum_recv, turned, sum_send_sem, sum_recv_sem, gate_sem, *plane,
 ):
     me, at = lax.axis_index("mp"), lax.axis_index("dp")
     peer_barrier((("mp", me, n), ("dp", at, n_dp)))()
@@ -535,12 +536,16 @@
         return pl.ds(pl.multiple_of(owner * part_width, part_width), part_width)
 
     by_qkv = PlaneGather(at, chips, part_width, lambda owner: vqkv.at[part(owner)], plane[:4])
-    by_out = PlaneGather(at, chips, width, lambda owner: vout.at[:, part(owner)], plane[4:])
+    by_out = PlaneGather(at, chips, width, lambda owner: vout.at[:, part(owner)], plane[4:8])
+    by_gate = PlaneGather(
+        at, chips, part_width, lambda owner: full_gate.at[part(owner)], plane[8:]
+    )
+    gate_copy = pltpu.make_async_copy(wg, full_gate.at[part(at)], gate_sem)
+    gate_copy.start()
     for k, weight in enumerate((wq, wk, wv)):
         vqkv[part(at), k * width : (k + 1) * width] = weight[...]
     by_qkv.send(False)
     vout[:, part(at)] = wo[...]
-    by_out.send(False)
     copies = exchange(
         "dp", at, n_dp, lambda peer: gains, gain_recv, gain_send_sem, gain_recv_sem
     )
@@ -578,47 +583,55 @@
     early = [r for r in range(1, chips) if len(bits_of(r)) == 1]
     late = [r for r in range(1, chips) if len(bits_of(r)) > 1]
 
-    def weights_here():
+    def next_weights():
+        by_qkv.send(True)
+        by_out.send(False)
+        gate_copy.wait()
+        by_gate.send(False)
+
+    def qkv_here():
         by_qkv.finish()
         saves[0].start()
         block(me, x)
 
-    hooks = [
-        lambda: by_qkv.send(True),
-        None,
-        None,
-        lambda: by_qkv.swap(early),
-        lambda: (by_qkv.swap(late), by_out.send(True)),
-        lambda: by_out.swap(early + late),
-        weights_here,
-    ]
-    ready = 1
-    for step in range(2, n):
+    def out_here():
+        by_out.swap(late)
+        by_out.finish()
+        saves[1].start()
+
+    hooks = {
+        0: next_weights,
+        3: lambda: by_qkv.swap(early),
+        4: lambda: by_qkv.swap(late),
+        5: qkv_here,
+        6: lambda: by_out.send(True),
+        7: lambda: (by_out.swap(early), by_gate.send(True)),
+        8: out_here,
+        9: lambda: by_gate.swap(early),
+    }
+    ready, number = 1, 0
+    for step in range(2, n + 1):
         for c in range(CHUNKS):
-            gather.step(c, step)
-            if hooks:
-                hook = hooks.pop(0)
-                if hook is not None:
-                    hook()
-        if not hooks:
-            while ready < step:
-                blocks_at(ready)
-                ready += 1
-    for hook in hooks:
-        if hook is not None:
-            hook()
-    while ready < n - 1:
+            if step < n:
+                gather.step(c, step)
+            else:
+                gather.last(c)
+            if number in hooks:
+                hooks.pop(number)()
+            number += 1
+        while number > 5 and ready < step:
+            blocks_at(ready)
+            ready += 1
+    for hook in hooks.values():
+        hook()
+    while ready < n:
         blocks_at(ready)
         ready += 1
     gain_parts[at] = gains[...]
     for shift, copy in enumerate(copies, 1):
         copy.wait_recv()
         gain_parts[lax.rem(at + n_dp - shift, n_dp)] = gain_recv[shift - 1]
-    by_out.finish()
-    saves[1].start()
-    for c in range(CHUNKS):
-        gather.last(c)
-    blocks_at(n - 1)
+    by_gate.swap(late)
     q_sum, k_sum = sum_held(n, me, held, sum_recv, turned, sum_send_sem, sum_recv_sem)
     q_inv[...] = lax.rsqrt(q_sum / model_width + EPS)
     k_inv[...] = lax.rsqrt(k_sum / model_width + EPS)
@@ -626,13 +639,14 @@
         gather.drain(c)
     for copy in copies:
         copy.wait_send()
-    for gathered in (by_qkv, by_out):
+    by_gate.finish()
+    for gathered in (by_qkv, by_out, by_gate):
         gathered.drain()
     for copy in saves:
         copy.wait()
 
 
-def front(n, n_dp, block, wq, wk, wv, wo, gains):
+def front(n, n_dp, block, wq, wk, wv, wo, gains, wg):
     row_count, model_width = block.shape
     rows = row_count // CHUNKS
     size = n * row_count
@@ -649,9 +663,10 @@
             jax.ShapeDtypeStruct((n_dp,) + gains.shape, F32),
             column,
             column,
+            jax.ShapeDtypeStruct((model_width, wg.shape[1]), BF),
         ),
-        in_specs=[HBM] + [VMEM] * 5,
-        out_specs=(HBM, VMEM, HBM, HBM, VMEM, VMEM, VMEM),
+        in_specs=[VMEM] * 7,
+        out_specs=(HBM, VMEM, HBM, HBM, VMEM, VMEM, VMEM, HBM),
         scratch_shapes=gather_scratch(n, rows, model_width)[1:]
         + [
             pltpu.VMEM((n_dp - 1,) + gains.shape, F32),
@@ -665,146 +680,119 @@
             pltpu.VMEM((3, row_count, 1), F32),
         ]
         + sum_scratch(n, size)
-        + plane_sems(chips) * 2,
+        + [pltpu.SemaphoreType.DMA]
+        + plane_sems(chips) * 3,
         compiler_params=pltpu.CompilerParams(
-            collective_id=0, has_side_effects=True, vmem_limit_bytes=48 * MIB
+            collective_id=0, has_side_effects=True, vmem_limit_bytes=63 * MIB
         ),
         name="front",
         cost_estimate=cost(80),
-    )(block, wq, wk, wv, wo, gains)
-
-
-def attn_out_kernel(
-    n, rows, att, wo, x, scale, branch, middle, full,
+    )(block, wq, wk, wv, wo, gains, wg)
+
+
+class WeightTiles:
+    def __init__(self, source, held, sem, axis, size):
+        self.source, self.held, self.sem, self.axis, self.size = source, held, sem, axis, size
+        self.count = source.shape[axis] // size
+
+    def at(self, ref, tile):
+        span = pl.ds(pl.multiple_of(tile * self.size, self.size), self.size)
+        return ref.at[:, span] if self.axis == 1 else ref.at[span]
+
+    def copy(self, tile):
+        return pltpu.make_async_copy(
+            self.at(self.source, tile), self.at(self.held, tile), self.sem.at[tile]
+        )
+
+    def start(self):
+        for tile in range(self.count):
+            self.copy(tile).start()
+
+
+def middle_kernel(
+    n, n_dp, rows, att, wo, wg, wu, wd, x, upstream_in, row_valid, mlp_scale, attn_scale,
+    h_full, output, dm_full, hidden_out, mlp_gain, middle_grad, da_full, attn_gain, gate_out, up_out,
     part, recv, rs_send_sem, rs_recv_sem, total, own, ag_send_sem, ag_recv_sem, local_sem,
-    packed,
+    vg, vu, vd, wsem, in_buf, in_sem, gate_all, up_all, hidden_buf, hidden_sem, packed,
+    middle, branch, mg_sem, h_buf, h_sem, extra, ready, *more,
 ):
-    me = lax.axis_index("mp")
-    neighbour_barrier(me, n)
-    width = wo.shape[1]
-    block_rows = rows * CHUNKS
-
-    def compute(c):
+    me, at = lax.axis_index("mp"), lax.axis_index("dp")
+    width, hidden_width = vg.shape
+    local_width = wo.shape[0]
+    chips = n_dp // 2
+    part_width = width // n_dp
+    plane, more = more[:16], more[16:]
+    v_out = more[0] if more else gate_all.at[pl.ds(0, local_width)]
+    v_att = up_all.at[:, pl.ds(0, local_width)]
+
+    def start(copies):
+        for copy in copies:
+            copy.start()
+
+    def wait(copies):
+        for copy in copies:
+            copy.wait()
+
+    def weight_part(owner):
+        return pl.ds(pl.multiple_of(owner * part_width, part_width), part_width)
+
+    by_up = PlaneGather(at, chips, part_width, lambda owner: vu.at[weight_part(owner)], plane[8:12])
+    by_down = PlaneGather(
+        at, chips, hidden_width, lambda owner: vd.at[:, weight_part(owner)], plane[12:]
+    )
+    own_weights = [
+        pltpu.make_async_copy(wu, by_up.place(0), wsem.at[0]),
+        pltpu.make_async_copy(wd, by_down.place(0), wsem.at[1]),
+    ]
+    gate_copy = pltpu.make_async_copy(wg, vg, wsem.at[2])
+    att_copies = [
+        pltpu.make_async_copy(wo, v_out, wsem.at[3]),
+        pltpu.make_async_copy(att, v_att, wsem.at[4]),
+    ]
+    start(att_copies)
+    start(own_weights)
+    gate_copy.start()
+    stage_barrier(me, n, at, chips)
+    wait(own_weights)
+    by_up.send(False)
+
+    scatter = LineScatter(n, me, rows, part, recv, rs_send_sem, rs_recv_sem)
+    gathers = [
+        make_gather(n, me, rows, own, full, ag_send_sem, ag_recv_sem, local_sem)
+        for full in (h_full, dm_full, da_full)
+    ]
+
+    def in_copies(phase, c):
+        source = gathers[phase - 1].full
+        return [
+            pltpu.make_async_copy(
+                source(j, c), in_buf.at[c % 2, pl.ds(j * rows, rows)], in_sem.at[c % 2, j]
+            )
+            for j in range(n)
+        ]
+
+    def attend_out(c):
+        if c == 0:
+            wait(att_copies)
+        block_rows = rows * CHUNKS
         for j in range(n):
-            packed[j * rows : (j + 1) * rows] = att[
+            packed[j * rows : (j + 1) * rows] = v_att[
                 j * block_rows + c * rows : j * block_rows + (c + 1) * rows
             ]
 
         @pl.loop(0, width // TILE)
         def _(tile):
             cols = pl.ds(pl.multiple_of(tile * TILE, TILE), TILE)
-            part[c, :, cols] = plain_dot(packed[...], wo[:, cols]).astype(BF)
-
-    scatter = LineScatter(n, me, rows, part, recv, rs_send_sem, rs_recv_sem)
-    gather = make_gather(n, me, rows, own, full, ag_send_sem, ag_recv_sem, local_sem)
-
-    def row_work(c):
+            part[c, :, cols] = plain_dot(packed[...], v_out[:, cols]).astype(BF)
+
+    def attend_rows(c):
         scatter.total(c, total)
         span = chunk_span(c, rows)
         value = total[...]
         branch[span] = value
-        new = x[span].astype(F32) + value * inverse_rms(value) * scale[...]
+        new = x[span].astype(F32) + value * inverse_rms(value) * attn_scale[...]
         middle[span] = new
         own[c] = new.astype(BF)
-
-    run_line(n, CHUNKS, STAGGER, compute, scatter, row_work, gather)
-
-
-def attn_out(n, attended, full_out, layer_input, scale):
-    row_count, width = layer_input.shape
-    rows = row_count // CHUNKS
-    return pl.pallas_call(
-        functools.partial(attn_out_kernel, n, rows),
-        out_shape=(
-            jax.ShapeDtypeStruct((row_count, width), F32),
-            jax.ShapeDtypeStruct((row_count, width), F32),
-            jax.ShapeDtypeStruct((n, row_count, width), BF),
-        ),
-        in_specs=[VMEM] * 4,
-        out_specs=(VMEM, VMEM, HBM),
-        scratch_shapes=scatter_scratch(n, rows, width)
-        + gather_scratch(n, rows, width)
-        + [pltpu.VMEM((n * rows, attended.shape[1]), BF)],
-        compiler_params=pltpu.CompilerParams(
-            collective_id=1, has_side_effects=True, vmem_limit_bytes=56 * MIB
-        ),
-        name="attn_out",
-        cost_estimate=cost(115),
-    )(attended, full_out, layer_input, scale)
-
-
-class WeightTiles:
-    def __init__(self, source, held, sem, axis, size):
-        self.source, self.held, self.sem, self.axis, self.size = source, held, sem, axis, size
-        self.count = source.shape[axis] // size
-
-    def at(self, ref, tile):
-        span = pl.ds(pl.multiple_of(tile * self.size, self.size), self.size)
-        return ref.at[:, span] if self.axis == 1 else ref.at[span]
-
-    def copy(self, tile):
-        return pltpu.make_async_copy(
-            self.at(self.source, tile), self.at(self.held, tile), self.sem.at[tile]
-        )
-
-    def start(self):
-        for tile in range(self.count):
-            self.copy(tile).start()
-
-
-def mlp_kernel(
-    n, n_dp, rows, h_full, wg, wu, wd, middle, branch, upstream_in, row_valid, mlp_scale, attn_scale,
-    output, dm_full, hidden_out, mlp_gain, middle_grad, da_full, attn_gain, gate_out, up_out,
-    part, recv, rs_send_sem, rs_recv_sem, total, own, ag_send_sem, ag_recv_sem, local_sem,
-    vg, vu, vd, wsem, in_buf, in_sem, gate_all, up_all, hidden_buf, hidden_sem,
-    row_buf, row_sem, mg_buf, mg_sem, h_buf, h_sem, extra, ready, *plane,
-):
-    me, at = lax.axis_index("mp"), lax.axis_index("dp")
-    width, hidden_width = wg.shape
-    chips = n_dp // 2
-    part_width = width // n_dp
-
-    def in_copies(phase, c):
-        source = h_full if phase == 0 else dm_full
-        return [
-            pltpu.make_async_copy(
-                source.at[j, chunk_span(c, rows)],
-                in_buf.at[c % 2, pl.ds(j * rows, rows)],
-                in_sem.at[c % 2, j],
-            )
-            for j in range(n)
-        ]
-
-    def start(copies):
-        for copy in copies:
-            copy.start()
-
-    def wait(copies):
-        for copy in copies:
-            copy.wait()
-
-    def row_copy(phase, c):
-        source = middle if phase == 0 else branch
-        return pltpu.make_async_copy(
-            source.at[chunk_span(c, rows)], row_buf.at[c % 2], row_sem.at[c % 2]
-        )
-
-    start(in_copies(0, 0))
-    gate_tiles = WeightTiles(wg, vg, wsem.at[0], 1, TILE)
-    up_tiles = WeightTiles(wu, vu, wsem.at[1], 1, TILE)
-    down_tiles = WeightTiles(wd, vd, wsem.at[2], 1, TILE)
-    for tile in range(gate_tiles.count):
-        gate_tiles.copy(tile).start()
-        up_tiles.copy(tile).start()
-    down_tiles.start()
-    row_copy(0, 0).start()
-    stage_barrier(me, n, at, chips)
-
-    scatter = LineScatter(n, me, rows, part, recv, rs_send_sem, rs_recv_sem)
-    gathers = [
-        make_gather(n, me, rows, own, full, ag_send_sem, ag_recv_sem, local_sem)
-        for full in (dm_full, da_full)
-    ]
 
     def hidden_copies(c):
         return [
@@ -816,20 +804,23 @@
             for j in range(n)
         ]
 
+    def clear(phase, c):
+        scatter.drain(c)
+        gathers[phase - 1].drain_sends(c)
+        wait(in_copies(phase, c))
+
     def forward(c):
         here = pl.ds(c * n * rows, n * rows)
         slot = c % 2
-        wait(in_copies(0, c))
-        if c + 1 < CHUNKS:
-            start(in_copies(0, c + 1))
+        clear(1, c)
+        if c == 0:
+            by_up.finish()
+            gate_copy.wait()
         if c >= 2:
             wait(hidden_copies(c - 2))
 
         @pl.loop(0, hidden_width // TILE)
         def _(tile):
-            if c == 0:
-                gate_tiles.copy(tile).wait()
-                up_tiles.copy(tile).wait()
             cols = pl.ds(pl.multiple_of(tile * TILE, TILE), TILE)
             gate = plain_dot(in_buf[slot], vg[:, cols])
             up = plain_dot(in_buf[slot], vu[:, cols])
@@ -838,19 +829,18 @@
             hidden_buf[slot, :, cols] = (gate * jax.nn.sigmoid(gate) * up).astype(BF)
 
         start(hidden_copies(c))
+        if c == 0:
+            by_down.swap(late_chips)
+            by_down.finish()
 
         @pl.loop(0, width // TILE)
         def _(tile):
-            if c == 0:
-                down_tiles.copy(tile).wait()
             cols = pl.ds(pl.multiple_of(tile * TILE, TILE), TILE)
             part[c, :, cols] = plain_dot(hidden_buf[slot], vd[:, cols]).astype(BF)
 
     def backward(c):
         here = pl.ds(c * n * rows, n * rows)
-        scatter.drain(c)
-        gathers[0].drain_sends(c)
-        wait(in_copies(1, c))
+        clear(2, c)
 
         @pl.loop(0, hidden_width // TILE)
         def _(tile):
@@ -872,28 +862,24 @@
             ).astype(BF)
 
         if c + 1 == CHUNKS:
+            for last in range(max(CHUNKS - 2, 0), CHUNKS):
+                wait(hidden_copies(last))
+            for gathered in (by_up, by_down):
+                gathered.drain()
             start(h_copies(0))
             signal_partners(ready, at, chips)
 
     def mg_copy(c):
         return pltpu.make_async_copy(
-            mg_buf.at[c % 2], middle_grad.at[chunk_span(c, rows)], mg_sem.at[c % 2]
+            middle.at[chunk_span(c, rows)], middle_grad.at[chunk_span(c, rows)], mg_sem.at[c]
         )
-
-    def next_row_copy(phase, c):
-        if c + 1 < CHUNKS:
-            row_copy(phase, c + 1).start()
-        elif phase == 0:
-            row_copy(1, 0).start()
 
     def forward_rows(c):
         scatter.total(c, total)
         span = chunk_span(c, rows)
-        row_copy(0, c).wait()
-        next_row_copy(0, c)
         value = total[...]
         inverse = inverse_rms(value)
-        output[span] = (row_buf[c % 2] + value * inverse * mlp_scale[...]).astype(BF)
+        output[span] = (middle[span] + value * inverse * mlp_scale[...]).astype(BF)
         upstream = upstream_in[span].astype(F32) * row_valid[span]
         grad, gain = norm_back(value, inverse, mlp_scale[...], upstream)
         own[c] = grad.astype(BF)
@@ -902,14 +888,10 @@
     def backward_rows(c):
         scatter.total(c, total)
         span = chunk_span(c, rows)
-        row_copy(1, c).wait()
-        next_row_copy(1, c)
         upstream = upstream_in[span].astype(F32) * row_valid[span] + total[...]
-        if c >= 2:
-            mg_copy(c - 2).wait()
-        mg_buf[c % 2] = upstream
+        middle[span] = upstream
         mg_copy(c).start()
-        value = row_buf[c % 2]
+        value = branch[span]
         grad, gain = norm_back(value, inverse_rms(value), attn_scale[...], upstream)
         own[c] = grad.astype(BF)
         attn_gain[...] = gain if c == 0 else attn_gain[...] + gain
@@ -922,6 +904,10 @@
             if index < count:
                 return ref.at[pl.ds(index * part_width, part_width), block_width]
             index -= count
+        for ref in (hidden_buf, in_buf):
+            if index < ref.shape[0]:
+                return ref.at[index, pl.ds(0, part_width), block_width]
+            index -= ref.shape[0]
         return extra.at[index]
 
     reduces = []
@@ -1007,33 +993,49 @@
                         work.append(functools.partial(reduces[which].push, late, half))
     pending = iter(work)
 
+    early_chips = [r for r in range(1, chips) if len(bits_of(r)) == 1]
+    late_chips = [r for r in range(1, chips) if len(bits_of(r)) > 1]
+    hooks = {
+        HOOKS[0]: lambda: (by_up.send(True), by_down.send(False)),
+        HOOKS[1]: lambda: by_up.swap(early_chips),
+        HOOKS[2]: lambda: by_up.swap(late_chips),
+        HOOKS[3]: lambda: by_down.send(True),
+        HOOKS[4]: lambda: by_down.swap(early_chips),
+    }
     last_step = 2 * n - 2
     events = sorted(
-        (max(PERIOD, last_step + 1) * phase + step + STAGGER * c - (0.5 if step == 0 else 0), phase, c, step)
-        for phase in range(2)
+        (
+            max(PERIOD, last_step + 1) * phase + step + STAGGER * c - (0.5 if step == 0 else 0),
+            phase,
+            c,
+            step,
+        )
+        for phase in range(3)
         for c in range(CHUNKS)
         for step in range(last_step + 1)
     )
     filling = False
-    for _, phase, c, step in events:
+    for number, (_, phase, c, step) in enumerate(events):
         gather = gathers[phase]
+        if number in hooks:
+            hooks.pop(number)()
         if step == 0:
-            (forward, backward)[phase](c)
-            filling = filling or (phase == 1 and c + 1 == CHUNKS)
+            (attend_out, forward, backward)[phase](c)
+            filling = filling or (phase == 2 and c + 1 == CHUNKS)
         if step < n - 1:
             scatter.edge(c, step)
             if step > 0:
                 scatter.step(c, step)
         elif step == n - 1:
-            (forward_rows, backward_rows)[phase](c)
+            (attend_rows, forward_rows, backward_rows)[phase](c)
             gather.step(c, 1)
         elif step < last_step:
             gather.step(c, step - n + 2)
         else:
             gather.last(c)
-            if phase == 0:
+            if phase < 2:
                 gather.local_copy(c).wait()
-                start(in_copies(1, c))
+                start(in_copies(phase + 1, c))
         if filling:
             for _ in range(FILL):
                 job = next(pending, None)
@@ -1043,81 +1045,82 @@
         job()
     for c in range(CHUNKS):
         scatter.drain(c)
-        gathers[1].drain(c)
+        gathers[2].drain(c)
     for reduce in reduces:
         reduce.finish()
         reduce.drain()
     for r in range(chips):
         reduces[1].drain_core(r)
-    for c in range(max(CHUNKS - 2, 0), CHUNKS):
+    for c in range(CHUNKS):
         mg_copy(c).wait()
-        wait(hidden_copies(c))
-
-
-def mlp(n, n_dp, h_full, wg, wu, wd, middle, branch, out_grad, row_valid, mlp_scale, attn_scale):
-    row_count, width = branch.shape
+
+
+def middle(n, n_dp, attended, full_out, wg, wu, wd, x, out_grad, row_valid, mlp_scale, attn_scale):
+    row_count, width = x.shape
     hidden_width = wg.shape[1]
     rows = row_count // CHUNKS
     size = n * row_count
     chips = n_dp // 2
     part_width = width // n_dp
     block = (part_width, hidden_width)
-    most = max(width, hidden_width) // TILE
-    slots = (2 * width + hidden_width) // part_width
+    slots = (2 * width + hidden_width) // part_width + 4
     extra = 7 * chips - 1 - slots
+    by_rows = jax.ShapeDtypeStruct((n, row_count, width), BF)
     return pl.pallas_call(
-        functools.partial(mlp_kernel, n, n_dp, rows),
+        functools.partial(middle_kernel, n, n_dp, rows),
         out_shape=(
+            by_rows,
             jax.ShapeDtypeStruct((row_count, width), BF),
-            jax.ShapeDtypeStruct((n, row_count, width), BF),
+            by_rows,
             jax.ShapeDtypeStruct((n, row_count, hidden_width), BF),
             jax.ShapeDtypeStruct((1, width), F32),
             jax.ShapeDtypeStruct((row_count, width), F32),
-            jax.ShapeDtypeStruct((n, row_count, width), BF),
+            by_rows,
             jax.ShapeDtypeStruct((1, width), F32),
             jax.ShapeDtypeStruct(block, F32),
             jax.ShapeDtypeStruct(block, F32),
         ),
-        in_specs=[HBM] * 6 + [VMEM] * 4,
-        out_specs=(VMEM, HBM, HBM, VMEM, HBM, HBM, VMEM, VMEM, VMEM),
+        in_specs=[HBM] * 5 + [VMEM] * 5,
+        out_specs=(HBM, VMEM, HBM, HBM, VMEM, HBM, HBM, VMEM, VMEM, VMEM),
         scratch_shapes=scatter_scratch(n, rows, width)
         + gather_scratch(n, rows, width)
         + [
-            pltpu.VMEM(wg.shape, BF),
-            pltpu.VMEM(wu.shape, BF),
-            pltpu.VMEM(wd.shape, BF),
-            pltpu.SemaphoreType.DMA((3, most)),
+            pltpu.VMEM((width, hidden_width), BF),
+            pltpu.VMEM((width, hidden_width), BF),
+            pltpu.VMEM((hidden_width, width), BF),
+            pltpu.SemaphoreType.DMA((5,)),
             pltpu.VMEM((2, n * rows, width), BF),
             pltpu.SemaphoreType.DMA((2, n)),
             pltpu.VMEM((size, hidden_width), BF),
             pltpu.VMEM((size, hidden_width), BF),
             pltpu.VMEM((2, n * rows, hidden_width), BF),
             pltpu.SemaphoreType.DMA((2, n)),
-            pltpu.VMEM((2, rows, width), F32),
-            pltpu.SemaphoreType.DMA((2,)),
-            pltpu.VMEM((2, rows, width), F32),
-            pltpu.SemaphoreType.DMA((2,)),
+            pltpu.VMEM((n * rows, attended.shape[1]), BF),
+            pltpu.VMEM((row_count, width), F32),
+            pltpu.VMEM((row_count, width), F32),
+            pltpu.SemaphoreType.DMA((CHUNKS,)),
             pltpu.VMEM((2, n, row_count, part_width), BF),
             pltpu.SemaphoreType.DMA((2, n)),
             pltpu.VMEM((extra,) + block if extra > 0 else (1, 16, 128), BF),
             pltpu.SemaphoreType.REGULAR,
         ]
-        + plane_sems(chips) * 2,
+        + plane_sems(chips) * 4
+        + ([pltpu.VMEM(full_out.shape, BF)] if hidden_width < width else []),
         compiler_params=pltpu.CompilerParams(
             collective_id=2, has_side_effects=True, vmem_limit_bytes=63 * MIB
         ),
-        name="mlp",
-        cost_estimate=cost(260),
-    )(h_full, wg, wu, wd, middle, branch, out_grad, row_valid, mlp_scale, attn_scale)
+        name="middle",
+        cost_estimate=cost(350),
+    )(attended, full_out, wg, wu, wd, x, out_grad, row_valid, mlp_scale, attn_scale)
 
 
 def last_grads_kernel(
-    n, n_dp, rows, grads, weight, base, inputs, att, da, gains,
+    n, n_dp, rows, grads, weight, base, inputs, att, da, attn_gain, mlp_gain, q_gain, k_gain,
     input_grad, qkv_out, out_out, gain_out,
     part, recv, rs_send_sem, rs_recv_sem, total, packed,
     x_buf, da_buf, load_sem,
     send_qkv, recv_qkv, held_qkv, message_qkv, send_out, recv_out, held_out, message_out,
-    gain_recv, gain_send_sem, gain_recv_sem, mp_recv, mp_send_sem, mp_recv_sem, *plane,
+    gains, gain_recv, gain_send_sem, gain_recv_sem, mp_recv, mp_send_sem, mp_recv_sem, *plane,
 ):
     me, at = lax.axis_index("mp"), lax.axis_index("dp")
     entered = peer_barrier((("mp", me, n), ("dp", at, n_dp)))
@@ -1210,6 +1213,12 @@
                     if not reduce.before(r, half):
                         reduce.push(r, half)
 
+    for index in range(n_dp):
+        span = slice(index * part_width, (index + 1) * part_width)
+        gains[index, :, :part_width] = attn_gain[:, span]
+        gains[index, :, part_width : 2 * part_width] = mlp_gain[:, span]
+        gains[index, :, 2 * part_width : 2 * part_width + local_width] = q_gain[...]
+        gains[index, :, 2 * part_width + local_width :] = k_gain[...]
     gain_copies = exchange(
         "dp", at, n_dp, lambda peer: gains.at[peer], gain_recv, gain_send_sem, gain_recv_sem
     )
@@ -1275,7 +1284,7 @@
         reduce.drain()
 
 
-def last_grads(n, n_dp, grads, weight, base, inputs, attended, da_full, gains):
+def last_grads(n, n_dp, grads, weight, base, inputs, attended, da_full, *gains):
     row_count, width = base.shape
     rows = row_count // CHUNKS
     size, local_width = attended.shape
@@ -1283,7 +1292,7 @@
     chips = n_dp // 2
     qkv_block = (part_width, 3 * local_width)
     out_block = (local_width, part_width)
-    gain_block = gains.shape[1:]
+    gain_block = (1, 2 * part_width + 2 * local_width)
     return pl.pallas_call(
         functools.partial(last_grads_kernel, n, n_dp, rows),
         out_shape=(
@@ -1292,7 +1301,7 @@
             jax.ShapeDtypeStruct(out_block, F32),
             jax.ShapeDtypeStruct(gain_block, F32),
         ),
-        in_specs=[VMEM, VMEM, VMEM, HBM, VMEM, HBM, VMEM],
+        in_specs=[VMEM, VMEM, VMEM, HBM, VMEM, HBM] + [VMEM] * 4,
         out_specs=(VMEM,) * 4,
         scratch_shapes=scatter_scratch(n, rows, width)
         + [
@@ -1306,17 +1315,17 @@
             for block in (qkv_block, out_block)
             for count in (chips, chips, chips - 1, chips - 1)
         ]
-        + [pltpu.VMEM((n_dp - 1,) + gain_block, F32)]
+        + [pltpu.VMEM((n_dp,) + gain_block, F32), pltpu.VMEM((n_dp - 1,) + gain_block, F32)]
         + [pltpu.SemaphoreType.DMA((n_dp - 1,))] * 2
         + [pltpu.VMEM((n - 1,) + gain_block, F32)]
         + [pltpu.SemaphoreType.DMA((n - 1,))] * 2
         + plane_sems(chips) * 2,
         compiler_params=pltpu.CompilerParams(
-            collective_id=4, has_side_effects=True, vmem_limit_bytes=60 * MIB
+            collective_id=4, has_side_effects=True, vmem_limit_bytes=63 * MIB
         ),
         name="last_grads",
         cost_estimate=cost(80),
-    )(grads, weight, base, inputs, attended, da_full, gains)
+    )(grads, weight, base, inputs, attended, da_full, *gains)
 
 
 def turn(values, cos, sin):
@@ -1406,7 +1415,7 @@
         in_specs=head_specs(size, head, heads, 3)
         + [column, column, gain, gain, table, table, column],
         out_specs=(by_head,) * 4 + (pl.BlockSpec((None, size, 1), lambda h: (h, 0, 0)),),
-        compiler_params=pltpu.CompilerParams(vmem_limit_bytes=48 * MIB),
+        compiler_params=pltpu.CompilerParams(vmem_limit_bytes=63 * MIB),
         name="attention",
         cost_estimate=cost(18),
     )(qkv_raw, qkv_raw, qkv_raw, q_inv, k_inv, q_gain, k_gain, cos, sin, starts)
@@ -1500,7 +1509,7 @@
         + [pltpu.VMEM((size, 1), F32)] * 2
         + sum_scratch(n, size),
         compiler_params=pltpu.CompilerParams(
-            collective_id=6, has_side_effects=True, vmem_limit_bytes=56 * MIB
+            collective_id=6, has_side_effects=True, vmem_limit_bytes=63 * MIB
         ),
         name="attention_back",
         cost_estimate=cost(30),
@@ -1535,16 +1544,14 @@
     head_size = gain_part * n_dp
     local_width = local_heads * head_size
 
-    full_gate = lax.all_gather(gate_weight, "dp", axis=0, tiled=True)
-    full_up = lax.all_gather(up_weight, "dp", axis=0, tiled=True)
-    full_down = lax.all_gather(down_weight, "dp", axis=1, tiled=True)
     head_part = local_heads * gain_part
     width_part = attn_gain.shape[0]
     own_gains = jnp.concatenate(
         [attn_gain, mlp_gain, query_gain.reshape(head_part), key_gain.reshape(head_part)]
     ).astype(F32)[None]
-    inputs_full, qkv_raw, full_qkv, full_out, gain_parts, query_inv, key_inv = front(
-        n, n_dp, layer_input, query_weight, key_weight, value_weight, out_weight, own_gains
+    inputs_full, qkv_raw, full_qkv, full_out, gain_parts, query_inv, key_inv, full_gate = front(
+        n, n_dp, layer_input, query_weight, key_weight, value_weight, out_weight, own_gains,
+        gate_weight,
     )
     inputs_full = inputs_full.reshape(group_size, model_width)
     gain_parts = gain_parts[:, 0]
@@ -1567,13 +1574,12 @@
         qkv_raw, query_inv, key_inv, query_scale, key_scale, cos_table, sin_table, starts,
         local_heads,
     )
-    branch, middle, middle_full = attn_out(n, attended, full_out, layer_input, attn_scale)
     (
-        layer_output, mlp_grad_full, hidden, mlp_gain_part, middle_grad, branch_full,
+        middle_full, layer_output, mlp_grad_full, hidden, mlp_gain_part, middle_grad, branch_full,
         attn_gain_part, grad_gate, grad_up,
-    ) = mlp(
-        n, n_dp, middle_full, full_gate, full_up, full_down, middle, branch, out_grad, row_valid,
-        mlp_scale, attn_scale,
+    ) = middle(
+        n, n_dp, attended, full_out, full_gate, up_weight, down_weight, layer_input, out_grad,
+        row_valid, mlp_scale, attn_scale,
     )
 
     def flat(rows):
@@ -1590,27 +1596,18 @@
         query_inv, key_inv, query_scale, key_scale, cos_table, sin_table, starts,
     )
 
-    def by_part(row):
-        return row.reshape(n_dp, -1)
-
-    def by_head_part(row):
-        pieces = row.reshape(local_heads, n_dp, gain_part).transpose(1, 0, 2)
-        return pieces.reshape(n_dp, head_part)
-
-    gain_grads = jnp.concatenate(
-        [
-            by_part(attn_gain_part),
-            by_part(mlp_gain_part),
-            by_head_part(query_gain_part),
-            by_head_part(key_gain_part),
-        ],
-        axis=1,
-    )[:, None]
     input_grad, grad_qkv, grad_out, gain_sums = last_grads(
-        n, n_dp, qkv_grad, full_qkv, middle_grad, inputs_full, attended, branch_full, gain_grads
+        n, n_dp, qkv_grad, full_qkv, middle_grad, inputs_full, attended, branch_full,
+        attn_gain_part, mlp_gain_part, query_gain_part, key_gain_part,
     )
     gain_sums = gain_sums[0]
     heads_at = 2 * width_part
+    head_sums = lax.dynamic_index_in_dim(
+        gain_sums[heads_at:].reshape(2, local_heads, n_dp, gain_part),
+        lax.axis_index("dp"),
+        2,
+        keepdims=False,
+    )
     return (
         layer_output,
         input_grad,
@@ -1621,8 +1618,8 @@
         grad_gate,
         grad_up,
         grad_down.astype(F32),
-        gain_sums[heads_at : heads_at + head_part].reshape(local_heads, gain_part),
-        gain_sums[heads_at + head_part :].reshape(local_heads, gain_part),
+        head_sums[0],
+        head_sums[1],
         gain_sums[:width_part],
         gain_sums[width_part:heads_at],
     )

time: 679 us -> 645 us (0.950)
  Pallas kernels: 592 us -> 570 us
  local copies, waits for them, and re-layouts: 30.3 us -> 21.4 us
    pallas_call x2 -> x1, Pallas kernels: 366 us -> 348 us  [middle(): pl.pallas_call(functools.partial(middle_kernel, n, n_dp, rows), out_shape...]
    unnamed x59 -> x21, local copies, waits for them, and re-layouts: 17.8 us -> 9.25 us
  transfers between devices with their start and end apart: 4 -> 1, of which waited for: 0 -> 0; matrix products, arithmetic and copies ran while one was open for 4% -> 2% of each run, Pallas kernels for 51% -> 18%
where the time goes in v6:
time: 645 us; the launch traced here: 636 us
  Pallas kernels  570 us (88%)
  local copies, waits for them, and re-layouts  21.4 us (3%)
  matrix products  20.1 us (3%)
  between operations  14.3 us (2%)
  other arithmetic  9.66 us (1%)
    pallas_call x1, Pallas kernels, middle(): pl.pallas_call(functools.partial(middle_kernel, n, n_dp, rows), out_shape...  348 us
    pallas_call x1, Pallas kernels, front(): pl.pallas_call(functools.partial(front_kernel, n, n_dp, rows, model_width...  88.8 us
    pallas_call x1, Pallas kernels, last_grads(): pl.pallas_call(functools.partial(last_grads_kernel, n, n_dp, rows), out_s...  85.7 us
    pallas_call x1, Pallas kernels, attention_back(): pl.pallas_call(functools.partial(attention_back_kernel, n, heads, model_w...  30.1 us
    pallas_call x1, Pallas kernels, attention(): pl.pallas_call(attention_kernel, grid=(heads,), out_shape=(low, low, low,...  18 us
    dot_general x1, matrix products, inner_dot(): lax.dot_general(former, latter, (((0,), (0,)), ((), ())), preferred_eleme...  14.5 us
  transfers between devices with their start and end apart: 1, of which 0 were waited for; matrix products, arithmetic and copies ran while one was open for 2% of the time, Pallas kernels for 18%

profile of v6, /device:TPU:0, one launch (start us, length us, event | category | flops | bytes accessed | tf_op | source)
XLA Modules:
  0.0 635.9 jit_solution(12279032188005832759)
XLA Ops:
  7.2 0.8 reduce-window.4
  10.6 0.8 concatenate.26
  11.4 0.8 concatenate.27
  12.8 88.8 %front.1 = (bf16[4,256,2048]{2,1,0:T(8,128)(2,1)}, f32[1024,1536]{1,0:T(8,128)}, bf16[2048,1536]{1,0:T(8,128)(2,1)}, bf16[512,2048]{1,0:T(8,128)(2,1)}, f32[8,1,...) custom-call(bf16[256,2048]{1,0:T(8,128)(2,1)} %x.3, bf16[256,512]{1,0:T(8,128)(2,1)} %wq.1, ...), custom_call_target="tpu_custom_call" | custom-call | flops 80000000000 | bytes 240000000 | tf_op jit(solution)/shard_map/front/pallas_call | solution.py:656
  103.9 1.0 copy.40.starts
  106.5 0.8 copy.41.row_valid
  108.5 1.9 fusion
  110.4 1.3 pad_maximum_fusion
  111.7 18.0 %attention.1 = (bf16[1024,512]{1,0:T(8,128)(2,1)}, bf16[1024,512]{1,0:T(8,128)(2,1)}, bf16[1024,512]{1,0:T(8,128)(2,1)}, bf16[1024,512]{1,0:T(8,128)(2,1)}, f32[4,1024,1]{2,1,0:T(8,128)}) custom-call(f32[1024,1536]{1,0:T(8,128)} %get-tuple-element.44.q_raw.k_raw.v_raw.qkv, f32[1024,1536]{1,0:T(8,128)} %get-tuple-element.44.q_raw.k_raw.v_raw.qkv, ...), custom_call_target="tpu_custom_call" | custom-call | flops 17999998976 | bytes 54000000 | tf_op jit(solution)/shard_map/attention/pallas_call | solution.py:1411
  129.8 347.6 %middle.1 = (bf16[4,256,2048]{2,1,0:T(8,128)(2,1)}, bf16[256,2048]{1,0:T(8,128)(2,1)}, bf16[4,256,2048]{2,1,0:T(8,128)(2,1)}, bf16[4,256,2048]{2,1,0:T(8,128)(2,...) custom-call(bf16[1024,512]{1,0:T(8,128)(2,1)} %get-tuple-element.48., ...), custom_call_target="tpu_custom_call" | custom-call | flops 349999988736 | bytes 1050000000 | tf_op jit(solution)/shard_map/middle/pallas_call | solution.py:1069
  477.4 14.5 %bitcast_convert_fusion = bf16[2048,2048]{1,0:T(8,128)(2,1)} fusion(bf16[4,256,2048]{2,1,0:T(8,128)(2,1)} %get-tuple-element.56, bf16[4,256,2048]{2,1,0:T(8,128)(2,1)} %get-tuple-element.57), kind=kOutput, calls=%fused_computation | convolution fusion | flops 8594128896 | bytes 16777216 | tf_op jit(solution)/shard_map/dot_general | solution.py:40
  492.0 1.6 copy-done.5
  493.5 5.6 convolution_convert_fusion.out_grad
  499.1 30.1 %attention_back.1 = (bf16[1024,1536]{1,0:T(8,128)(2,1)}, f32[1,512]{1,0:T(1,128)}, f32[1,512]{1,0:T(1,128)}) custom-call(f32[1024,1536]{1,0:T(8,128)} %get-tuple-element.44.q_raw.k_raw.v_raw.qkv, bf16[1024,512]{1,0:T(8,128)(2,1)} %get-tuple-element.52.q_low, bf16[1024,512]{1,0:T(8,128)(2,1)} %get-tuple-element.53.k_low, ...), custom_call_target="tpu_custom_call" | custom-call | flops 30000001024 | bytes 90000000 | tf_op jit(solution)/shard_map/attention_back/pallas_call | solution.py:1502
  529.2 85.7 %last_grads.1 = (f32[256,2048]{1,0:T(8,128)}, f32[256,1536]{1,0:T(8,128)}, f32[512,256]{1,0:T(8,128)}, f32[1,1536]{1,0:T(1,128)}) custom-call(bf16[1024,1536]{1,0:T(8,128)(2,1)} %get-tuple-element.60.grads, bf16[2048,1536]{1,0:T(8,128)(2,1)} %get-tuple-element.61.weight, f32[256,2048]{1,0:T(8,128)} %get-tuple-element.62.base, bf16[1024,2048]{1,0:T(8,128)(2,1)} %bitcast.59, ...), custom_call_target="tpu_custom_call" | custom-call | flops 80000000000 | bytes 240000000 | tf_op jit(solution)/shard_map/last_grads/pallas_call | solution.py:1296
  615.0 0.8 slice_reduce_fusion
  616.5 1.2 fusion.6
  617.6 2.7 fusion.4
  620.3 2.8 convert_element_type.37
  623.1 1.0 copy.63
  624.1 1.3 copy.64
  625.4 0.8 copy.65
  626.2 1.3 copy.66
  627.5 1.3 copy.67
  (38 shorter events, 9.0 us)
Async XLA Ops:
  7.2 613.2 %reduce-scatter.2.cloned.1.call-start = ((), (), s32[]{:S(2)}) async-start(), calls=%async_computation.1 | async-start | bytes 9437184 | tf_op jit(solution)/shard_map/reduce_scatter | solution.py:1591
  491.9 1.6 copy-start.5
  615.0 8.1 %copy-start.3 = (bf16[256,2048]{1,0:T(8,128)(2,1)S(1)}, bf16[256,2048]{1,0:T(8,128)(2,1)}, u32[]{:S(2)}) copy-start(bf16[256,2048]{1,0:T(8,128)(2,1)} %get-tuple-element.106) | copy-start | bytes 3145732
  617.6 6.4 %copy-start.2 = (f32[256,2048]{1,0:T(8,128)S(1)}, f32[256,2048]{1,0:T(8,128)}, u32[]{:S(2)}) copy-start(f32[256,2048]{1,0:T(8,128)} %get-tuple-element.107) | copy-start | bytes 6291460
  620.3 5.1 copy-start.4
  623.1 3.1 copy-start.1
  624.1 3.4 copy-start
Sparse Core Ops, SparseCore 0:
  492.1 75.6 reduce-scatter.1

commit v7 on v6

--- a/solution.py
+++ b/solution.py
@@ -16,6 +16,7 @@
 EDGES = False
 FILL = 2
 PERIOD = 8
+LINE_FROM = 8
 HOOKS = (3, 7, 10, 13, 16)
 TILE = 512
 QUERY_ROWS = 256
@@ -1115,11 +1116,13 @@
 
 
 def last_grads_kernel(
-    n, n_dp, rows, grads, weight, base, inputs, att, da, attn_gain, mlp_gain, q_gain, k_gain,
-    input_grad, qkv_out, out_out, gain_out,
+    n, n_dp, rows, grads, weight, base, inputs, att, da, hidden, dm,
+    attn_gain, mlp_gain, q_gain, k_gain,
+    input_grad, qkv_out, out_out, down_out, gain_out,
     part, recv, rs_send_sem, rs_recv_sem, total, packed,
-    x_buf, da_buf, load_sem,
-    send_qkv, recv_qkv, held_qkv, message_qkv, send_out, recv_out, held_out, message_out,
+    x_buf, da_buf, dm_buf, load_sem, v_hidden, hidden_sem,
+    send_qkv, recv_qkv, message_qkv, send_out, recv_out, message_out,
+    send_down, recv_down, message_down,
     gains, gain_recv, gain_send_sem, gain_recv_sem, mp_recv, mp_send_sem, mp_recv_sem, *plane,
 ):
     me, at = lax.axis_index("mp"), lax.axis_index("dp")
@@ -1130,34 +1133,45 @@
     chips = n_dp // 2
     part_width = width // n_dp
     order = relative_order(chips)
-    jobs = [(same_core, r) for same_core in (False, True) for r in order]
-
-    def views(send, recv, held, message):
+
+    def views(send, recv, message):
         return (
             lambda r: send.at[r],
             lambda r: recv.at[r],
-            lambda r: held.at[r - 1],
+            lambda r: send.at[r],
             lambda r: message.at[r - 1],
         )
 
     by_qkv = PlaneReduce(
-        at, chips, part_width, views(send_qkv, recv_qkv, held_qkv, message_qkv), plane[:4], qkv_out
+        at, chips, part_width, views(send_qkv, recv_qkv, message_qkv), plane[:4], qkv_out
     )
     by_out = PlaneReduce(
-        at, chips, local_width, views(send_out, recv_out, held_out, message_out), plane[4:], out_out
-    )
+        at, chips, local_width, views(send_out, recv_out, message_out), plane[4:8], out_out
+    )
+    by_down = PlaneReduce(
+        at, chips, part_width, views(send_down, recv_down, message_down), plane[8:], down_out
+    )
+    jobs = [
+        (down, same_core, r)
+        for down in (True, False)
+        for same_core in (False, True)
+        for r in order
+    ]
 
     def loads(k):
-        same_core, r = jobs[k]
+        down, same_core, r = jobs[k]
         first = by_qkv.owner(r, same_core) * part_width
         cols = pl.ds(pl.multiple_of(first, part_width), part_width)
+        pairs = ((dm, dm_buf),) if down else ((inputs, x_buf), (da, da_buf))
         return [
-            pltpu.make_async_copy(inputs.at[:, cols], x_buf.at[k % 2], load_sem.at[k % 2, 0]),
-            pltpu.make_async_copy(da.at[:, cols], da_buf.at[k % 2], load_sem.at[k % 2, 1]),
+            pltpu.make_async_copy(source.at[:, cols], buf.at[k % 2], load_sem.at[k % 2, which])
+            for which, (source, buf) in enumerate(pairs)
         ]
 
+    load_hidden = pltpu.make_async_copy(hidden, v_hidden, hidden_sem)
     for copy in loads(0):
         copy.start()
+    load_hidden.start()
 
     def compute(c):
         for j in range(n):
@@ -1178,16 +1192,20 @@
         input_grad[span] = base[span] + total[...]
 
     def weight_block(k):
-        same_core, r = jobs[k]
+        down, same_core, r = jobs[k]
         slot = k % 2
+        reduces = (by_down,) if down else (by_qkv, by_out)
         for copy in loads(k):
             copy.wait()
         if k + 1 < len(jobs):
             for copy in loads(k + 1):
                 copy.start()
+        if k == 0:
+            load_hidden.wait()
         if same_core:
-            by_qkv.core_copy(r).wait_recv()
-            by_out.core_copy(r).wait_recv()
+            for reduce in reduces:
+                reduce.core_copy(r).wait_recv()
+                reduce.drain_core(r)
 
         def keep(reduce, block, cols):
             if not same_core:
@@ -1199,18 +1217,34 @@
             else:
                 reduce.out[:, cols] = block
 
-        @pl.loop(0, 3)
-        def _(tile):
-            cols = pl.ds(pl.multiple_of(tile * local_width, local_width), local_width)
-            keep(by_qkv, inner_dot(x_buf[slot], grads[:, cols]), cols)
-
-        keep(by_out, inner_dot(att[...], da_buf[slot]), slice(None))
-        for reduce in (by_qkv, by_out):
+        if down:
+
+            @pl.loop(0, hidden.shape[1] // TILE)
+            def _(tile):
+                cols = pl.ds(pl.multiple_of(tile * TILE, TILE), TILE)
+                keep(by_down, inner_dot(dm_buf[slot], v_hidden[:, cols]), cols)
+
+        else:
+
+            @pl.loop(0, 3)
+            def _(tile):
+                cols = pl.ds(pl.multiple_of(tile * local_width, local_width), local_width)
+                keep(by_qkv, inner_dot(x_buf[slot], grads[:, cols]), cols)
+
+            keep(by_out, inner_dot(att[...], da_buf[slot]), slice(None))
+        for reduce in reduces:
             if not same_core:
                 reduce.core_copy(r).start()
             elif r > 0:
                 for half in range(2):
                     if not reduce.before(r, half):
+                        reduce.push(r, half)
+
+    def push_late(reduces):
+        for r in order:
+            for half in range(2):
+                if r > 0 and reduces[0].before(r, half):
+                    for reduce in reduces:
                         reduce.push(r, half)
 
     for index in range(n_dp):
@@ -1244,19 +1278,18 @@
     send_edges(0)
     for copy in gain_copies:
         copy.start()
-    blocks = iter(range(len(jobs)))
-    for c in range(1, CHUNKS):
-        weight_block(next(blocks))
-        compute(c)
-        send_edges(c)
-    for k in blocks:
+    sent = 1
+    for k in range(len(jobs)):
         weight_block(k)
-        line_steps(2)
-    late = [(r, half) for r in order for half in range(2) if r > 0 and by_qkv.before(r, half)]
-    for r, half in late:
-        for reduce in (by_qkv, by_out):
-            reduce.push(r, half)
-        line_steps(1)
+        if k % 4 == 3 and sent < CHUNKS:
+            compute(sent)
+            send_edges(sent)
+            sent += 1
+        if k >= LINE_FROM:
+            line_steps(1)
+        if k == 3 * chips:
+            push_late((by_down,))
+    push_late((by_qkv, by_out))
     gain_out[...] = gains[at]
     for shift, copy in enumerate(gain_copies, 1):
         copy.wait_recv()
@@ -1264,7 +1297,7 @@
     for copy in mp_copies:
         copy.start()
     line_steps(n * CHUNKS)
-    for reduce in (by_qkv, by_out):
+    for reduce in (by_down, by_qkv, by_out):
         reduce.finish()
     for copy in mp_copies:
         copy.wait_recv()
@@ -1278,13 +1311,11 @@
         copy.wait_send()
     for c in range(CHUNKS):
         scatter.drain(c)
-    for reduce in (by_qkv, by_out):
-        for r in range(chips):
-            reduce.drain_core(r)
+    for reduce in (by_down, by_qkv, by_out):
         reduce.drain()
 
 
-def last_grads(n, n_dp, grads, weight, base, inputs, attended, da_full, *gains):
+def last_grads(n, n_dp, grads, weight, base, inputs, attended, da_full, hidden, dm, *gains):
     row_count, width = base.shape
     rows = row_count // CHUNKS
     size, local_width = attended.shape
@@ -1292,6 +1323,7 @@
     chips = n_dp // 2
     qkv_block = (part_width, 3 * local_width)
     out_block = (local_width, part_width)
+    down_block = (part_width, hidden.shape[1])
     gain_block = (1, 2 * part_width + 2 * local_width)
     return pl.pallas_call(
         functools.partial(last_grads_kernel, n, n_dp, rows),
@@ -1299,33 +1331,37 @@
             jax.ShapeDtypeStruct((row_count, width), F32),
             jax.ShapeDtypeStruct(qkv_block, F32),
             jax.ShapeDtypeStruct(out_block, F32),
+            jax.ShapeDtypeStruct(down_block, F32),
             jax.ShapeDtypeStruct(gain_block, F32),
         ),
-        in_specs=[VMEM, VMEM, VMEM, HBM, VMEM, HBM] + [VMEM] * 4,
-        out_specs=(VMEM,) * 4,
+        in_specs=[VMEM, VMEM, VMEM, HBM, VMEM, HBM, HBM, HBM] + [VMEM] * 4,
+        out_specs=(VMEM,) * 5,
         scratch_shapes=scatter_scratch(n, rows, width)
         + [
             pltpu.VMEM((n * rows, 3 * local_width), BF),
             pltpu.VMEM((2, size, part_width), BF),
             pltpu.VMEM((2, size, part_width), BF),
+            pltpu.VMEM((2, size, part_width), BF),
             pltpu.SemaphoreType.DMA((2, 2)),
+            pltpu.VMEM(hidden.shape, BF),
+            pltpu.SemaphoreType.DMA,
         ]
         + [
             pltpu.VMEM((count,) + block, BF)
-            for block in (qkv_block, out_block)
-            for count in (chips, chips, chips - 1, chips - 1)
+            for block in (qkv_block, out_block, down_block)
+            for count in (chips, chips, chips - 1)
         ]
         + [pltpu.VMEM((n_dp,) + gain_block, F32), pltpu.VMEM((n_dp - 1,) + gain_block, F32)]
         + [pltpu.SemaphoreType.DMA((n_dp - 1,))] * 2
         + [pltpu.VMEM((n - 1,) + gain_block, F32)]
         + [pltpu.SemaphoreType.DMA((n - 1,))] * 2
-        + plane_sems(chips) * 2,
+        + plane_sems(chips) * 3,
         compiler_params=pltpu.CompilerParams(
             collective_id=4, has_side_effects=True, vmem_limit_bytes=63 * MIB
         ),
         name="last_grads",
         cost_estimate=cost(80),
-    )(grads, weight, base, inputs, attended, da_full, *gains)
+    )(grads, weight, base, inputs, attended, da_full, hidden, dm, *gains)
 
 
 def turn(values, cos, sin):
@@ -1586,19 +1622,16 @@
         return rows.reshape(group_size, rows.shape[-1])
 
     branch_full = flat(branch_full)
-    down_part = inner_dot(flat(hidden), flat(mlp_grad_full)).astype(BF)
-    branch_full, down_part = lax.optimization_barrier((branch_full, down_part))
-    grad_down = lax.psum_scatter(down_part, "dp", scatter_dimension=1, tiled=True)
-
     mixed_grad = outer_dot(branch_full, full_out).astype(BF)
     qkv_grad, query_gain_part, key_gain_part = attention_back(
         n, local_heads, model_width, qkv_raw, query_low, key_low, value_low, mixed_grad, log_total,
         query_inv, key_inv, query_scale, key_scale, cos_table, sin_table, starts,
     )
 
-    input_grad, grad_qkv, grad_out, gain_sums = last_grads(
+    input_grad, grad_qkv, grad_out, grad_down, gain_sums = last_grads(
         n, n_dp, qkv_grad, full_qkv, middle_grad, inputs_full, attended, branch_full,
-        attn_gain_part, mlp_gain_part, query_gain_part, key_gain_part,
+        flat(hidden), flat(mlp_grad_full), attn_gain_part, mlp_gain_part, query_gain_part,
+        key_gain_part,
     )
     gain_sums = gain_sums[0]
     heads_at = 2 * width_part
@@ -1617,7 +1650,7 @@
         grad_out,
         grad_gate,
         grad_up,
-        grad_down.astype(F32),
+        grad_down.T,
         head_sums[0],
         head_sums[1],
         gain_sums[:width_part],

time: 645 us -> 624 us (0.967)
  matrix products: 20.1 us -> 6.21 us
  between operations: 14.3 us -> 0.98 us
  Pallas kernels: 570 us -> 581 us
    dot_general x1 -> x0, matrix products: 14.5 us -> none  [inner_dot(): lax.dot_general(former, latter, (((0,), (0,)), ((), ())), preferred_eleme...]
    pallas_call x1, Pallas kernels: 85.7 us -> 97.1 us  [last_grads(): pl.pallas_call(functools.partial(last_grads_kernel, n, n_dp, rows), out_s...]
  transfers between devices with their start and end apart: 1 -> 0, of which waited for: 0 -> 0; matrix products, arithmetic and copies ran while one was open for 2% -> 0% of each run, Pallas kernels for 18% -> 0%
where the time goes in v7:
time: 624 us; the launch traced here: 615 us
  Pallas kernels  581 us (93%)
  local copies, waits for them, and re-layouts  20.3 us (3%)
  other arithmetic  6.91 us (1%)
    pallas_call x1, Pallas kernels, middle(): pl.pallas_call(functools.partial(middle_kernel, n, n_dp, rows), out_shape...  347 us
    pallas_call x1, Pallas kernels, last_grads(): pl.pallas_call(functools.partial(last_grads_kernel, n, n_dp, rows), out_s...  97.1 us
    pallas_call x1, Pallas kernels, front(): pl.pallas_call(functools.partial(front_kernel, n, n_dp, rows, model_width...  88.8 us
    pallas_call x1, Pallas kernels, attention_back(): pl.pallas_call(functools.partial(attention_back_kernel, n, heads, model_w...  30 us
    pallas_call x1, Pallas kernels, attention(): pl.pallas_call(attention_kernel, grid=(heads,), out_shape=(low, low, low,...  18 us

profile of v7, /device:TPU:0, one launch (start us, length us, event | category | flops | bytes accessed | tf_op | source)
XLA Modules:
  0.0 615.4 jit_solution(2939405520440408783)
XLA Ops:
  0.6 0.8 reduce-window.4
  1.6 0.7 fusion.3
  3.6 1.9 fusion
  5.5 1.3 pad_maximum_fusion
  6.8 1.0 copy.40.starts
  8.1 0.7 maximum_convert_fusion.gains
  8.7 88.8 %front.1 = (bf16[4,256,2048]{2,1,0:T(8,128)(2,1)}, f32[1024,1536]{1,0:T(8,128)}, bf16[2048,1536]{1,0:T(8,128)(2,1)}, bf16[512,2048]{1,0:T(8,128)(2,1)}, f32[8,1,...) custom-call(bf16[256,2048]{1,0:T(8,128)(2,1)} %x.3, bf16[256,512]{1,0:T(8,128)(2,1)} %wq.1, ...), custom_call_target="tpu_custom_call" | custom-call | flops 80000000000 | bytes 240000000 | tf_op jit(solution)/shard_map/front/pallas_call | solution.py:657
  97.5 0.7 copy.54
  98.4 0.7 reshape.177.q_gain
  99.2 0.7 reshape.179.k_gain
  99.8 18.0 %attention.1 = (bf16[1024,512]{1,0:T(8,128)(2,1)}, bf16[1024,512]{1,0:T(8,128)(2,1)}, bf16[1024,512]{1,0:T(8,128)(2,1)}, bf16[1024,512]{1,0:T(8,128)(2,1)}, f32[4,1024,1]{2,1,0:T(8,128)}) custom-call(f32[1024,1536]{1,0:T(8,128)} %get-tuple-element.43.q_raw.k_raw.v_raw.qkv, f32[1024,1536]{1,0:T(8,128)} %get-tuple-element.43.q_raw.k_raw.v_raw.qkv, ...), custom_call_target="tpu_custom_call" | custom-call | flops 17999998976 | bytes 54000000 | tf_op jit(solution)/shard_map/attention/pallas_call | solution.py:1447
  118.6 0.8 copy.41.row_valid
  120.6 347.0 %middle.1 = (bf16[4,256,2048]{2,1,0:T(8,128)(2,1)}, bf16[256,2048]{1,0:T(8,128)(2,1)}, bf16[4,256,2048]{2,1,0:T(8,128)(2,1)}, bf16[4,256,2048]{2,1,0:T(8,128)(2,...) custom-call(bf16[1024,512]{1,0:T(8,128)(2,1)} %get-tuple-element.47., ...), custom_call_target="tpu_custom_call" | custom-call | flops 349999988736 | bytes 1050000000 | tf_op jit(solution)/shard_map/middle/pallas_call | solution.py:1070
  467.6 6.2 %convolution_convert_fusion.out_grad = bf16[1024,512]{1,0:T(8,128)(2,1)} fusion(bf16[1024,2048]{1,0:T(8,128)(2,1)} %bitcast.62, bf16[512,2048]{1,0:T(8,128)(2,1)} %get-tuple-element.48.wo), kind=kOutput, calls=%fused_computation | convolution fusion | flops 2148007936 | bytes 7340032 | tf_op jit(solution)/shard_map/dot_general | solution.py:47
  473.8 30.0 %attention_back.1 = (bf16[1024,1536]{1,0:T(8,128)(2,1)}, f32[1,512]{1,0:T(1,128)}, f32[1,512]{1,0:T(1,128)}) custom-call(f32[1024,1536]{1,0:T(8,128)} %get-tuple-element.43.q_raw.k_raw.v_raw.qkv, bf16[1024,512]{1,0:T(8,128)(2,1)} %get-tuple-element.51.q_low, bf16[1024,512]{1,0:T(8,128)(2,1)} %get-tuple-element.52.k_low, ...), custom_call_target="tpu_custom_call" | custom-call | flops 30000001024 | bytes 90000000 | tf_op jit(solution)/shard_map/attention_back/pallas_call | solution.py:1538
  503.9 97.1 %last_grads.1 = (f32[256,2048]{1,0:T(8,128)}, f32[256,1536]{1,0:T(8,128)}, f32[512,256]{1,0:T(8,128)}, f32[256,2048]{1,0:T(8,128)}, f32[1,1536]{1,0:T(1,128)}) custom-call(bf16[1024,1536]{1,0:T(8,128)(2,1)} %get-tuple-element.56.grads, bf16[2048,1536]{1,0:T(8,128)(2,1)} %get-tuple-element.57.weight, f32[256,2048]{1,0:T(8,128)} %get-tuple-element.58.base, ...), custom_call_target="tpu_custom_call" | custom-call | flops 80000000000 | bytes 240000000 | tf_op jit(solution)/shard_map/last_grads/pallas_call | solution.py:1328
  601.0 2.9 copy.44
  603.9 2.7 fusion.4
  607.8 1.0 copy.62
  608.8 1.3 copy.63
  610.2 0.8 copy.64
  611.5 1.3 copy.65
  612.8 1.0 copy-done
  613.8 1.3 copy.66
  (42 shorter events, 5.6 us)
Async XLA Ops:
  3.6 4.3 copy-start.8
  3.6 4.3 copy-start.9
  3.6 4.3 copy-start.6
  3.6 4.4 copy-start.7
  603.9 2.7 copy-start.5
  603.9 3.9 copy-start.3
  603.9 4.9 copy-start.2
  608.8 1.4 copy-start.4
  608.8 2.7 copy-start.1
  611.5 2.3 copy-start

commit v8 on v7

--- a/solution.py
+++ b/solution.py
@@ -16,7 +16,7 @@
 EDGES = False
 FILL = 2
 PERIOD = 8
-LINE_FROM = 8
+LINE_FROM = 11
 HOOKS = (3, 7, 10, 13, 16)
 TILE = 512
 QUERY_ROWS = 256
@@ -511,9 +511,9 @@
 
 def front_kernel(
     n, n_dp, rows, model_width, x, wq, wk, wv, wo, gains, wg,
-    full, qkv, full_qkv, full_out, gain_parts, q_inv, k_inv, full_gate,
+    full, qkv_out, full_qkv, full_out, gain_parts, attn_scale, mlp_scale, q_inv, k_inv, full_gate,
     send_sem, recv_sem, local_sem, gain_recv, gain_send_sem, gain_recv_sem,
-    vqkv, vout, save_sem, x_buf, x_sem, squares,
+    vqkv, vout, qkv, save_sem, x_buf, x_sem, squares,
     held, sum_recv, turned, sum_send_sem, sum_recv_sem, gate_sem, *plane,
 ):
     me, at = lax.axis_index("mp"), lax.axis_index("dp")
@@ -566,6 +566,7 @@
             qkv[here, cols] = value
             squares[tile] = jnp.sum(value * value, axis=1, keepdims=True)
 
+        pltpu.make_async_copy(qkv.at[here], qkv_out.at[here], save_sem.at[2]).start()
         held[:, here] = columns_to_rows(squares[0], squares[1])
 
     def blocks_at(step):
@@ -580,6 +581,7 @@
     saves = [
         pltpu.make_async_copy(vqkv, full_qkv, save_sem.at[0]),
         pltpu.make_async_copy(vout, full_out, save_sem.at[1]),
+        pltpu.make_async_copy(qkv, qkv_out, save_sem.at[2]),
     ]
     early = [r for r in range(1, chips) if len(bits_of(r)) == 1]
     late = [r for r in range(1, chips) if len(bits_of(r)) > 1]
@@ -628,10 +630,15 @@
     while ready < n:
         blocks_at(ready)
         ready += 1
-    gain_parts[at] = gains[...]
+    def keep_gains(owner, row):
+        gain_parts[owner] = row[:, 2 * part_width :]
+        attn_scale[:, part(owner)] = row[:, :part_width]
+        mlp_scale[:, part(owner)] = row[:, part_width : 2 * part_width]
+
+    keep_gains(at, gains[...])
     for shift, copy in enumerate(copies, 1):
         copy.wait_recv()
-        gain_parts[lax.rem(at + n_dp - shift, n_dp)] = gain_recv[shift - 1]
+        keep_gains(lax.rem(at + n_dp - shift, n_dp), gain_recv[shift - 1])
     by_gate.swap(late)
     q_sum, k_sum = sum_held(n, me, held, sum_recv, turned, sum_send_sem, sum_recv_sem)
     q_inv[...] = lax.rsqrt(q_sum / model_width + EPS)
@@ -661,13 +668,15 @@
             jax.ShapeDtypeStruct((size, 3 * width), F32),
             jax.ShapeDtypeStruct((model_width, 3 * width), BF),
             jax.ShapeDtypeStruct((width, model_width), BF),
-            jax.ShapeDtypeStruct((n_dp,) + gains.shape, F32),
+            jax.ShapeDtypeStruct((n_dp, 1, gains.shape[1] - 2 * model_width // n_dp), F32),
+            jax.ShapeDtypeStruct((1, model_width), F32),
+            jax.ShapeDtypeStruct((1, model_width), F32),
             column,
             column,
             jax.ShapeDtypeStruct((model_width, wg.shape[1]), BF),
         ),
         in_specs=[VMEM] * 7,
-        out_specs=(HBM, VMEM, HBM, HBM, VMEM, VMEM, VMEM, HBM),
+        out_specs=(HBM, HBM, HBM, HBM, VMEM, VMEM, VMEM, VMEM, VMEM, HBM),
         scratch_shapes=gather_scratch(n, rows, model_width)[1:]
         + [
             pltpu.VMEM((n_dp - 1,) + gains.shape, F32),
@@ -675,7 +684,8 @@
             pltpu.SemaphoreType.DMA((n_dp - 1,)),
             pltpu.VMEM((model_width, 3 * width), BF),
             pltpu.VMEM((width, model_width), BF),
-            pltpu.SemaphoreType.DMA((2,)),
+            pltpu.VMEM((size, 3 * width), F32),
+            pltpu.SemaphoreType.DMA((3,)),
             pltpu.VMEM((row_count, model_width), BF),
             pltpu.SemaphoreType.DMA,
             pltpu.VMEM((3, row_count, 1), F32),
@@ -1585,7 +1595,10 @@
     own_gains = jnp.concatenate(
         [attn_gain, mlp_gain, query_gain.reshape(head_part), key_gain.reshape(head_part)]
     ).astype(F32)[None]
-    inputs_full, qkv_raw, full_qkv, full_out, gain_parts, query_inv, key_inv, full_gate = front(
+    (
+        inputs_full, qkv_raw, full_qkv, full_out, gain_parts, attn_scale, mlp_scale, query_inv,
+        key_inv, full_gate,
+    ) = front(
         n, n_dp, layer_input, query_weight, key_weight, value_weight, out_weight, own_gains,
         gate_weight,
     )
@@ -1596,10 +1609,8 @@
         piece = gain_parts[:, first : first + head_part].reshape(n_dp, local_heads, gain_part)
         return piece.transpose(1, 0, 2).reshape(1, local_width)
 
-    query_scale = head_gain(2 * width_part)
-    key_scale = head_gain(2 * width_part + head_part)
-    attn_scale = gain_parts[:, :width_part].reshape(1, model_width)
-    mlp_scale = gain_parts[:, width_part : 2 * width_part].reshape(1, model_width)
+    query_scale = head_gain(0)
+    key_scale = head_gain(head_part)
 
     starts, positions, valid = layout(seq_lens[0], group_size)
     starts = starts[:, None]

time: 624 us -> 618 us (level)
  Pallas kernels: 581 us -> 573 us
where the time goes in v8:
time: 618 us; the launch traced here: 607 us
  Pallas kernels  573 us (93%)
  local copies, waits for them, and re-layouts  19.1 us (3%)
  other arithmetic  6.91 us (1%)
  matrix products  6.21 us (1%)
    pallas_call x1, Pallas kernels, middle(): pl.pallas_call(functools.partial(middle_kernel, n, n_dp, rows), out_shape...  347 us
    pallas_call x1, Pallas kernels, last_grads(): pl.pallas_call(functools.partial(last_grads_kernel, n, n_dp, rows), out_s...  91.5 us
    pallas_call x1, Pallas kernels, front(): pl.pallas_call(functools.partial(front_kernel, n, n_dp, rows, model_width...  86.9 us
    pallas_call x1, Pallas kernels, attention_back(): pl.pallas_call(functools.partial(attention_back_kernel, n, heads, model_w...  30.2 us
    pallas_call x1, Pallas kernels, attention(): pl.pallas_call(attention_kernel, grid=(heads,), out_shape=(low, low, low,...  18 us

profile of v8, /device:TPU:0, one launch (start us, length us, event | category | flops | bytes accessed | tf_op | source)
XLA Modules:
  0.0 606.6 jit_solution(17278310827244707492)
XLA Ops:
  0.6 0.8 reduce-window.4
  1.6 0.7 fusion.3
  3.6 1.9 fusion
  5.5 1.3 pad_maximum_fusion
  6.8 1.0 copy.40.starts
  8.1 0.7 maximum_convert_fusion.gains
  8.7 86.9 %front.1 = (bf16[4,256,2048]{2,1,0:T(8,128)(2,1)}, f32[1024,1536]{1,0:T(8,128)}, bf16[2048,1536]{1,0:T(8,128)(2,1)}, bf16[512,2048]{1,0:T(8,128)(2,1)}, f32[8,1,...) custom-call(bf16[256,2048]{1,0:T(8,128)(2,1)} %x.3, ...), custom_call_target="tpu_custom_call" | custom-call | flops 80000000000 | bytes 240000000 | tf_op jit(solution)/shard_map/front/pallas_call | solution.py:664
  95.6 0.8 fusion.6
  96.5 0.7 reshape.171.q_gain
  97.3 0.7 reshape.173.k_gain
  97.9 18.0 %attention.1 = (bf16[1024,512]{1,0:T(8,128)(2,1)}, bf16[1024,512]{1,0:T(8,128)(2,1)}, bf16[1024,512]{1,0:T(8,128)(2,1)}, bf16[1024,512]{1,0:T(8,128)(2,1)}, f32[4,1024,1]{2,1,0:T(8,128)}) custom-call(f32[1024,1536]{1,0:T(8,128)} %get-tuple-element.45.q_raw.k_raw.v_raw.qkv, f32[1024,1536]{1,0:T(8,128)} %get-tuple-element.45.q_raw.k_raw.v_raw.qkv, ...), custom_call_target="tpu_custom_call" | custom-call | flops 17999998976 | bytes 54000000 | tf_op jit(solution)/shard_map/attention/pallas_call | solution.py:1457
  116.7 0.8 copy.41.row_valid
  117.5 346.7 %middle.1 = (bf16[4,256,2048]{2,1,0:T(8,128)(2,1)}, bf16[256,2048]{1,0:T(8,128)(2,1)}, bf16[4,256,2048]{2,1,0:T(8,128)(2,1)}, bf16[4,256,2048]{2,1,0:T(8,128)(2,...) custom-call(bf16[1024,512]{1,0:T(8,128)(2,1)} %get-tuple-element.49., ...), custom_call_target="tpu_custom_call" | custom-call | flops 349999988736 | bytes 1050000000 | tf_op jit(solution)/shard_map/middle/pallas_call | solution.py:1080
  464.3 6.2 %convolution_convert_fusion.out_grad = bf16[1024,512]{1,0:T(8,128)(2,1)} fusion(bf16[1024,2048]{1,0:T(8,128)(2,1)} %bitcast.49, bf16[512,2048]{1,0:T(8,128)(2,1)} %get-tuple-element.50.wo), kind=kOutput, calls=%fused_computation | convolution fusion | flops 2148007936 | bytes 7340032 | tf_op jit(solution)/shard_map/dot_general | solution.py:47
  470.5 30.2 %attention_back.1 = (bf16[1024,1536]{1,0:T(8,128)(2,1)}, f32[1,512]{1,0:T(1,128)}, f32[1,512]{1,0:T(1,128)}) custom-call(f32[1024,1536]{1,0:T(8,128)} %get-tuple-element.45.q_raw.k_raw.v_raw.qkv, bf16[1024,512]{1,0:T(8,128)(2,1)} %get-tuple-element.55.q_low, bf16[1024,512]{1,0:T(8,128)(2,1)} %get-tuple-element.56.k_low, ...), custom_call_target="tpu_custom_call" | custom-call | flops 30000001024 | bytes 90000000 | tf_op jit(solution)/shard_map/attention_back/pallas_call | solution.py:1548
  500.7 91.5 %last_grads.1 = (f32[256,2048]{1,0:T(8,128)}, f32[256,1536]{1,0:T(8,128)}, f32[512,256]{1,0:T(8,128)}, f32[256,2048]{1,0:T(8,128)}, f32[1,1536]{1,0:T(1,128)}) custom-call(bf16[1024,1536]{1,0:T(8,128)(2,1)} %get-tuple-element.60.grads, bf16[2048,1536]{1,0:T(8,128)(2,1)} %get-tuple-element.61.weight, f32[256,2048]{1,0:T(8,128)} %get-tuple-element.62.base, ...), custom_call_target="tpu_custom_call" | custom-call | flops 80000000000 | bytes 240000000 | tf_op jit(solution)/shard_map/last_grads/pallas_call | solution.py:1338
  592.3 2.9 copy.44
  595.1 2.7 fusion.4
  599.1 1.0 copy.57
  600.1 1.3 copy.58
  601.4 0.8 copy.59
  602.8 1.3 copy.60
  604.1 1.0 copy-done
  605.1 1.3 copy.61
  (38 shorter events, 4.4 us)
Async XLA Ops:
  3.6 4.3 copy-start.8
  3.6 4.3 copy-start.9
  3.6 4.3 copy-start.6
  3.6 4.4 copy-start.7
  595.1 2.7 copy-start.5
  595.1 3.9 copy-start.3
  595.1 4.9 copy-start.2
  600.1 1.4 copy-start.4
  600.1 2.7 copy-start.1
  602.8 2.3 copy-start

commit v9 on v8

--- a/solution.py
+++ b/solution.py
@@ -19,7 +19,8 @@
 LINE_FROM = 11
 HOOKS = (3, 7, 10, 13, 16)
 TILE = 512
-QUERY_ROWS = 256
+QUERY_ROWS = 512
+BACK_ROWS = 256
 BF = jnp.bfloat16
 F32 = jnp.float32
 MIB = 1 << 20
@@ -1479,7 +1480,7 @@
     width = qkv.shape[1] // 3
     head = width // heads
     score_scale = 1.0 / math.sqrt(head)
-    rows = min(QUERY_ROWS, size)
+    rows = min(BACK_ROWS, size)
     q_dots[...] = jnp.zeros_like(q_dots)
     k_dots[...] = jnp.zeros_like(k_dots)
 

time: 618 us -> 612 us (level)
  no operation moved by 1% of the time
where the time goes in v9:
time: 612 us; the launch traced here: 604 us
  Pallas kernels  570 us (93%)
  local copies, waits for them, and re-layouts  19.1 us (3%)
  other arithmetic  6.91 us (1%)
  matrix products  6.21 us (1%)
    pallas_call x1, Pallas kernels, middle(): pl.pallas_call(functools.partial(middle_kernel, n, n_dp, rows), out_shape...  348 us
    pallas_call x1, Pallas kernels, last_grads(): pl.pallas_call(functools.partial(last_grads_kernel, n, n_dp, rows), out_s...  91.5 us
    pallas_call x1, Pallas kernels, front(): pl.pallas_call(functools.partial(front_kernel, n, n_dp, rows, model_width...  86.9 us
    pallas_call x1, Pallas kernels, attention_back(): pl.pallas_call(functools.partial(attention_back_kernel, n, heads, model_w...  28.5 us
    pallas_call x1, Pallas kernels, attention(): pl.pallas_call(attention_kernel, grid=(heads,), out_shape=(low, low, low,...  15.5 us

profile of v9, /device:TPU:0, one launch (start us, length us, event | category | flops | bytes accessed | tf_op | source)
XLA Modules:
  0.0 603.6 jit_solution(14705501470531805931)
XLA Ops:
  0.6 0.8 reduce-window.4
  1.6 0.7 fusion.3
  3.6 1.9 fusion
  5.5 1.3 pad_maximum_fusion
  6.8 1.0 copy.40.starts
  8.1 0.7 maximum_convert_fusion.gains
  8.7 86.9 %front.1 = (bf16[4,256,2048]{2,1,0:T(8,128)(2,1)}, f32[1024,1536]{1,0:T(8,128)}, bf16[2048,1536]{1,0:T(8,128)(2,1)}, bf16[512,2048]{1,0:T(8,128)(2,1)}, f32[8,1,...) custom-call(bf16[256,2048]{1,0:T(8,128)(2,1)} %x.3, ...), custom_call_target="tpu_custom_call" | custom-call | flops 80000000000 | bytes 240000000 | tf_op jit(solution)/shard_map/front/pallas_call | solution.py:665
  95.6 0.8 fusion.6
  96.5 0.7 reshape.171.q_gain
  97.3 0.7 reshape.173.k_gain
  97.9 15.5 %attention.1 = (bf16[1024,512]{1,0:T(8,128)(2,1)}, bf16[1024,512]{1,0:T(8,128)(2,1)}, bf16[1024,512]{1,0:T(8,128)(2,1)}, bf16[1024,512]{1,0:T(8,128)(2,1)}, f32[4,1024,1]{2,1,0:T(8,128)}) custom-call(f32[1024,1536]{1,0:T(8,128)} %get-tuple-element.45.q_raw.k_raw.v_raw.qkv, f32[1024,1536]{1,0:T(8,128)} %get-tuple-element.45.q_raw.k_raw.v_raw.qkv, ...), custom_call_target="tpu_custom_call" | custom-call | flops 17999998976 | bytes 54000000 | tf_op jit(solution)/shard_map/attention/pallas_call | solution.py:1458
  114.2 0.8 copy.41.row_valid
  115.0 348.1 %middle.1 = (bf16[4,256,2048]{2,1,0:T(8,128)(2,1)}, bf16[256,2048]{1,0:T(8,128)(2,1)}, bf16[4,256,2048]{2,1,0:T(8,128)(2,1)}, bf16[4,256,2048]{2,1,0:T(8,128)(2,...) custom-call(bf16[1024,512]{1,0:T(8,128)(2,1)} %get-tuple-element.49., ...), custom_call_target="tpu_custom_call" | custom-call | flops 349999988736 | bytes 1050000000 | tf_op jit(solution)/shard_map/middle/pallas_call | solution.py:1081
  463.1 6.2 %convolution_convert_fusion.out_grad = bf16[1024,512]{1,0:T(8,128)(2,1)} fusion(bf16[1024,2048]{1,0:T(8,128)(2,1)} %bitcast.49, bf16[512,2048]{1,0:T(8,128)(2,1)} %get-tuple-element.50.wo), kind=kOutput, calls=%fused_computation | convolution fusion | flops 2148007936 | bytes 7340032 | tf_op jit(solution)/shard_map/dot_general | solution.py:48
  469.3 28.5 %attention_back.1 = (bf16[1024,1536]{1,0:T(8,128)(2,1)}, f32[1,512]{1,0:T(1,128)}, f32[1,512]{1,0:T(1,128)}) custom-call(f32[1024,1536]{1,0:T(8,128)} %get-tuple-element.45.q_raw.k_raw.v_raw.qkv, bf16[1024,512]{1,0:T(8,128)(2,1)} %get-tuple-element.55.q_low, bf16[1024,512]{1,0:T(8,128)(2,1)} %get-tuple-element.56.k_low, ...), custom_call_target="tpu_custom_call" | custom-call | flops 30000001024 | bytes 90000000 | tf_op jit(solution)/shard_map/attention_back/pallas_call | solution.py:1549
  497.7 91.5 %last_grads.1 = (f32[256,2048]{1,0:T(8,128)}, f32[256,1536]{1,0:T(8,128)}, f32[512,256]{1,0:T(8,128)}, f32[256,2048]{1,0:T(8,128)}, f32[1,1536]{1,0:T(1,128)}) custom-call(bf16[1024,1536]{1,0:T(8,128)(2,1)} %get-tuple-element.60.grads, bf16[2048,1536]{1,0:T(8,128)(2,1)} %get-tuple-element.61.weight, f32[256,2048]{1,0:T(8,128)} %get-tuple-element.62.base, ...), custom_call_target="tpu_custom_call" | custom-call | flops 80000000000 | bytes 240000000 | tf_op jit(solution)/shard_map/last_grads/pallas_call | solution.py:1339
  589.3 2.9 copy.44
  592.2 2.7 fusion.4
  596.1 1.0 copy.57
  597.1 1.3 copy.58
  598.5 0.8 copy.59
  599.8 1.3 copy.60
  601.1 1.0 copy-done
  602.1 1.3 copy.61
  (38 shorter events, 4.4 us)
Async XLA Ops:
  3.6 4.3 copy-start.8
  3.6 4.3 copy-start.9
  3.6 4.3 copy-start.6
  3.6 4.4 copy-start.7
  592.2 2.7 copy-start.5
  592.2 3.9 copy-start.3
  592.2 4.9 copy-start.2
  597.1 1.4 copy-start.4
  597.1 2.7 copy-start.1
  599.8 2.3 copy-start

commit v10 on v9

--- a/solution.py
+++ b/solution.py
@@ -17,7 +17,7 @@
 FILL = 2
 PERIOD = 8
 LINE_FROM = 11
-HOOKS = (3, 7, 10, 13, 16)
+HOOKS = (4, 8, 11, 14, 17)
 TILE = 512
 QUERY_ROWS = 512
 BACK_ROWS = 256

time: 612 us -> 608 us (level)
    pallas_call x1, Pallas kernels: 348 us -> 338 us  [middle(): pl.pallas_call(functools.partial(middle_kernel, n, n_dp, rows), out_shape...]
    pallas_call x1, Pallas kernels: 91.5 us -> 98.1 us  [last_grads(): pl.pallas_call(functools.partial(last_grads_kernel, n, n_dp, rows), out_s...]
where the time goes in v10:
time: 608 us; the launch traced here: 599 us
  Pallas kernels  566 us (93%)
  local copies, waits for them, and re-layouts  19.1 us (3%)
  other arithmetic  6.91 us (1%)
  matrix products  6.21 us (1%)
    pallas_call x1, Pallas kernels, middle(): pl.pallas_call(functools.partial(middle_kernel, n, n_dp, rows), out_shape...  338 us
    pallas_call x1, Pallas kernels, last_grads(): pl.pallas_call(functools.partial(last_grads_kernel, n, n_dp, rows), out_s...  98.1 us
    pallas_call x1, Pallas kernels, front(): pl.pallas_call(functools.partial(front_kernel, n, n_dp, rows, model_width...  86.9 us
    pallas_call x1, Pallas kernels, attention_back(): pl.pallas_call(functools.partial(attention_back_kernel, n, heads, model_w...  26.9 us
    pallas_call x1, Pallas kernels, attention(): pl.pallas_call(attention_kernel, grid=(heads,), out_shape=(low, low, low,...  15.5 us

profile of v10, /device:TPU:0, one launch (start us, length us, event | category | flops | bytes accessed | tf_op | source)
XLA Modules:
  0.0 599.0 jit_solution(7916114935879012765)
XLA Ops:
  0.6 0.8 reduce-window.4
  1.6 0.7 fusion.3
  3.6 1.9 fusion
  5.5 1.3 pad_maximum_fusion
  6.8 1.0 copy.40.starts
  8.1 0.7 maximum_convert_fusion.gains
  8.7 86.9 %front.1 = (bf16[4,256,2048]{2,1,0:T(8,128)(2,1)}, f32[1024,1536]{1,0:T(8,128)}, bf16[2048,1536]{1,0:T(8,128)(2,1)}, bf16[512,2048]{1,0:T(8,128)(2,1)}, f32[8,1,...) custom-call(bf16[256,2048]{1,0:T(8,128)(2,1)} %x.3, ...), custom_call_target="tpu_custom_call" | custom-call | flops 80000000000 | bytes 240000000 | tf_op jit(solution)/shard_map/front/pallas_call | solution.py:665
  95.6 0.8 fusion.6
  96.5 0.7 reshape.171.q_gain
  97.3 0.7 reshape.173.k_gain
  97.9 15.5 %attention.1 = (bf16[1024,512]{1,0:T(8,128)(2,1)}, bf16[1024,512]{1,0:T(8,128)(2,1)}, bf16[1024,512]{1,0:T(8,128)(2,1)}, bf16[1024,512]{1,0:T(8,128)(2,1)}, f32[4,1024,1]{2,1,0:T(8,128)}) custom-call(f32[1024,1536]{1,0:T(8,128)} %get-tuple-element.45.q_raw.k_raw.v_raw.qkv, f32[1024,1536]{1,0:T(8,128)} %get-tuple-element.45.q_raw.k_raw.v_raw.qkv, ...), custom_call_target="tpu_custom_call" | custom-call | flops 17999998976 | bytes 54000000 | tf_op jit(solution)/shard_map/attention/pallas_call | solution.py:1458
  114.2 0.8 copy.41.row_valid
  115.0 338.4 %middle.1 = (bf16[4,256,2048]{2,1,0:T(8,128)(2,1)}, bf16[256,2048]{1,0:T(8,128)(2,1)}, bf16[4,256,2048]{2,1,0:T(8,128)(2,1)}, bf16[4,256,2048]{2,1,0:T(8,128)(2,...) custom-call(bf16[1024,512]{1,0:T(8,128)(2,1)} %get-tuple-element.49., ...), custom_call_target="tpu_custom_call" | custom-call | flops 349999988736 | bytes 1050000000 | tf_op jit(solution)/shard_map/middle/pallas_call | solution.py:1081
  453.4 6.2 %convolution_convert_fusion.out_grad = bf16[1024,512]{1,0:T(8,128)(2,1)} fusion(bf16[1024,2048]{1,0:T(8,128)(2,1)} %bitcast.49, bf16[512,2048]{1,0:T(8,128)(2,1)} %get-tuple-element.50.wo), kind=kOutput, calls=%fused_computation | convolution fusion | flops 2148007936 | bytes 7340032 | tf_op jit(solution)/shard_map/dot_general | solution.py:48
  459.6 26.9 %attention_back.1 = (bf16[1024,1536]{1,0:T(8,128)(2,1)}, f32[1,512]{1,0:T(1,128)}, f32[1,512]{1,0:T(1,128)}) custom-call(f32[1024,1536]{1,0:T(8,128)} %get-tuple-element.45.q_raw.k_raw.v_raw.qkv, bf16[1024,512]{1,0:T(8,128)(2,1)} %get-tuple-element.55.q_low, bf16[1024,512]{1,0:T(8,128)(2,1)} %get-tuple-element.56.k_low, ...), custom_call_target="tpu_custom_call" | custom-call | flops 30000001024 | bytes 90000000 | tf_op jit(solution)/shard_map/attention_back/pallas_call | solution.py:1549
  486.5 98.1 %last_grads.1 = (f32[256,2048]{1,0:T(8,128)}, f32[256,1536]{1,0:T(8,128)}, f32[512,256]{1,0:T(8,128)}, f32[256,2048]{1,0:T(8,128)}, f32[1,1536]{1,0:T(1,128)}) custom-call(bf16[1024,1536]{1,0:T(8,128)(2,1)} %get-tuple-element.60.grads, bf16[2048,1536]{1,0:T(8,128)(2,1)} %get-tuple-element.61.weight, f32[256,2048]{1,0:T(8,128)} %get-tuple-element.62.base, ...), custom_call_target="tpu_custom_call" | custom-call | flops 80000000000 | bytes 240000000 | tf_op jit(solution)/shard_map/last_grads/pallas_call | solution.py:1339
  584.6 2.9 copy.44
  587.5 2.7 fusion.4
  591.5 1.0 copy.57
  592.4 1.3 copy.58
  593.8 0.8 copy.59
  595.1 1.3 copy.60
  596.5 1.0 copy-done
  597.5 1.3 copy.61
  (38 shorter events, 4.4 us)
Async XLA Ops:
  3.6 4.3 copy-start.8
  3.6 4.3 copy-start.9
  3.6 4.3 copy-start.6
  3.6 4.4 copy-start.7
  587.5 2.7 copy-start.5
  587.5 3.9 copy-start.3
  587.5 4.9 copy-start.2
  592.4 1.4 copy-start.4
  592.4 2.7 copy-start.1
  595.1 2.3 copy-start
